TPU v7x, 256 devices: a whole 4x4x8 slice. The times are simulated.
256 devices in a mesh: layer: 4 (over x), ex: 64 (over z, y, core).
Axes of the slice: x: 4, y: 4, z: 8, core: 2. Of those that a mesh axis runs over, the one named last changes fastest.
Arguments:
- query_factors: bfloat16 [4, 1024, 512, 128], P('layer', 'ex'), may hold values from -1.2578125 to 1.2578125
- response_lengths: int32 [1024], P('ex'), may hold values from 1 to 512, 262144 in all
- inverse_hessian: float32 [4, 4096, 4096], P('layer', 'ex'), as said below
- stored_gradients: bfloat16 [4, 16384, 4096], P('layer', 'ex'), may hold values from -0.015625 to 0.015625
Outputs:
- scores: float32 [1024, 16384], P('layer', 'ex')
Inputs may be any that keep to these rules, and one draw needn't show every extreme that they name: inverse_hessian[l] is symmetric for every layer l.
All inputs are finite; a program needn't handle non-finite values. No bound on the sum of `response_lengths` on one device may be relied on, other than what follows from the above.
Results may differ from a plain program's by a relative error of at most 0.004.
Values may be sent and summed in bfloat16 or wider, within the bound.
No kernel may reach another device: no remote copies, remote signals or barrier semaphores. Data moves between devices by JAX's collectives and lax.ppermute only.
A program may use at most 64 MiB of HBM per device.

v0:
```python
import jax
import jax.numpy as jnp
from jax import lax
from jax.sharding import PartitionSpec as P


def form_gradients(query_layer, response_lengths):
    steps = lax.broadcasted_iota(jnp.int32, (query_layer.shape[0], query_layer.shape[1]), 1)
    mask = (steps < response_lengths[:, None]).astype(jnp.bfloat16)
    rank = query_layer.shape[2] // 2
    inputs = query_layer[:, :, :rank] * mask[:, :, None]
    outputs = query_layer[:, :, rank:]
    projected = jnp.einsum("qti,qtj->qij", outputs, inputs, preferred_element_type=jnp.float32)
    return projected.reshape(query_layer.shape[0], rank * rank).astype(jnp.bfloat16)


def per_device(query_factors, response_lengths, inverse_hessian, stored_gradients):
    projected = form_gradients(query_factors[0], response_lengths)
    inverse_rows = inverse_hessian[0]
    stored_layer = stored_gradients[0]
    columns = lax.all_to_all(projected, "ex", split_axis=1, concat_axis=0, tiled=True)
    summed = lax.psum_scatter(
        jnp.dot(
            columns.astype(jnp.float32),
            inverse_rows,
            precision=lax.Precision.HIGHEST,
            preferred_element_type=jnp.float32,
        ),
        "ex",
        scatter_dimension=0,
        tiled=True,
    )
    preconditioned = summed.astype(jnp.bfloat16)
    layer_total = lax.dot_general(
        lax.all_gather(preconditioned, "ex", axis=0, tiled=True),
        stored_layer,
        (((1,), (1,)), ((), ())),
        preferred_element_type=jnp.float32,
    )
    whole = lax.psum(layer_total, "layer")
    share_rows = whole.shape[0] // lax.axis_size("layer")
    return lax.dynamic_slice_in_dim(whole, lax.axis_index("layer") * share_rows, share_rows, 0)


def solution(mesh):
    placed = (P("layer", "ex", None, None), P("ex"), P("layer", "ex", None), P("layer", "ex", None))
    return jax.shard_map(
        per_device, mesh=mesh, in_specs=placed, out_specs=P("layer", "ex"), check_vma=False
    )
```

profile of v0, /device:TPU:1, one launch (start us, length us, event | category | flops | bytes accessed | tf_op | source)
XLA Modules:
  0.0 380.0 jit_solution(5849574436239446630)
XLA Ops:
  6.5 0.0 copy-start
  6.5 0.0 copy-start.2
  6.5 0.0 reduce-scatter.2.cloned.1.call-start
  6.5 4.1 %copy.8 = bf16[1,16,512,128]{2,3,1,0:T(8,128)(2,1)} copy(bf16[1,16,512,128]{3,2,1,0:T(8,128)(2,1)} %param.4) | data formatting | bytes 4194304 | tf_op args[0]
  10.6 0.0 copy-done.2
  10.6 0.1 fusion.7
  10.7 0.0 copy-start.1
  10.7 2.8 fusion.2
  13.5 1.2 copy.9
  14.7 0.2 reshape.24
  14.9 24.2 %all_to_all.16 = bf16[64,2,512]{2,1,0:T(2,128)(2,1)} all-to-all(bf16[64,2,512]{2,1,0:T(2,128)(2,1)S(1)} %reshape.24), channel_id=1, replica_groups=mesh['layer'=4,'ex'=64] {'ex'}, dimensions={0} | all-to-all | bytes 262144 | tf_op jit(solution)/shard_map/all_to_all | solution.py:21
  39.0 1.1 reshape.25
  40.2 0.0 copy-done.1
  40.2 9.6 %fusion.4 = f32[1024,4096]{1,0:T(8,128)} fusion(bf16[1024,64]{1,0:T(8,128)(2,1)S(1)} %bitcast.17, f32[1,64,4096]{2,1,0:T(8,128)S(1)} %copy-done.1), kind=kOutput, calls=%fused_computation.6 | convolution fusion | flops 3221225472 | bytes 17956864 | tf_op jit(solution)/shard_map/dot_general | solution.py:23
  49.7 0.0 reduce-scatter.2.cloned.1.call-update
  49.8 0.0 all-gather.2.cloned.1.call-start
  49.8 180.0 %reduce-scatter.2.cloned.1.call-done = f32[16,4096]{1,0:T(8,128)} async-done(((f32[1024,4096]{1,0:T(8,128)}), f32[16,4096]{1,0:T(8,128)}) %reduce-scatter.2.cloned.1.call-update) | async-done | bytes 262160 | tf_op jit(solution)/shard_map/reduce_scatter | solution.py:22
  229.8 1.6 convert_element_type.21
  231.5 0.0 all-gather.2.cloned.1.call-update
  231.5 0.0 all-reduce.2.cloned.1.call-start
  231.5 87.1 %all-gather.2.cloned.1.call-done = bf16[1024,4096]{1,0:T(8,128)(2,1)} async-done(((bf16[16,4096]{1,0:T(8,128)(2,1)}), bf16[1024,4096]{1,0:T(8,128)(2,1)}) %all-gather.2.cloned.1.call-update) | async-done | bytes 8388624 | tf_op jit(solution)/shard_map/all_gather | solution.py:35
  318.6 0.0 copy-done
  318.6 6.8 %fusion = f32[1024,256]{1,0:T(8,128)} fusion(bf16[1024,4096]{1,0:T(8,128)(2,1)} %all-gather.2.cloned.1.call-done, bf16[1,256,4096]{2,1,0:T(8,128)(2,1)S(1)} %copy-done), kind=kOutput, calls=%fused_computation | convolution fusion | flops 2147483648 | bytes 11534336 | tf_op jit(solution)/shard_map/dot_general | solution.py:34
  325.4 0.0 all-reduce.2.cloned.1.call-update
  325.5 46.4 %all-reduce.2.cloned.1.call-done = f32[1024,256]{1,0:T(8,128)} async-done(((f32[1024,256]{1,0:T(8,128)}), f32[1024,256]{1,0:T(8,128)}) %all-reduce.2.cloned.1.call-update) | async-done | bytes 1048592 | tf_op jit(solution)/shard_map/psum | solution.py:40
  371.8 1.7 constant_dynamic-slice_fusion
Async XLA Ops:
  6.5 312.1 %copy-start = (bf16[1,256,4096]{2,1,0:T(8,128)(2,1)S(1)}, bf16[1,256,4096]{2,1,0:T(8,128)(2,1)}, u32[]{:S(2)}) copy-start(bf16[1,256,4096]{2,1,0:T(8,128)(2,1)} %param.7) | copy-start | bytes 6291460
  6.5 4.1 %copy-start.2 = (s32[16]{0:T(128)S(1)}, s32[16]{0:T(128)}, u32[]{:S(2)}) copy-start(s32[16]{0:T(128)} %param.5) | copy-start | bytes 196
  6.5 223.3 %reduce-scatter.2.cloned.1.call-start = ((), (), s32[]{:S(2)}) async-start(), calls=%async_computation.2 | async-start | bytes 17039360 | tf_op jit(solution)/shard_map/reduce_scatter | solution.py:22
  10.7 29.5 %copy-start.1 = (f32[1,64,4096]{2,1,0:T(8,128)S(1)}, f32[1,64,4096]{2,1,0:T(8,128)}, u32[]{:S(2)}) copy-start(f32[1,64,4096]{2,1,0:T(8,128)} %param.6) | copy-start | bytes 3145732
  49.8 268.9 %all-gather.2.cloned.1.call-start = ((), (), s32[]{:S(2)}) async-start(), calls=%async_computation.3 | async-start | bytes 8519680 | tf_op jit(solution)/shard_map/all_gather | solution.py:35
  231.5 140.4 %all-reduce.2.cloned.1.call-start = ((), (), s32[]{:S(2)}) async-start(), calls=%async_computation.4 | async-start | bytes 2097152 | tf_op jit(solution)/shard_map/psum | solution.py:40
Sparse Core Ops, SparseCore 0:
  49.9 179.9 reduce-scatter.1
  232.6 85.9 all-gather.1
  325.6 46.2 all-reduce.1
where the time goes:
time: 381 us; the launch traced here: 380 us
  waiting for transfers between devices  314 us (82%)
  blocking collectives  24.2 us (6%)
  matrix products  19.1 us (5%)
  between operations  13.1 us (3%)
  local copies, waits for them, and re-layouts  8.27 us (2%)
    reduce_scatter x1, waiting for transfers between devices, per_device(): lax.psum_scatter(jnp.dot(columns.astype(jnp.float32), inverse_rows, preci...  180 us
    all_gather x1, waiting for transfers between devices, per_device(): lax.all_gather(preconditioned, 'ex', axis=0, tiled=True)  87.1 us
    psum x1, waiting for transfers between devices, per_device(): whole = lax.psum(layer_total, 'layer')  46.4 us
    all_to_all x1, blocking collectives, per_device(): lax.all_to_all(projected, 'ex', split_axis=1, concat_axis=0, tiled=True)  24.2 us
    dot_general x1, matrix products, per_device(): jnp.dot(columns.astype(jnp.float32), inverse_rows, precision=lax.Precisio...  9.56 us
  transfers between devices with their start and end apart: 3, of which 3 were waited for; matrix products, arithmetic and copies ran while one was open for 0% of the time, Pallas kernels for 0%

commit v1 on v0

v1 whole, which is shorter than its diff:
```python
import jax
import jax.numpy as jnp
from jax import lax
from jax.experimental import pallas as pl
from jax.experimental.pallas import tpu as pltpu
from jax.sharding import Mesh, PartitionSpec as P

LAYER, Z, Y, CORE = 4, 8, 4, 2
PIECES = Z * Y // 2
BF = jnp.bfloat16
F32 = jnp.float32
VMEM = pl.BlockSpec(memory_space=pltpu.VMEM)
SMEM = pl.BlockSpec(memory_space=pltpu.SMEM)
NT = (((1,), (1,)), ((), ()))
TN = (((0,), (0,)), ((), ()))


def params(mib=8):
    return pltpu.CompilerParams(vmem_limit_bytes=mib << 20)


def cost(flops, moved):
    return pl.CostEstimate(flops=flops // 1000, bytes_accessed=moved // 1000, transcendentals=0)


def gradient_kernel(lengths_ref, factors_ref, out_ref):
    queries, steps, width = factors_ref.shape
    rank = width // 2
    step = lax.broadcasted_iota(jnp.int32, (steps, width), 0)
    for q in range(queries):
        x = factors_ref[q]
        masked = jnp.where(step < lengths_ref[pl.program_id(0) * queries + q], x, jnp.zeros_like(x))
        both = lax.dot_general(x, masked, TN, preferred_element_type=F32)
        out_ref[q] = both[rank:, :rank].astype(BF)


def gradients(factors, lengths, group=4):
    queries, steps, width = factors.shape
    rank = width // 2
    projected = pl.pallas_call(
        gradient_kernel,
        out_shape=jax.ShapeDtypeStruct((queries, rank, rank), BF),
        grid_spec=pltpu.PrefetchScalarGridSpec(
            num_scalar_prefetch=1,
            grid=(queries // group,),
            in_specs=[pl.BlockSpec((group, steps, width), lambda i, _: (i, 0, 0))],
            out_specs=pl.BlockSpec((group, rank, rank), lambda i, _: (i, 0, 0)),
        ),
        compiler_params=params(6),
        cost_estimate=cost(queries * steps * width * width * 2, factors.size * 2),
        name="form_gradients",
    )(lengths, factors)
    return projected.reshape(queries, rank * rank)


def split_kernel(where_ref, own_ref, core_ref, chip_ref, both_ref, high_ref, low_ref):
    rows = own_ref.shape[0]
    me = where_ref[PIECES]
    for k, ref in enumerate((own_ref, core_ref, chip_ref, both_ref)):
        place = pl.ds(pl.multiple_of((me ^ k) * rows, rows), rows)
        whole = ref[...]
        high = whole.astype(BF)
        high_ref[place, :] = high
        low_ref[place, :] = (whole - high.astype(F32)).astype(BF)


def split_rows(where, parts):
    rows, columns = parts[0].shape
    shape = jax.ShapeDtypeStruct((4 * rows, columns), BF)
    return pl.pallas_call(
        split_kernel,
        out_shape=(shape, shape),
        in_specs=[SMEM] + [VMEM] * 4,
        out_specs=(VMEM, VMEM),
        compiler_params=params(16),
        cost_estimate=cost(rows * columns * 8, rows * columns * 32),
        name="split_inverse",
    )(where, *parts)


def precondition_kernel(count, where_ref, *refs):
    pieces, (high_ref, low_ref, out_ref) = refs[:count], refs[count:]
    rows = pieces[0].shape[0]
    left = jnp.concatenate([ref[...] for ref in pieces], axis=0)
    total = lax.dot_general(left, high_ref[...], NT, preferred_element_type=F32)
    total += lax.dot_general(left, low_ref[...], NT, preferred_element_type=F32)
    total = total.astype(BF)
    for k in range(count):
        place = pl.ds(pl.multiple_of(where_ref[k] * rows, rows), rows)
        out_ref[place, :] = total[k * rows : (k + 1) * rows]


def precondition(where, pieces, high, low):
    rows, depth = pieces[0].shape
    count = rows * len(pieces)
    return pl.pallas_call(
        lambda *refs: precondition_kernel(len(pieces), *refs),
        out_shape=jax.ShapeDtypeStruct((count, high.shape[0]), BF),
        in_specs=[SMEM] + [VMEM] * (len(pieces) + 2),
        out_specs=VMEM,
        compiler_params=params(16),
        cost_estimate=cost(4 * count * depth * high.shape[0], 2 * depth * (count + 2 * high.shape[0])),
        name="precondition",
    )(where, *pieces, high, low)


def score_kernel(some, held, first, cut, where_ref, *refs):
    count = len(some)
    pieces, stored, refs = refs[:count], refs[count : count + held], refs[count + held :]
    before, outs = (None, refs) if first else (refs[0], refs[1:])
    columns = pieces[0].shape[1]
    total = outs[-1] if cut else outs[0]
    start = 0
    for ref in stored:
        span = (slice(None), slice(start, start + ref.shape[0]))
        start += ref.shape[0]
        acc = None if first else before[span]
        for k, piece in enumerate(pieces):
            place = pl.ds(pl.multiple_of(where_ref[some[k]] * columns, columns), columns)
            term = lax.dot_general(piece[...], ref[:, place], NT, preferred_element_type=F32)
            acc = term if acc is None else acc + term
        total[span] = acc
    if cut:
        block = total.shape[0] // LAYER
        for k, out in enumerate(outs[:-1]):
            owner = lax.rem(where_ref[PIECES + 1] + k, LAYER)
            out[...] = total[pl.ds(pl.multiple_of(owner * block, block), block), :].astype(out.dtype)


def score(where, some, pieces, stored, before=None, cut=False):
    count = len(pieces)
    queries, columns = pieces[0].shape
    examples = sum(part.shape[0] for part in stored)
    whole = (queries, examples)
    block = (queries // LAYER, examples)
    depth = count * columns
    blocks = [jax.ShapeDtypeStruct(block, F32)] + [jax.ShapeDtypeStruct(block, BF)] * (LAYER - 1)
    more = [] if before is None else [before]
    return pl.pallas_call(
        lambda *refs: score_kernel(some, len(stored), before is None, cut, *refs),
        out_shape=blocks if cut else jax.ShapeDtypeStruct(whole, F32),
        in_specs=[SMEM] + [VMEM] * (count + len(stored) + len(more)),
        out_specs=[VMEM] * LAYER if cut else VMEM,
        scratch_shapes=[pltpu.VMEM(whole, F32)] if cut else [],
        compiler_params=params(20),
        cost_estimate=cost(2 * queries * depth * examples, 2 * depth * (queries + examples)),
        name="score",
    )(where, *pieces, *stored, *more)


def add_kernel(own_ref, a_ref, b_ref, c_ref, *outs):
    width = outs[0].shape[1]
    for k, out in enumerate(outs):
        part = (slice(None), slice(k * width, (k + 1) * width))
        out[...] = (own_ref[part] + a_ref[part].astype(F32)) + (b_ref[part].astype(F32) + c_ref[part].astype(F32))


def add_layers(own, others):
    rows, width = own.shape
    return pl.pallas_call(
        add_kernel,
        out_shape=[jax.ShapeDtypeStruct((rows, width // 4), F32)] * 4,
        in_specs=[VMEM] * 4,
        out_specs=[VMEM] * 4,
        compiler_params=params(6),
        cost_estimate=cost(rows * width * 3, rows * width * 14),
        name="add_layers",
    )(own, *others)


def place_kernel(where_ref, *refs):
    parts, out_ref = refs[:-1], refs[-1]
    rows = parts[0].shape[0] // 4
    for k, part in enumerate(parts):
        for group in range(4):
            start = pl.multiple_of(group * 4 * rows + (where_ref[PIECES] ^ k) * rows, rows)
            out_ref[pl.ds(start, rows), :] = part[group * rows : (group + 1) * rows, :]


def place_parts(where, parts):
    rows, width = parts[0].shape
    return pl.pallas_call(
        place_kernel,
        out_shape=jax.ShapeDtypeStruct((4 * rows, width), F32),
        in_specs=[SMEM] + [VMEM] * 4,
        out_specs=VMEM,
        compiler_params=params(6),
        cost_estimate=cost(rows * width * 4, rows * width * 32),
        name="place_parts",
    )(where, *parts)


def shift(value, axis, size, by):
    return lax.ppermute(value, axis, [(i, (i + by) % size) for i in range(size)])


def after(value, other):
    return lax.optimization_barrier((value, other))[0]


def swap_core(value):
    return lax.ppermute(value, "core", [(0, 1), (1, 0)])


def gather(own, across):
    pieces = []
    for side, value in enumerate((own, across)):
        pieces.append((0, side, value))
        up = down = value
        for distance in range(1, Z // 2):
            up = shift(up, "z", Z, 1)
            down = shift(down, "z", Z, -1)
            pieces.append((-distance, side, up))
            pieces.append((distance, side, down))
        last = shift(up, "z", Z, 1) if side == 0 else shift(down, "z", Z, -1)
        pieces.append((Z // 2, side, last))
    return pieces


def most(pieces):
    return [value for dz, side, value in pieces if abs(dz) + side == 3]


def per_device(factors, lengths, inverse, stored):
    layer, z, y, core = (lax.axis_index(name) for name in ("layer", "z", "y", "core"))
    apart = [distance for step in range(1, Z // 2) for distance in (-step, step)]
    apart = jnp.array([0] + apart + [Z // 2], jnp.int32)
    where = jnp.concatenate([((z + apart) % Z) * 2 + (y // 2 ^ side) for side in (0, 1)])
    where = jnp.concatenate([where, jnp.stack([(y % 2) * 2 + core, layer])]).astype(jnp.int32)
    inverse_rows, stored_rows = inverse[0], stored[0]

    def swap_chip(value, *pairs):
        return lax.ppermute(value, "y", [pair for a, b in pairs for pair in ((a, b), (b, a))])

    with jax.named_scope("swap_stored"):
        chip_stored = swap_chip(stored_rows, (0, 3), (1, 2))
    with jax.named_scope("gradients"):
        projected = gradients(factors[0], after(lengths, where))
    with jax.named_scope("gather_projected"):
        pieces = gather(projected, shift(projected, "y", Y, 2))
    with jax.named_scope("swap_inverse"):
        core_rows = swap_core(inverse_rows)
        chip_rows = swap_chip(after(inverse_rows, projected), (0, 1), (2, 3))
        both_rows = swap_core(after(chip_rows, most(pieces)))
    with jax.named_scope("split_inverse"):
        high, low = split_rows(where, (inverse_rows, core_rows, chip_rows, both_rows))
    with jax.named_scope("precondition"):
        own = precondition(where, [value for _, _, value in pieces], high, low)
    with jax.named_scope("gather_preconditioned"):
        pieces = gather(own, shift(own, "y", Y, 2))
    with jax.named_scope("swap_stored"):
        core_stored = swap_core(after(stored_rows, own))
        both_stored = swap_core(after(chip_stored, most(pieces)))
    with jax.named_scope("score"):
        late = [k for k, (dz, side, _) in enumerate(pieces) if abs(dz) == 4 or (side and abs(dz) == 3)]
        soon = [k for k in range(len(pieces)) if k not in late]
        stored_parts = (stored_rows, core_stored, chip_stored, both_stored)
        total = None
        for some in (soon, late):
            total = score(where, some, [pieces[k][2] for k in some], stored_parts, total, some is late)
        kept, *sent = total
    with jax.named_scope("sum_layers"):
        others = [shift(value, "layer", LAYER, k + 1) for k, value in enumerate(sent)]
        parts = add_layers(kept, others)
    with jax.named_scope("exchange_examples"):
        pairs = []
        for k in range(1, 4):
            pairs.append([(a * 2 + b, ((3 - a) if k & 2 else a) * 2 + (b ^ (k & 1))) for a in range(Y) for b in range(CORE)])
        parts = [parts[0]] + [lax.ppermute(parts[k], ("y", "core"), pairs[k - 1]) for k in range(1, 4)]
        return place_parts(where, parts)


def solution(mesh):
    shape = (LAYER, Z, Y, CORE)
    fine = Mesh(mesh.devices.reshape(shape), ("layer", "z", "y", "core"))
    ex = ("z", "y", "core")
    placed = (P("layer", ex, None, None), P(ex), P("layer", ex, None), P("layer", ex, None))
    return jax.shard_map(per_device, mesh=fine, in_specs=placed, out_specs=P("layer", ex), check_vma=False)
```

time: 381 us -> 131 us (0.34)
  waiting for transfers between devices: 314 us -> 47.8 us
  starting transfers between devices: 0.09 us -> 68.2 us
  blocking collectives: 24.2 us -> 0 us
  matrix products: 19.1 us -> 0 us
  between operations: 13.1 us -> 0.12 us
  Pallas kernels: 0 us -> 10.3 us
  local copies, waits for them, and re-layouts: 8.27 us -> 3.75 us
    reduce_scatter x1 -> x0, waiting for transfers between devices: 180 us -> none  [per_device(): lax.psum_scatter(jnp.dot(columns.astype(jnp.float32), inverse_rows, preci...]
    all_gather x1 -> x0, waiting for transfers between devices: 87.1 us -> none  [per_device(): lax.all_gather(preconditioned, 'ex', axis=0, tiled=True)]
    ppermute x0 -> x42, starting transfers between devices: none -> 68.2 us  [the longest x33 42.2 us: shift(): lax.ppermute(value, axis, [(i, (i + by) % size) for i in range(size)])]
    ppermute x0 -> x42, waiting for transfers between devices: none -> 47.8 us  [the longest x33 44.3 us: shift(): lax.ppermute(value, axis, [(i, (i + by) % size) for i in range(size)])]
    psum x1 -> x0, waiting for transfers between devices: 46.4 us -> none  [per_device(): whole = lax.psum(layer_total, 'layer')]
    all_to_all x1 -> x0, blocking collectives: 24.2 us -> none  [per_device(): lax.all_to_all(projected, 'ex', split_axis=1, concat_axis=0, tiled=True)]
    dot_general x3 -> x0, matrix products: 19.1 us -> none  [the longest x1 9.56 us: per_device(): jnp.dot(columns.astype(jnp.float32), inverse_rows, precision=lax.Precisio...]
    pallas_call x0 -> x7, Pallas kernels: none -> 10.3 us  [the longest x2 3.79 us: score(): pl.pallas_call(lambda *refs: score_kernel(some, len(stored), before is No...]
  transfers between devices with their start and end apart: 3 -> 42, of which waited for: 3 -> 17; matrix products, arithmetic and copies ran while one was open for 0% -> 0% of each run, Pallas kernels for 0% -> 4%
where the time goes in v1:
time: 131 us
  starting transfers between devices  68.2 us (52%)
  waiting for transfers between devices  47.8 us (36%)
  Pallas kernels  10.3 us (8%)
  local copies, waits for them, and re-layouts  3.75 us (3%)
    ppermute x33, waiting for transfers between devices, shift(): lax.ppermute(value, axis, [(i, (i + by) % size) for i in range(size)])  44.3 us
    ppermute x33, starting transfers between devices, shift(): lax.ppermute(value, axis, [(i, (i + by) % size) for i in range(size)])  42.2 us
    ppermute x4, starting transfers between devices, swap_core(): return lax.ppermute(value, 'core', [(0, 1), (1, 0)])  16.6 us
    ppermute x3, starting transfers between devices, per_device(): lax.ppermute(parts[k], ('y', 'core'), pairs[k - 1])  5.19 us
    ppermute x2, starting transfers between devices, swap_chip(): lax.ppermute(value, 'y', [pair for a, b in pairs for pair in ((a, b), (b,...  4.11 us
    pallas_call x2, Pallas kernels, score(): pl.pallas_call(lambda *refs: score_kernel(some, len(stored), before is No...  3.79 us
    ppermute x3, waiting for transfers between devices, per_device(): lax.ppermute(parts[k], ('y', 'core'), pairs[k - 1])  3.51 us
    unnamed x8, local copies, waits for them, and re-layouts  3.48 us
  transfers between devices with their start and end apart: 42, of which 17 were waited for; matrix products, arithmetic and copies ran while one was open for 0% of the time, Pallas kernels for 4%

profile of v1, /device:TPU:1, one launch (start us, length us, event | category | flops | bytes accessed | tf_op | source)
XLA Modules:
  0.0 131.0 jit_solution(17698790881274630597)
XLA Ops:
  0.0 0.8 broadcast_add_fusion.1
  0.8 0.1 pad_add_fusion.where_ref.refs_0_
  0.9 1.6 %copy-done.1 = bf16[1,16,512,128]{3,2,1,0:T(8,128)(2,1)S(1)} copy-done((bf16[1,16,512,128]{3,2,1,0:T(8,128)(2,1)S(1)}, bf16[1,16,512,128]{3,2,1,0:T(8,128)(2,1)}, u32[]{:S(2)}) %copy-start.1) | copy-done | bytes 2097176
  2.5 0.7 copy-done.3
  3.2 2.1 %form_gradients.1 = bf16[16,64,64]{2,1,0:T(8,128)(2,1)S(1)} custom-call(s32[16]{0:T(128)S(1)} %copy-done.3, bf16[16,512,128]{2,1,0:T(8,128)(2,1)S(1)} %bitcast.9), custom_call_target="tpu_custom_call" | custom-call | flops 268435 | bytes 2097 | tf_op jit(solution)/shard_map/gradients/form_gradients/pallas_call | solution.py:40
  5.3 0.3 reshape.3.refs_1_
  5.6 2.2 %collective-permute-start.16 = (f32[64,4096]{1,0:T(8,128)}, f32[64,4096]{1,0:T(8,128)S(1)}, u32[]{:S(2)}, u32[]{:S(2)}) collective-permute-start(f32[64,4096]{1,0:T(8,128)} %bitcast.10), channel_id=1, source_target_pairs={{0,2},{2,0},{4,6},{6,4},{1,3},{3,1},{5,7},{7,5},{8,10},{10,8},{12,... | collective-permute-start | bytes 3145736 | tf_op jit(solution)/shard_map/swap_inverse/ppermute | solution.py:233
  7.8 1.9 %collective-permute-start.31 = (bf16[256,4096]{1,0:T(8,128)(2,1)S(1)}, bf16[256,4096]{1,0:T(8,128)(2,1)S(1)}, u32[]{:S(2)}, u32[]{:S(2)}) collective-permute-start(bf16[256,4096]{1,0:T(8,128)(2,1)S(1)} %bitcast.5), channel_id=1, source_target_pairs={{0,6},{6,0},{2,4},{4,2},{1,7},{7,1},{3,5},{5,3},{8,14},{14,8},{10,... | collective-permute-start | bytes 6291464 | tf_op jit(solution)/shard_map/swap_stored/ppermute | solution.py:233
  9.7 0.7 collective-permute-start.7
  10.4 1.6 %collective-permute-start = (bf16[16,4096]{1,0:T(8,128)(2,1)S(1)}, bf16[16,4096]{1,0:T(8,128)(2,1)S(1)}, u32[]{:S(2)}, u32[]{:S(2)}) collective-permute-start(bf16[16,4096]{1,0:T(8,128)(2,1)S(1)} %reshape.3.refs_1_), channel_id=1, source_target_pairs={{0,8},{8,16},{16,24},{24,32},{32,40},{40,48},{48,56},{56,0},{1,9},... | collective-permute-start | bytes 393224 | tf_op jit(solution)/shard_map/gather_projected/ppermute | solution.py:194
  12.1 3.9 %collective-permute-start.1 = (bf16[16,4096]{1,0:T(8,128)(2,1)S(1)}, bf16[16,4096]{1,0:T(8,128)(2,1)S(1)}, u32[]{:S(2)}, u32[]{:S(2)}) collective-permute-start(bf16[16,4096]{1,0:T(8,128)(2,1)S(1)} %reshape.3.refs_1_), channel_id=1, source_target_pairs={{0,56},{8,0},{16,8},{24,16},{32,24},{40,32},{48,40},{56,48},{1,57}... | collective-permute-start | bytes 393224 | tf_op jit(solution)/shard_map/gather_projected/ppermute | solution.py:194
  16.0 20.0 %collective-permute-done.7.refs_9_ = bf16[16,4096]{1,0:T(8,128)(2,1)S(1)} collective-permute-done((bf16[16,4096]{1,0:T(8,128)(2,1)S(1)}, bf16[16,4096]{1,0:T(8,128)(2,1)S(1)}, u32[]{:S(2)}, u32[]{:S(2)}) %collective-permute-start.7) | collective-permute-done | bytes 131104 | tf_op jit(solution)/shard_map/gather_projected/ppermute | solution.py:194
  36.0 1.6 %collective-permute-start.8 = (bf16[16,4096]{1,0:T(8,128)(2,1)S(1)}, bf16[16,4096]{1,0:T(8,128)(2,1)S(1)}, u32[]{:S(2)}, u32[]{:S(2)}) collective-permute-start(bf16[16,4096]{1,0:T(8,128)(2,1)S(1)} %collective-permute-done.7.refs_9_), channel_id=1, source_target_pairs={{0,8},{8,16},{16,24},{24,32},{32,40},{40,48},{48,56},{56,0},{1,9},... | collective-permute-start | bytes 393224 | tf_op jit(solution)/shard_map/gather_projected/ppermute | solution.py:194
  37.6 3.9 %collective-permute-start.9 = (bf16[16,4096]{1,0:T(8,128)(2,1)S(1)}, bf16[16,4096]{1,0:T(8,128)(2,1)S(1)}, u32[]{:S(2)}, u32[]{:S(2)}) collective-permute-start(bf16[16,4096]{1,0:T(8,128)(2,1)S(1)} %collective-permute-done.7.refs_9_), channel_id=1, source_target_pairs={{0,56},{8,0},{16,8},{24,16},{32,24},{40,32},{48,40},{56,48},{1,57}... | collective-permute-start | bytes 393224 | tf_op jit(solution)/shard_map/gather_projected/ppermute | solution.py:194
  41.6 2.6 %collective-permute-done.8.refs_10_ = bf16[16,4096]{1,0:T(8,128)(2,1)S(1)} collective-permute-done((bf16[16,4096]{1,0:T(8,128)(2,1)S(1)}, bf16[16,4096]{1,0:T(8,128)(2,1)S(1)}, u32[]{:S(2)}, u32[]{:S(2)}) %collective-permute-start.8) | collective-permute-done | bytes 131104 | tf_op jit(solution)/shard_map/gather_projected/ppermute | solution.py:194
  44.2 1.5 %collective-permute-start.3 = (bf16[16,4096]{1,0:T(8,128)(2,1)S(1)}, bf16[16,4096]{1,0:T(8,128)(2,1)S(1)}, u32[]{:S(2)}, u32[]{:S(2)}) collective-permute-start(bf16[16,4096]{1,0:T(8,128)(2,1)S(1)} %collective-permute-done.1.refs_3_), channel_id=1, source_target_pairs={{0,56},{8,0},{16,8},{24,16},{32,24},{40,32},{48,40},{56,48},{1,57}... | collective-permute-start | bytes 393224 | tf_op jit(solution)/shard_map/gather_projected/ppermute | solution.py:194
  45.7 1.8 %collective-permute-done.2.refs_4_ = bf16[16,4096]{1,0:T(8,128)(2,1)S(1)} collective-permute-done((bf16[16,4096]{1,0:T(8,128)(2,1)S(1)}, bf16[16,4096]{1,0:T(8,128)(2,1)S(1)}, u32[]{:S(2)}, u32[]{:S(2)}) %collective-permute-start.2) | collective-permute-done | bytes 131104 | tf_op jit(solution)/shard_map/gather_projected/ppermute | solution.py:194
  47.5 0.9 collective-permute-start.11
  48.4 0.6 collective-permute-start.4
  48.9 2.1 %collective-permute-done.10.refs_12_ = bf16[16,4096]{1,0:T(8,128)(2,1)S(1)} collective-permute-done((bf16[16,4096]{1,0:T(8,128)(2,1)S(1)}, bf16[16,4096]{1,0:T(8,128)(2,1)S(1)}, u32[]{:S(2)}, u32[]{:S(2)}) %collective-permute-start.10) | collective-permute-done | bytes 131104 | tf_op jit(solution)/shard_map/gather_projected/ppermute | solution.py:194
  51.0 0.4 collective-permute-start.5
  51.4 1.6 %collective-permute-done.11.refs_13_ = bf16[16,4096]{1,0:T(8,128)(2,1)S(1)} collective-permute-done((bf16[16,4096]{1,0:T(8,128)(2,1)S(1)}, bf16[16,4096]{1,0:T(8,128)(2,1)S(1)}, u32[]{:S(2)}, u32[]{:S(2)}) %collective-permute-start.11) | collective-permute-done | bytes 131104 | tf_op jit(solution)/shard_map/gather_projected/ppermute | solution.py:194
  52.9 3.7 %collective-permute-start.15 = (f32[64,4096]{1,0:T(8,128)}, f32[64,4096]{1,0:T(8,128)S(1)}, u32[]{:S(2)}, u32[]{:S(2)}) collective-permute-start(f32[64,4096]{1,0:T(8,128)} %bitcast.11), channel_id=1, source_target_pairs={{0,1},{1,0},{2,3},{3,2},{4,5},{5,4},{6,7},{7,6},{8,9},{9,8},{10,11... | collective-permute-start | bytes 3145736 | tf_op jit(solution)/shard_map/swap_inverse/ppermute | solution.py:202
  56.6 3.8 %collective-permute-start.17 = (f32[64,4096]{1,0:T(8,128)S(1)}, f32[64,4096]{1,0:T(8,128)S(1)}, u32[]{:S(2)}, u32[]{:S(2)}) collective-permute-start(f32[64,4096]{1,0:T(8,128)S(1)} %collective-permute-done.16.chip_ref), channel_id=1, source_target_pairs={{0,1},{1,0},{2,3},{3,2},{4,5},{5,4},{6,7},{7,6},{8,9},{9,8},{10,11... | collective-permute-start | bytes 3145736 | tf_op jit(solution)/shard_map/swap_inverse/ppermute | solution.py:202
  60.5 2.1 %collective-permute-start.13 = (bf16[16,4096]{1,0:T(8,128)(2,1)S(1)}, bf16[16,4096]{1,0:T(8,128)(2,1)S(1)}, u32[]{:S(2)}, u32[]{:S(2)}) collective-permute-start(bf16[16,4096]{1,0:T(8,128)(2,1)S(1)} %collective-permute-done.11.refs_13_), channel_id=1, source_target_pairs={{0,56},{8,0},{16,8},{24,16},{32,24},{40,32},{48,40},{56,48},{1,57}... | collective-permute-start | bytes 393224 | tf_op jit(solution)/shard_map/gather_projected/ppermute | solution.py:194
  62.5 3.1 %collective-permute-done.13.refs_15_ = bf16[16,4096]{1,0:T(8,128)(2,1)S(1)} collective-permute-done((bf16[16,4096]{1,0:T(8,128)(2,1)S(1)}, bf16[16,4096]{1,0:T(8,128)(2,1)S(1)}, u32[]{:S(2)}, u32[]{:S(2)}) %collective-permute-start.13) | collective-permute-done | bytes 131104 | tf_op jit(solution)/shard_map/gather_projected/ppermute | solution.py:194
  65.6 0.6 collective-permute-start.6
  66.2 2.7 %collective-permute-start.14 = (bf16[16,4096]{1,0:T(8,128)(2,1)S(1)}, bf16[16,4096]{1,0:T(8,128)(2,1)S(1)}, u32[]{:S(2)}, u32[]{:S(2)}) collective-permute-start(bf16[16,4096]{1,0:T(8,128)(2,1)S(1)} %collective-permute-done.13.refs_15_), channel_id=1, source_target_pairs={{0,56},{8,0},{16,8},{24,16},{32,24},{40,32},{48,40},{56,48},{1,57}... | collective-permute-start | bytes 393224 | tf_op jit(solution)/shard_map/gather_projected/ppermute | solution.py:194
  68.9 1.2 copy-done.2
  70.1 1.2 split_inverse.1
  71.3 0.6 collective-permute-done.6.refs_8_
  72.0 1.8 %precondition.1.refs_1_ = bf16[256,256]{1,0:T(8,128)(2,1)S(1)} custom-call(s32[18]{0:T(128)S(1)} %pad_add_fusion.where_ref.refs_0_, bf16[16,4096]{1,0:T(8,128)(2,1)S(1)} %reshape.3.refs_1_, bf16[16,4096]{1,0:T(8,128)(2,1)S(1)} %collective-permute-done.refs_2_, bf16[16,4096]{1,0:T(8,128)(2,1)S(1)} %collective-permute-done.1.refs_3_, ...), custom_call_target="tpu_custom_call" | custom-call | flops 1073741 | bytes 6291 | tf_op jit(solution)/shard_map/precondition/precondition/pallas_call | solution.py:96
  73.8 2.2 %collective-permute-start.18 = (bf16[256,256]{1,0:T(8,128)(2,1)S(1)}, bf16[256,256]{1,0:T(8,128)(2,1)S(1)}, u32[]{:S(2)}, u32[]{:S(2)}) collective-permute-start(bf16[256,256]{1,0:T(8,128)(2,1)S(1)} %precondition.1.refs_1_), channel_id=1, source_target_pairs={{0,8},{8,16},{16,24},{24,32},{32,40},{40,48},{48,56},{56,0},{1,9},... | collective-permute-start | bytes 393224 | tf_op jit(solution)/shard_map/gather_preconditioned/ppermute | solution.py:194
  76.1 0.5 collective-permute-start.32
  76.6 2.3 %collective-permute-done.18.refs_2_ = bf16[256,256]{1,0:T(8,128)(2,1)S(1)} collective-permute-done((bf16[256,256]{1,0:T(8,128)(2,1)S(1)}, bf16[256,256]{1,0:T(8,128)(2,1)S(1)}, u32[]{:S(2)}, u32[]{:S(2)}) %collective-permute-start.18) | collective-permute-done | bytes 131104 | tf_op jit(solution)/shard_map/gather_preconditioned/ppermute | solution.py:194
  78.9 0.9 collective-permute-start.19
  79.8 1.5 %collective-permute-done.22.refs_8_ = bf16[256,256]{1,0:T(8,128)(2,1)S(1)} collective-permute-done((bf16[256,256]{1,0:T(8,128)(2,1)S(1)}, bf16[256,256]{1,0:T(8,128)(2,1)S(1)}, u32[]{:S(2)}, u32[]{:S(2)}) %collective-permute-start.22) | collective-permute-done | bytes 131104 | tf_op jit(solution)/shard_map/gather_preconditioned/ppermute | solution.py:194
  81.3 1.0 collective-permute-start.23
  82.4 1.6 %collective-permute-start.26 = (bf16[256,256]{1,0:T(8,128)(2,1)S(1)}, bf16[256,256]{1,0:T(8,128)(2,1)S(1)}, u32[]{:S(2)}, u32[]{:S(2)}) collective-permute-start(bf16[256,256]{1,0:T(8,128)(2,1)S(1)} %collective-permute-done.22.refs_8_), channel_id=1, source_target_pairs={{0,56},{8,0},{16,8},{24,16},{32,24},{40,32},{48,40},{56,48},{1,57}... | collective-permute-start | bytes 393224 | tf_op jit(solution)/shard_map/gather_preconditioned/ppermute | solution.py:194
  84.0 1.4 %collective-permute-start.20 = (bf16[256,256]{1,0:T(8,128)(2,1)S(1)}, bf16[256,256]{1,0:T(8,128)(2,1)S(1)}, u32[]{:S(2)}, u32[]{:S(2)}) collective-permute-start(bf16[256,256]{1,0:T(8,128)(2,1)S(1)} %collective-permute-done.19.refs_4_), channel_id=1, source_target_pairs={{0,8},{8,16},{16,24},{24,32},{32,40},{40,48},{48,56},{56,0},{1,9},... | collective-permute-start | bytes 393224 | tf_op jit(solution)/shard_map/gather_preconditioned/ppermute | solution.py:194
  85.5 2.1 %collective-permute-done.23.refs_9_ = bf16[256,256]{1,0:T(8,128)(2,1)S(1)} collective-permute-done((bf16[256,256]{1,0:T(8,128)(2,1)S(1)}, bf16[256,256]{1,0:T(8,128)(2,1)S(1)}, u32[]{:S(2)}, u32[]{:S(2)}) %collective-permute-start.23) | collective-permute-done | bytes 131104 | tf_op jit(solution)/shard_map/gather_preconditioned/ppermute | solution.py:194
  87.6 2.7 %collective-permute-start.27 = (bf16[256,256]{1,0:T(8,128)(2,1)S(1)}, bf16[256,256]{1,0:T(8,128)(2,1)S(1)}, u32[]{:S(2)}, u32[]{:S(2)}) collective-permute-start(bf16[256,256]{1,0:T(8,128)(2,1)S(1)} %collective-permute-done.26.refs_10_), channel_id=1, source_target_pairs={{0,56},{8,0},{16,8},{24,16},{32,24},{40,32},{48,40},{56,48},{1,57}... | collective-permute-start | bytes 393224 | tf_op jit(solution)/shard_map/gather_preconditioned/ppermute | solution.py:194
  90.3 0.2 collective-permute-start.34
  90.4 5.1 %collective-permute-start.30 = (bf16[256,4096]{1,0:T(8,128)(2,1)S(1)}, bf16[256,4096]{1,0:T(8,128)(2,1)S(1)}, u32[]{:S(2)}, u32[]{:S(2)}) collective-permute-start(bf16[256,4096]{1,0:T(8,128)(2,1)S(1)} %bitcast.6), channel_id=1, source_target_pairs={{0,1},{1,0},{2,3},{3,2},{4,5},{5,4},{6,7},{7,6},{8,9},{9,8},{10,11... | collective-permute-start | bytes 6291464 | tf_op jit(solution)/shard_map/swap_stored/ppermute | solution.py:202
  95.6 4.0 %collective-permute-start.35 = (bf16[256,4096]{1,0:T(8,128)(2,1)S(1)}, bf16[256,4096]{1,0:T(8,128)(2,1)S(1)}, u32[]{:S(2)}, u32[]{:S(2)}) collective-permute-start(bf16[256,4096]{1,0:T(8,128)(2,1)S(1)} %collective-permute-done.31.refs_15_.refs_7_), channel_id=1, source_target_pairs={{0,1},{1,0},{2,3},{3,2},{4,5},{5,4},{6,7},{7,6},{8,9},{9,8},{10,11... | collective-permute-start | bytes 6291464 | tf_op jit(solution)/shard_map/swap_stored/ppermute | solution.py:202
  99.6 2.2 %collective-permute-start.28 = (bf16[256,256]{1,0:T(8,128)(2,1)S(1)}, bf16[256,256]{1,0:T(8,128)(2,1)S(1)}, u32[]{:S(2)}, u32[]{:S(2)}) collective-permute-start(bf16[256,256]{1,0:T(8,128)(2,1)S(1)} %collective-permute-done.27.refs_12_), channel_id=1, source_target_pairs={{0,56},{8,0},{16,8},{24,16},{32,24},{40,32},{48,40},{56,48},{1,57}... | collective-permute-start | bytes 393224 | tf_op jit(solution)/shard_map/gather_preconditioned/ppermute | solution.py:194
  101.8 0.5 collective-permute-start.25
  102.3 2.5 %collective-permute-done.28.refs_3_ = bf16[256,256]{1,0:T(8,128)(2,1)S(1)} collective-permute-done((bf16[256,256]{1,0:T(8,128)(2,1)S(1)}, bf16[256,256]{1,0:T(8,128)(2,1)S(1)}, u32[]{:S(2)}, u32[]{:S(2)}) %collective-permute-start.28) | collective-permute-done | bytes 131104 | tf_op jit(solution)/shard_map/gather_preconditioned/ppermute | solution.py:194
  104.7 3.4 %collective-permute-start.29 = (bf16[256,256]{1,0:T(8,128)(2,1)S(1)}, bf16[256,256]{1,0:T(8,128)(2,1)S(1)}, u32[]{:S(2)}, u32[]{:S(2)}) collective-permute-start(bf16[256,256]{1,0:T(8,128)(2,1)S(1)} %collective-permute-done.28.refs_3_), channel_id=1, source_target_pairs={{0,56},{8,0},{16,8},{24,16},{32,24},{40,32},{48,40},{56,48},{1,57}... | collective-permute-start | bytes 393224 | tf_op jit(solution)/shard_map/gather_preconditioned/ppermute | solution.py:194
  108.2 2.4 %score.2.refs_9_ = f32[256,1024]{1,0:T(8,128)S(1)} custom-call(s32[18]{0:T(128)S(1)} %pad_add_fusion.where_ref.refs_0_, bf16[256,256]{1,0:T(8,128)(2,1)S(1)} %precondition.1.refs_1_, bf16[256,256]{1,0:T(8,128)(2,1)S(1)} %collective-permute-done.18.refs_2_, bf16[256,256]{1,0:T(8,128)(2,1)S(1)} %collective-permute-done.32.refs_3_, ...), custom_call_target="tpu_custom_call" | custom-call | flops 1610612 | bytes 7864 | tf_op jit(solution)/shard_map/score/score/pallas_call | solution.py:139
  110.5 0.1 collective-permute-done.25.refs_2_
  110.6 1.4 %score.3 = (f32[64,1024]{1,0:T(8,128)S(1)}, bf16[64,1024]{1,0:T(8,128)(2,1)S(1)}, bf16[64,1024]{1,0:T(8,128)(2,1)S(1)}, bf16[64,1024]{1,0:T(8,128)(2,1)S(1)}) custom-call(s32[18]{0:T(128)S(1)} %pad_add_fusion.where_ref.refs_0_, bf16[256,256]{1,0:T(8,128)(2,1)S(1)} %collective-permute-done.21.refs_1_, bf16[256,256]{1,0:T(8,128)(2,1)S(1)} %collective-permute-done.25.refs_2_, ...), custom_call_target="tpu_custom_call" | custom-call | flops 536870 | bytes 2621 | tf_op jit(solution)/shard_map/score/score/pallas_call | solution.py:139
  112.1 1.3 collective-permute-start.36
  113.4 2.5 %collective-permute-start.37 = (bf16[64,1024]{1,0:T(8,128)(2,1)S(1)}, bf16[64,1024]{1,0:T(8,128)(2,1)S(1)}, u32[]{:S(2)}, u32[]{:S(2)}) collective-permute-start(bf16[64,1024]{1,0:T(8,128)(2,1)S(1)} %get-tuple-element.29), channel_id=1, source_target_pairs={{0,128},{64,192},{128,0},{192,64},{1,129},{65,193},{129,1},{193,65... | collective-permute-start | bytes 393224 | tf_op jit(solution)/shard_map/sum_layers/ppermute | solution.py:194
  115.8 1.1 collective-permute-start.38
  117.0 0.2 collective-permute-done.36.a_ref
  117.2 3.5 %collective-permute-done.37.b_ref = bf16[64,1024]{1,0:T(8,128)(2,1)S(1)} collective-permute-done((bf16[64,1024]{1,0:T(8,128)(2,1)S(1)}, bf16[64,1024]{1,0:T(8,128)(2,1)S(1)}, u32[]{:S(2)}, u32[]{:S(2)}) %collective-permute-start.37) | collective-permute-done | bytes 131104 | tf_op jit(solution)/shard_map/sum_layers/ppermute | solution.py:194
  120.6 0.3 collective-permute-done.38.c_ref
  121.0 0.1 add_layers.1
  121.1 2.3 %collective-permute-start.39 = (f32[64,256]{1,0:T(8,128)S(1)}, f32[64,256]{1,0:T(8,128)S(1)}, u32[]{:S(2)}, u32[]{:S(2)}) collective-permute-start(f32[64,256]{1,0:T(8,128)S(1)} %get-tuple-element.32), channel_id=1, source_target_pairs={{0,1},{1,0},{2,3},{3,2},{4,5},{5,4},{6,7},{7,6},{8,9},{9,8},{10,11... | collective-permute-start | bytes 196616 | tf_op jit(solution)/shard_map/exchange_examples/ppermute | solution.py:269
  123.3 2.9 %collective-permute-start.41 = (f32[64,256]{1,0:T(8,128)S(1)}, f32[64,256]{1,0:T(8,128)S(1)}, u32[]{:S(2)}, u32[]{:S(2)}) collective-permute-start(f32[64,256]{1,0:T(8,128)S(1)} %get-tuple-element.34), channel_id=1, source_target_pairs={{0,7},{1,6},{2,5},{3,4},{4,3},{5,2},{6,1},{7,0},{8,15},{9,14},{10,... | collective-permute-start | bytes 196616 | tf_op jit(solution)/shard_map/exchange_examples/ppermute | solution.py:269
  126.3 1.9 %collective-permute-done.40.refs_2_ = f32[64,256]{1,0:T(8,128)S(1)} collective-permute-done((f32[64,256]{1,0:T(8,128)S(1)}, f32[64,256]{1,0:T(8,128)S(1)}, u32[]{:S(2)}, u32[]{:S(2)}) %collective-permute-start.40) | collective-permute-done | bytes 65568 | tf_op jit(solution)/shard_map/exchange_examples/ppermute | solution.py:269
  128.2 1.6 %collective-permute-done.41.refs_3_ = f32[64,256]{1,0:T(8,128)S(1)} collective-permute-done((f32[64,256]{1,0:T(8,128)S(1)}, f32[64,256]{1,0:T(8,128)S(1)}, u32[]{:S(2)}, u32[]{:S(2)}) %collective-permute-start.41) | collective-permute-done | bytes 65568 | tf_op jit(solution)/shard_map/exchange_examples/ppermute | solution.py:269
  129.8 1.3 place_parts.1
  (39 shorter events, 0.2 us)
Async XLA Ops:
  0.0 7.8 %copy-start = (bf16[1,256,4096]{2,1,0:T(8,128)(2,1)S(1)}, bf16[1,256,4096]{2,1,0:T(8,128)(2,1)}, u32[]{:S(2)}) copy-start(bf16[1,256,4096]{2,1,0:T(8,128)(2,1)} %param.8) | copy-start | bytes 6291460
  0.9 1.6 %copy-start.1 = (bf16[1,16,512,128]{3,2,1,0:T(8,128)(2,1)S(1)}, bf16[1,16,512,128]{3,2,1,0:T(8,128)(2,1)}, u32[]{:S(2)}) copy-start(bf16[1,16,512,128]{3,2,1,0:T(8,128)(2,1)} %param.5) | copy-start | bytes 6291460
  2.5 0.7 copy-start.3
  5.6 51.0 %collective-permute-start.16 = (f32[64,4096]{1,0:T(8,128)}, f32[64,4096]{1,0:T(8,128)S(1)}, u32[]{:S(2)}, u32[]{:S(2)}) collective-permute-start(f32[64,4096]{1,0:T(8,128)} %bitcast.10), channel_id=1, source_target_pairs={{0,2},{2,0},{4,6},{6,4},{1,3},{3,1},{5,7},{7,5},{8,10},{10,8},{12,... | collective-permute-start | bytes 3145736 | tf_op jit(solution)/shard_map/swap_inverse/ppermute | solution.py:233
  7.8 82.7 %collective-permute-start.31 = (bf16[256,4096]{1,0:T(8,128)(2,1)S(1)}, bf16[256,4096]{1,0:T(8,128)(2,1)S(1)}, u32[]{:S(2)}, u32[]{:S(2)}) collective-permute-start(bf16[256,4096]{1,0:T(8,128)(2,1)S(1)} %bitcast.5), channel_id=1, source_target_pairs={{0,6},{6,0},{2,4},{4,2},{1,7},{7,1},{3,5},{5,3},{8,14},{14,8},{10,... | collective-permute-start | bytes 6291464 | tf_op jit(solution)/shard_map/swap_stored/ppermute | solution.py:233
  9.7 26.3 %collective-permute-start.7 = (bf16[16,4096]{1,0:T(8,128)(2,1)S(1)}, bf16[16,4096]{1,0:T(8,128)(2,1)S(1)}, u32[]{:S(2)}, u32[]{:S(2)}) collective-permute-start(bf16[16,4096]{1,0:T(8,128)(2,1)S(1)} %reshape.3.refs_1_), channel_id=1, source_target_pairs={{0,4},{2,6},{4,0},{6,2},{1,5},{3,7},{5,1},{7,3},{8,12},{10,14},{12... | collective-permute-start | bytes 393224 | tf_op jit(solution)/shard_map/gather_projected/ppermute | solution.py:194
  10.4 27.2 %collective-permute-start = (bf16[16,4096]{1,0:T(8,128)(2,1)S(1)}, bf16[16,4096]{1,0:T(8,128)(2,1)S(1)}, u32[]{:S(2)}, u32[]{:S(2)}) collective-permute-start(bf16[16,4096]{1,0:T(8,128)(2,1)S(1)} %reshape.3.refs_1_), channel_id=1, source_target_pairs={{0,8},{8,16},{16,24},{24,32},{32,40},{40,48},{48,56},{56,0},{1,9},... | collective-permute-start | bytes 393224 | tf_op jit(solution)/shard_map/gather_projected/ppermute | solution.py:194
  12.1 29.5 %collective-permute-start.1 = (bf16[16,4096]{1,0:T(8,128)(2,1)S(1)}, bf16[16,4096]{1,0:T(8,128)(2,1)S(1)}, u32[]{:S(2)}, u32[]{:S(2)}) collective-permute-start(bf16[16,4096]{1,0:T(8,128)(2,1)S(1)} %reshape.3.refs_1_), channel_id=1, source_target_pairs={{0,56},{8,0},{16,8},{24,16},{32,24},{40,32},{48,40},{56,48},{1,57}... | collective-permute-start | bytes 393224 | tf_op jit(solution)/shard_map/gather_projected/ppermute | solution.py:194
  36.0 8.2 %collective-permute-start.8 = (bf16[16,4096]{1,0:T(8,128)(2,1)S(1)}, bf16[16,4096]{1,0:T(8,128)(2,1)S(1)}, u32[]{:S(2)}, u32[]{:S(2)}) collective-permute-start(bf16[16,4096]{1,0:T(8,128)(2,1)S(1)} %collective-permute-done.7.refs_9_), channel_id=1, source_target_pairs={{0,8},{8,16},{16,24},{24,32},{32,40},{40,48},{48,56},{56,0},{1,9},... | collective-permute-start | bytes 393224 | tf_op jit(solution)/shard_map/gather_projected/ppermute | solution.py:194
  37.6 8.0 %collective-permute-start.9 = (bf16[16,4096]{1,0:T(8,128)(2,1)S(1)}, bf16[16,4096]{1,0:T(8,128)(2,1)S(1)}, u32[]{:S(2)}, u32[]{:S(2)}) collective-permute-start(bf16[16,4096]{1,0:T(8,128)(2,1)S(1)} %collective-permute-done.7.refs_9_), channel_id=1, source_target_pairs={{0,56},{8,0},{16,8},{24,16},{32,24},{40,32},{48,40},{56,48},{1,57}... | collective-permute-start | bytes 393224 | tf_op jit(solution)/shard_map/gather_projected/ppermute | solution.py:194
  41.6 5.9 %collective-permute-start.2 = (bf16[16,4096]{1,0:T(8,128)(2,1)S(1)}, bf16[16,4096]{1,0:T(8,128)(2,1)S(1)}, u32[]{:S(2)}, u32[]{:S(2)}) collective-permute-start(bf16[16,4096]{1,0:T(8,128)(2,1)S(1)} %collective-permute-done.refs_2_), channel_id=1, source_target_pairs={{0,8},{8,16},{16,24},{24,32},{32,40},{40,48},{48,56},{56,0},{1,9},... | collective-permute-start | bytes 393224 | tf_op jit(solution)/shard_map/gather_projected/ppermute | solution.py:194
  44.2 4.2 %collective-permute-start.3 = (bf16[16,4096]{1,0:T(8,128)(2,1)S(1)}, bf16[16,4096]{1,0:T(8,128)(2,1)S(1)}, u32[]{:S(2)}, u32[]{:S(2)}) collective-permute-start(bf16[16,4096]{1,0:T(8,128)(2,1)S(1)} %collective-permute-done.1.refs_3_), channel_id=1, source_target_pairs={{0,56},{8,0},{16,8},{24,16},{32,24},{40,32},{48,40},{56,48},{1,57}... | collective-permute-start | bytes 393224 | tf_op jit(solution)/shard_map/gather_projected/ppermute | solution.py:194
  45.7 5.3 %collective-permute-start.10 = (bf16[16,4096]{1,0:T(8,128)(2,1)S(1)}, bf16[16,4096]{1,0:T(8,128)(2,1)S(1)}, u32[]{:S(2)}, u32[]{:S(2)}) collective-permute-start(bf16[16,4096]{1,0:T(8,128)(2,1)S(1)} %collective-permute-done.8.refs_10_), channel_id=1, source_target_pairs={{0,8},{8,16},{16,24},{24,32},{32,40},{40,48},{48,56},{56,0},{1,9},... | collective-permute-start | bytes 393224 | tf_op jit(solution)/shard_map/gather_projected/ppermute | solution.py:194
  47.5 5.5 %collective-permute-start.11 = (bf16[16,4096]{1,0:T(8,128)(2,1)S(1)}, bf16[16,4096]{1,0:T(8,128)(2,1)S(1)}, u32[]{:S(2)}, u32[]{:S(2)}) collective-permute-start(bf16[16,4096]{1,0:T(8,128)(2,1)S(1)} %collective-permute-done.9.refs_11_), channel_id=1, source_target_pairs={{0,56},{8,0},{16,8},{24,16},{32,24},{40,32},{48,40},{56,48},{1,57}... | collective-permute-start | bytes 393224 | tf_op jit(solution)/shard_map/gather_projected/ppermute | solution.py:194
  48.4 8.3 %collective-permute-start.4 = (bf16[16,4096]{1,0:T(8,128)(2,1)S(1)}, bf16[16,4096]{1,0:T(8,128)(2,1)S(1)}, u32[]{:S(2)}, u32[]{:S(2)}) collective-permute-start(bf16[16,4096]{1,0:T(8,128)(2,1)S(1)} %collective-permute-done.2.refs_4_), channel_id=1, source_target_pairs={{0,8},{8,16},{16,24},{24,32},{32,40},{40,48},{48,56},{56,0},{1,9},... | collective-permute-start | bytes 393224 | tf_op jit(solution)/shard_map/gather_projected/ppermute | solution.py:194
  51.0 5.6 %collective-permute-start.5 = (bf16[16,4096]{1,0:T(8,128)(2,1)S(1)}, bf16[16,4096]{1,0:T(8,128)(2,1)S(1)}, u32[]{:S(2)}, u32[]{:S(2)}) collective-permute-start(bf16[16,4096]{1,0:T(8,128)(2,1)S(1)} %collective-permute-done.3.refs_5_), channel_id=1, source_target_pairs={{0,56},{8,0},{16,8},{24,16},{32,24},{40,32},{48,40},{56,48},{1,57}... | collective-permute-start | bytes 393224 | tf_op jit(solution)/shard_map/gather_projected/ppermute | solution.py:194
  52.9 13.2 %collective-permute-start.15 = (f32[64,4096]{1,0:T(8,128)}, f32[64,4096]{1,0:T(8,128)S(1)}, u32[]{:S(2)}, u32[]{:S(2)}) collective-permute-start(f32[64,4096]{1,0:T(8,128)} %bitcast.11), channel_id=1, source_target_pairs={{0,1},{1,0},{2,3},{3,2},{4,5},{5,4},{6,7},{7,6},{8,9},{9,8},{10,11... | collective-permute-start | bytes 3145736 | tf_op jit(solution)/shard_map/swap_inverse/ppermute | solution.py:202
  56.6 12.2 %collective-permute-start.17 = (f32[64,4096]{1,0:T(8,128)S(1)}, f32[64,4096]{1,0:T(8,128)S(1)}, u32[]{:S(2)}, u32[]{:S(2)}) collective-permute-start(f32[64,4096]{1,0:T(8,128)S(1)} %collective-permute-done.16.chip_ref), channel_id=1, source_target_pairs={{0,1},{1,0},{2,3},{3,2},{4,5},{5,4},{6,7},{7,6},{8,9},{9,8},{10,11... | collective-permute-start | bytes 3145736 | tf_op jit(solution)/shard_map/swap_inverse/ppermute | solution.py:202
  60.5 5.1 %collective-permute-start.13 = (bf16[16,4096]{1,0:T(8,128)(2,1)S(1)}, bf16[16,4096]{1,0:T(8,128)(2,1)S(1)}, u32[]{:S(2)}, u32[]{:S(2)}) collective-permute-start(bf16[16,4096]{1,0:T(8,128)(2,1)S(1)} %collective-permute-done.11.refs_13_), channel_id=1, source_target_pairs={{0,56},{8,0},{16,8},{24,16},{32,24},{40,32},{48,40},{56,48},{1,57}... | collective-permute-start | bytes 393224 | tf_op jit(solution)/shard_map/gather_projected/ppermute | solution.py:194
  62.5 8.8 %collective-permute-start.12 = (bf16[16,4096]{1,0:T(8,128)(2,1)S(1)}, bf16[16,4096]{1,0:T(8,128)(2,1)S(1)}, u32[]{:S(2)}, u32[]{:S(2)}) collective-permute-start(bf16[16,4096]{1,0:T(8,128)(2,1)S(1)} %collective-permute-done.10.refs_12_), channel_id=1, source_target_pairs={{0,8},{8,16},{16,24},{24,32},{32,40},{40,48},{48,56},{56,0},{1,9},... | collective-permute-start | bytes 393224 | tf_op jit(solution)/shard_map/gather_projected/ppermute | solution.py:194
  65.6 6.4 %collective-permute-start.6 = (bf16[16,4096]{1,0:T(8,128)(2,1)S(1)}, bf16[16,4096]{1,0:T(8,128)(2,1)S(1)}, u32[]{:S(2)}, u32[]{:S(2)}) collective-permute-start(bf16[16,4096]{1,0:T(8,128)(2,1)S(1)} %collective-permute-done.4.refs_6_), channel_id=1, source_target_pairs={{0,8},{8,16},{16,24},{24,32},{32,40},{40,48},{48,56},{56,0},{1,9},... | collective-permute-start | bytes 393224 | tf_op jit(solution)/shard_map/gather_projected/ppermute | solution.py:194
  66.2 5.8 %collective-permute-start.14 = (bf16[16,4096]{1,0:T(8,128)(2,1)S(1)}, bf16[16,4096]{1,0:T(8,128)(2,1)S(1)}, u32[]{:S(2)}, u32[]{:S(2)}) collective-permute-start(bf16[16,4096]{1,0:T(8,128)(2,1)S(1)} %collective-permute-done.13.refs_15_), channel_id=1, source_target_pairs={{0,56},{8,0},{16,8},{24,16},{32,24},{40,32},{48,40},{56,48},{1,57}... | collective-permute-start | bytes 393224 | tf_op jit(solution)/shard_map/gather_projected/ppermute | solution.py:194
  68.9 1.2 copy-start.2
  73.8 5.1 %collective-permute-start.18 = (bf16[256,256]{1,0:T(8,128)(2,1)S(1)}, bf16[256,256]{1,0:T(8,128)(2,1)S(1)}, u32[]{:S(2)}, u32[]{:S(2)}) collective-permute-start(bf16[256,256]{1,0:T(8,128)(2,1)S(1)} %precondition.1.refs_1_), channel_id=1, source_target_pairs={{0,8},{8,16},{16,24},{24,32},{32,40},{40,48},{48,56},{56,0},{1,9},... | collective-permute-start | bytes 393224 | tf_op jit(solution)/shard_map/gather_preconditioned/ppermute | solution.py:194
  76.0 5.3 %collective-permute-start.22 = (bf16[256,256]{1,0:T(8,128)(2,1)S(1)}, bf16[256,256]{1,0:T(8,128)(2,1)S(1)}, u32[]{:S(2)}, u32[]{:S(2)}) collective-permute-start(bf16[256,256]{1,0:T(8,128)(2,1)S(1)} %precondition.1.refs_1_), channel_id=1, source_target_pairs={{0,4},{2,6},{4,0},{6,2},{1,5},{3,7},{5,1},{7,3},{8,12},{10,14},{12... | collective-permute-start | bytes 393224 | tf_op jit(solution)/shard_map/gather_preconditioned/ppermute | solution.py:194
  76.1 8.0 %collective-permute-start.32 = (bf16[256,256]{1,0:T(8,128)(2,1)S(1)}, bf16[256,256]{1,0:T(8,128)(2,1)S(1)}, u32[]{:S(2)}, u32[]{:S(2)}) collective-permute-start(bf16[256,256]{1,0:T(8,128)(2,1)S(1)} %precondition.1.refs_1_), channel_id=1, source_target_pairs={{0,56},{8,0},{16,8},{24,16},{32,24},{40,32},{48,40},{56,48},{1,57}... | collective-permute-start | bytes 393224 | tf_op jit(solution)/shard_map/gather_preconditioned/ppermute | solution.py:194
  78.9 5.2 %collective-permute-start.19 = (bf16[256,256]{1,0:T(8,128)(2,1)S(1)}, bf16[256,256]{1,0:T(8,128)(2,1)S(1)}, u32[]{:S(2)}, u32[]{:S(2)}) collective-permute-start(bf16[256,256]{1,0:T(8,128)(2,1)S(1)} %collective-permute-done.18.refs_2_), channel_id=1, source_target_pairs={{0,8},{8,16},{16,24},{24,32},{32,40},{40,48},{48,56},{56,0},{1,9},... | collective-permute-start | bytes 393224 | tf_op jit(solution)/shard_map/gather_preconditioned/ppermute | solution.py:194
  81.3 6.3 %collective-permute-start.23 = (bf16[256,256]{1,0:T(8,128)(2,1)S(1)}, bf16[256,256]{1,0:T(8,128)(2,1)S(1)}, u32[]{:S(2)}, u32[]{:S(2)}) collective-permute-start(bf16[256,256]{1,0:T(8,128)(2,1)S(1)} %collective-permute-done.22.refs_8_), channel_id=1, source_target_pairs={{0,8},{8,16},{16,24},{24,32},{32,40},{40,48},{48,56},{56,0},{1,9},... | collective-permute-start | bytes 393224 | tf_op jit(solution)/shard_map/gather_preconditioned/ppermute | solution.py:194
  82.4 5.2 %collective-permute-start.26 = (bf16[256,256]{1,0:T(8,128)(2,1)S(1)}, bf16[256,256]{1,0:T(8,128)(2,1)S(1)}, u32[]{:S(2)}, u32[]{:S(2)}) collective-permute-start(bf16[256,256]{1,0:T(8,128)(2,1)S(1)} %collective-permute-done.22.refs_8_), channel_id=1, source_target_pairs={{0,56},{8,0},{16,8},{24,16},{32,24},{40,32},{48,40},{56,48},{1,57}... | collective-permute-start | bytes 393224 | tf_op jit(solution)/shard_map/gather_preconditioned/ppermute | solution.py:194
  84.0 6.3 %collective-permute-start.33 = (bf16[256,256]{1,0:T(8,128)(2,1)S(1)}, bf16[256,256]{1,0:T(8,128)(2,1)S(1)}, u32[]{:S(2)}, u32[]{:S(2)}) collective-permute-start(bf16[256,256]{1,0:T(8,128)(2,1)S(1)} %collective-permute-done.32.refs_3_), channel_id=1, source_target_pairs={{0,56},{8,0},{16,8},{24,16},{32,24},{40,32},{48,40},{56,48},{1,57}... | collective-permute-start | bytes 393224 | tf_op jit(solution)/shard_map/gather_preconditioned/ppermute | solution.py:194
  84.0 11.5 %collective-permute-start.20 = (bf16[256,256]{1,0:T(8,128)(2,1)S(1)}, bf16[256,256]{1,0:T(8,128)(2,1)S(1)}, u32[]{:S(2)}, u32[]{:S(2)}) collective-permute-start(bf16[256,256]{1,0:T(8,128)(2,1)S(1)} %collective-permute-done.19.refs_4_), channel_id=1, source_target_pairs={{0,8},{8,16},{16,24},{24,32},{32,40},{40,48},{48,56},{56,0},{1,9},... | collective-permute-start | bytes 393224 | tf_op jit(solution)/shard_map/gather_preconditioned/ppermute | solution.py:194
  87.6 8.0 %collective-permute-start.24 = (bf16[256,256]{1,0:T(8,128)(2,1)S(1)}, bf16[256,256]{1,0:T(8,128)(2,1)S(1)}, u32[]{:S(2)}, u32[]{:S(2)}) collective-permute-start(bf16[256,256]{1,0:T(8,128)(2,1)S(1)} %collective-permute-done.23.refs_9_), channel_id=1, source_target_pairs={{0,8},{8,16},{16,24},{24,32},{32,40},{40,48},{48,56},{56,0},{1,9},... | collective-permute-start | bytes 393224 | tf_op jit(solution)/shard_map/gather_preconditioned/ppermute | solution.py:194
  87.6 8.0 %collective-permute-start.27 = (bf16[256,256]{1,0:T(8,128)(2,1)S(1)}, bf16[256,256]{1,0:T(8,128)(2,1)S(1)}, u32[]{:S(2)}, u32[]{:S(2)}) collective-permute-start(bf16[256,256]{1,0:T(8,128)(2,1)S(1)} %collective-permute-done.26.refs_10_), channel_id=1, source_target_pairs={{0,56},{8,0},{16,8},{24,16},{32,24},{40,32},{48,40},{56,48},{1,57}... | collective-permute-start | bytes 393224 | tf_op jit(solution)/shard_map/gather_preconditioned/ppermute | solution.py:194
  90.3 5.3 %collective-permute-start.34 = (bf16[256,256]{1,0:T(8,128)(2,1)S(1)}, bf16[256,256]{1,0:T(8,128)(2,1)S(1)}, u32[]{:S(2)}, u32[]{:S(2)}) collective-permute-start(bf16[256,256]{1,0:T(8,128)(2,1)S(1)} %collective-permute-done.33.refs_5_), channel_id=1, source_target_pairs={{0,56},{8,0},{16,8},{24,16},{32,24},{40,32},{48,40},{56,48},{1,57}... | collective-permute-start | bytes 393224 | tf_op jit(solution)/shard_map/gather_preconditioned/ppermute | solution.py:194
  90.4 17.7 %collective-permute-start.30 = (bf16[256,4096]{1,0:T(8,128)(2,1)S(1)}, bf16[256,4096]{1,0:T(8,128)(2,1)S(1)}, u32[]{:S(2)}, u32[]{:S(2)}) collective-permute-start(bf16[256,4096]{1,0:T(8,128)(2,1)S(1)} %bitcast.6), channel_id=1, source_target_pairs={{0,1},{1,0},{2,3},{3,2},{4,5},{5,4},{6,7},{7,6},{8,9},{9,8},{10,11... | collective-permute-start | bytes 6291464 | tf_op jit(solution)/shard_map/swap_stored/ppermute | solution.py:202
  95.6 12.6 %collective-permute-start.35 = (bf16[256,4096]{1,0:T(8,128)(2,1)S(1)}, bf16[256,4096]{1,0:T(8,128)(2,1)S(1)}, u32[]{:S(2)}, u32[]{:S(2)}) collective-permute-start(bf16[256,4096]{1,0:T(8,128)(2,1)S(1)} %collective-permute-done.31.refs_15_.refs_7_), channel_id=1, source_target_pairs={{0,1},{1,0},{2,3},{3,2},{4,5},{5,4},{6,7},{7,6},{8,9},{9,8},{10,11... | collective-permute-start | bytes 6291464 | tf_op jit(solution)/shard_map/swap_stored/ppermute | solution.py:202
  99.6 5.1 %collective-permute-start.28 = (bf16[256,256]{1,0:T(8,128)(2,1)S(1)}, bf16[256,256]{1,0:T(8,128)(2,1)S(1)}, u32[]{:S(2)}, u32[]{:S(2)}) collective-permute-start(bf16[256,256]{1,0:T(8,128)(2,1)S(1)} %collective-permute-done.27.refs_12_), channel_id=1, source_target_pairs={{0,56},{8,0},{16,8},{24,16},{32,24},{40,32},{48,40},{56,48},{1,57}... | collective-permute-start | bytes 393224 | tf_op jit(solution)/shard_map/gather_preconditioned/ppermute | solution.py:194
  101.8 8.7 %collective-permute-start.21 = (bf16[256,256]{1,0:T(8,128)(2,1)S(1)}, bf16[256,256]{1,0:T(8,128)(2,1)S(1)}, u32[]{:S(2)}, u32[]{:S(2)}) collective-permute-start(bf16[256,256]{1,0:T(8,128)(2,1)S(1)} %collective-permute-done.20.refs_6_), channel_id=1, source_target_pairs={{0,8},{8,16},{16,24},{24,32},{32,40},{40,48},{48,56},{56,0},{1,9},... | collective-permute-start | bytes 393224 | tf_op jit(solution)/shard_map/gather_preconditioned/ppermute | solution.py:194
  101.8 8.8 %collective-permute-start.25 = (bf16[256,256]{1,0:T(8,128)(2,1)S(1)}, bf16[256,256]{1,0:T(8,128)(2,1)S(1)}, u32[]{:S(2)}, u32[]{:S(2)}) collective-permute-start(bf16[256,256]{1,0:T(8,128)(2,1)S(1)} %collective-permute-done.24.refs_11_), channel_id=1, source_target_pairs={{0,8},{8,16},{16,24},{24,32},{32,40},{40,48},{48,56},{56,0},{1,9},... | collective-permute-start | bytes 393224 | tf_op jit(solution)/shard_map/gather_preconditioned/ppermute | solution.py:194
  104.7 5.9 %collective-permute-start.29 = (bf16[256,256]{1,0:T(8,128)(2,1)S(1)}, bf16[256,256]{1,0:T(8,128)(2,1)S(1)}, u32[]{:S(2)}, u32[]{:S(2)}) collective-permute-start(bf16[256,256]{1,0:T(8,128)(2,1)S(1)} %collective-permute-done.28.refs_3_), channel_id=1, source_target_pairs={{0,56},{8,0},{16,8},{24,16},{32,24},{40,32},{48,40},{56,48},{1,57}... | collective-permute-start | bytes 393224 | tf_op jit(solution)/shard_map/gather_preconditioned/ppermute | solution.py:194
  112.1 5.1 %collective-permute-start.36 = (bf16[64,1024]{1,0:T(8,128)(2,1)S(1)}, bf16[64,1024]{1,0:T(8,128)(2,1)S(1)}, u32[]{:S(2)}, u32[]{:S(2)}) collective-permute-start(bf16[64,1024]{1,0:T(8,128)(2,1)S(1)} %get-tuple-element.28), channel_id=1, source_target_pairs={{0,64},{64,128},{128,192},{192,0},{1,65},{65,129},{129,193},{193,1... | collective-permute-start | bytes 393224 | tf_op jit(solution)/shard_map/sum_layers/ppermute | solution.py:194
  113.4 7.3 %collective-permute-start.37 = (bf16[64,1024]{1,0:T(8,128)(2,1)S(1)}, bf16[64,1024]{1,0:T(8,128)(2,1)S(1)}, u32[]{:S(2)}, u32[]{:S(2)}) collective-permute-start(bf16[64,1024]{1,0:T(8,128)(2,1)S(1)} %get-tuple-element.29), channel_id=1, source_target_pairs={{0,128},{64,192},{128,0},{192,64},{1,129},{65,193},{129,1},{193,65... | collective-permute-start | bytes 393224 | tf_op jit(solution)/shard_map/sum_layers/ppermute | solution.py:194
  115.8 5.2 %collective-permute-start.38 = (bf16[64,1024]{1,0:T(8,128)(2,1)S(1)}, bf16[64,1024]{1,0:T(8,128)(2,1)S(1)}, u32[]{:S(2)}, u32[]{:S(2)}) collective-permute-start(bf16[64,1024]{1,0:T(8,128)(2,1)S(1)} %get-tuple-element.30), channel_id=1, source_target_pairs={{0,192},{64,0},{128,64},{192,128},{1,193},{65,1},{129,65},{193,129... | collective-permute-start | bytes 393224 | tf_op jit(solution)/shard_map/sum_layers/ppermute | solution.py:194
  121.1 5.2 %collective-permute-start.39 = (f32[64,256]{1,0:T(8,128)S(1)}, f32[64,256]{1,0:T(8,128)S(1)}, u32[]{:S(2)}, u32[]{:S(2)}) collective-permute-start(f32[64,256]{1,0:T(8,128)S(1)} %get-tuple-element.32), channel_id=1, source_target_pairs={{0,1},{1,0},{2,3},{3,2},{4,5},{5,4},{6,7},{7,6},{8,9},{9,8},{10,11... | collective-permute-start | bytes 196616 | tf_op jit(solution)/shard_map/exchange_examples/ppermute | solution.py:269
  123.3 4.9 %collective-permute-start.40 = (f32[64,256]{1,0:T(8,128)S(1)}, f32[64,256]{1,0:T(8,128)S(1)}, u32[]{:S(2)}, u32[]{:S(2)}) collective-permute-start(f32[64,256]{1,0:T(8,128)S(1)} %get-tuple-element.33), channel_id=1, source_target_pairs={{0,6},{1,7},{2,4},{3,5},{4,2},{5,3},{6,0},{7,1},{8,14},{9,15},{10,... | collective-permute-start | bytes 196616 | tf_op jit(solution)/shard_map/exchange_examples/ppermute | solution.py:269
  123.3 6.4 %collective-permute-start.41 = (f32[64,256]{1,0:T(8,128)S(1)}, f32[64,256]{1,0:T(8,128)S(1)}, u32[]{:S(2)}, u32[]{:S(2)}) collective-permute-start(f32[64,256]{1,0:T(8,128)S(1)} %get-tuple-element.34), channel_id=1, source_target_pairs={{0,7},{1,6},{2,5},{3,4},{4,3},{5,2},{6,1},{7,0},{8,15},{9,14},{10,... | collective-permute-start | bytes 196616 | tf_op jit(solution)/shard_map/exchange_examples/ppermute | solution.py:269

commit v2 on v1

--- a/solution.py
+++ b/solution.py
@@ -7,6 +7,7 @@
 
 LAYER, Z, Y, CORE = 4, 8, 4, 2
 PIECES = Z * Y // 2
+SELF = 3 * PIECES
 BF = jnp.bfloat16
 F32 = jnp.float32
 VMEM = pl.BlockSpec(memory_space=pltpu.VMEM)
@@ -20,7 +21,7 @@
 
 
 def cost(flops, moved):
-    return pl.CostEstimate(flops=flops // 1000, bytes_accessed=moved // 1000, transcendentals=0)
+    return pl.CostEstimate(flops=flops, bytes_accessed=moved, transcendentals=0)
 
 
 def gradient_kernel(lengths_ref, factors_ref, out_ref):
@@ -55,7 +56,7 @@
 
 def split_kernel(where_ref, own_ref, core_ref, chip_ref, both_ref, high_ref, low_ref):
     rows = own_ref.shape[0]
-    me = where_ref[PIECES]
+    me = where_ref[SELF]
     for k, ref in enumerate((own_ref, core_ref, chip_ref, both_ref)):
         place = pl.ds(pl.multiple_of((me ^ k) * rows, rows), rows)
         whole = ref[...]
@@ -108,22 +109,26 @@
     count = len(some)
     pieces, stored, refs = refs[:count], refs[count : count + held], refs[count + held :]
     before, outs = (None, refs) if first else (refs[0], refs[1:])
-    columns = pieces[0].shape[1]
+    width = pieces[0].shape[1] // 2
     total = outs[-1] if cut else outs[0]
-    start = 0
+    examples = 0
     for ref in stored:
-        span = (slice(None), slice(start, start + ref.shape[0]))
-        start += ref.shape[0]
+        span = (slice(None), slice(examples, examples + ref.shape[0]))
+        examples += ref.shape[0]
         acc = None if first else before[span]
         for k, piece in enumerate(pieces):
-            place = pl.ds(pl.multiple_of(where_ref[some[k]] * columns, columns), columns)
-            term = lax.dot_general(piece[...], ref[:, place], NT, preferred_element_type=F32)
+            blocks = [
+                ref[:, pl.ds(pl.multiple_of(where_ref[start + some[k]] * width, width), width)]
+                for start in (PIECES, 2 * PIECES)
+            ]
+            right = jnp.concatenate(blocks, axis=1)
+            term = lax.dot_general(piece[...], right, NT, preferred_element_type=F32)
             acc = term if acc is None else acc + term
         total[span] = acc
     if cut:
         block = total.shape[0] // LAYER
         for k, out in enumerate(outs[:-1]):
-            owner = lax.rem(where_ref[PIECES + 1] + k, LAYER)
+            owner = lax.rem(where_ref[SELF + 1] + k, LAYER)
             out[...] = total[pl.ds(pl.multiple_of(owner * block, block), block), :].astype(out.dtype)
 
 
@@ -152,14 +157,15 @@
     width = outs[0].shape[1]
     for k, out in enumerate(outs):
         part = (slice(None), slice(k * width, (k + 1) * width))
-        out[...] = (own_ref[part] + a_ref[part].astype(F32)) + (b_ref[part].astype(F32) + c_ref[part].astype(F32))
+        total = (own_ref[part] + a_ref[part].astype(F32)) + (b_ref[part].astype(F32) + c_ref[part].astype(F32))
+        out[...] = total.astype(out.dtype)
 
 
 def add_layers(own, others):
     rows, width = own.shape
     return pl.pallas_call(
         add_kernel,
-        out_shape=[jax.ShapeDtypeStruct((rows, width // 4), F32)] * 4,
+        out_shape=[jax.ShapeDtypeStruct((rows, width // 4), F32 if k == 0 else BF) for k in range(4)],
         in_specs=[VMEM] * 4,
         out_specs=[VMEM] * 4,
         compiler_params=params(6),
@@ -172,9 +178,11 @@
     parts, out_ref = refs[:-1], refs[-1]
     rows = parts[0].shape[0] // 4
     for k, part in enumerate(parts):
+        giver = where_ref[SELF] ^ k
         for group in range(4):
-            start = pl.multiple_of(group * 4 * rows + (where_ref[PIECES] ^ k) * rows, rows)
-            out_ref[pl.ds(start, rows), :] = part[group * rows : (group + 1) * rows, :]
+            start = (group // 2) * 8 + (group % 2) * 2 + lax.shift_right_logical(giver, 1) * 4 + (giver & 1)
+            place = pl.ds(pl.multiple_of(start * rows, rows), rows)
+            out_ref[place, :] = part[group * rows : (group + 1) * rows, :].astype(out_ref.dtype)
 
 
 def place_parts(where, parts):
@@ -217,47 +225,51 @@
     return pieces
 
 
-def most(pieces):
-    return [value for dz, side, value in pieces if abs(dz) + side == 3]
+def some(pieces, *which):
+    return [value for dz, side, value in pieces if (dz, side) in which]
 
 
 def per_device(factors, lengths, inverse, stored):
     layer, z, y, core = (lax.axis_index(name) for name in ("layer", "z", "y", "core"))
     apart = [distance for step in range(1, Z // 2) for distance in (-step, step)]
     apart = jnp.array([0] + apart + [Z // 2], jnp.int32)
-    where = jnp.concatenate([((z + apart) % Z) * 2 + (y // 2 ^ side) for side in (0, 1)])
-    where = jnp.concatenate([where, jnp.stack([(y % 2) * 2 + core, layer])]).astype(jnp.int32)
+    depth, group = jnp.tile((z + apart) % Z, 2), y // 2
+    parity = jnp.repeat(jnp.stack([y % 2, 1 - y % 2]), Z)
+    first = parity ^ group
+    where = jnp.concatenate(
+        [depth * 2 + parity, depth * Y + first, depth * Y + Y - 1 - first, jnp.stack([group * 2 + core, layer])]
+    ).astype(jnp.int32)
     inverse_rows, stored_rows = inverse[0], stored[0]
 
     def swap_chip(value, *pairs):
         return lax.ppermute(value, "y", [pair for a, b in pairs for pair in ((a, b), (b, a))])
 
-    with jax.named_scope("swap_stored"):
-        chip_stored = swap_chip(stored_rows, (0, 3), (1, 2))
     with jax.named_scope("gradients"):
         projected = gradients(factors[0], after(lengths, where))
     with jax.named_scope("gather_projected"):
-        pieces = gather(projected, shift(projected, "y", Y, 2))
+        pieces = gather(projected, swap_chip(projected, (0, 1), (2, 3)))
     with jax.named_scope("swap_inverse"):
         core_rows = swap_core(inverse_rows)
-        chip_rows = swap_chip(after(inverse_rows, projected), (0, 1), (2, 3))
-        both_rows = swap_core(after(chip_rows, most(pieces)))
+        chip_rows = swap_chip(inverse_rows, (0, 3), (1, 2))
+        both_rows = swap_core(after(chip_rows, some(pieces, (2, 0), (-2, 0), (2, 1), (-2, 1))))
+    with jax.named_scope("swap_stored"):
+        chip_stored = swap_chip(after(stored_rows, some(pieces, (1, 0), (-1, 0), (0, 1))), (0, 3), (1, 2))
     with jax.named_scope("split_inverse"):
         high, low = split_rows(where, (inverse_rows, core_rows, chip_rows, both_rows))
     with jax.named_scope("precondition"):
         own = precondition(where, [value for _, _, value in pieces], high, low)
     with jax.named_scope("gather_preconditioned"):
-        pieces = gather(own, shift(own, "y", Y, 2))
+        pieces = gather(own, swap_chip(own, (0, 1), (2, 3)))
     with jax.named_scope("swap_stored"):
         core_stored = swap_core(after(stored_rows, own))
-        both_stored = swap_core(after(chip_stored, most(pieces)))
+        both_stored = swap_core(after(chip_stored, some(pieces, (2, 0), (-2, 0), (2, 1), (-2, 1))))
     with jax.named_scope("score"):
         late = [k for k, (dz, side, _) in enumerate(pieces) if abs(dz) == 4 or (side and abs(dz) == 3)]
         soon = [k for k in range(len(pieces)) if k not in late]
         stored_parts = (stored_rows, core_stored, chip_stored, both_stored)
         total = None
-        for some in (soon, late):
-            total = score(where, some, [pieces[k][2] for k in some], stored_parts, total, some is late)
+        for part in (soon, late):
+            total = score(where, part, [pieces[k][2] for k in part], stored_parts, total, part is late)
         kept, *sent = total
     with jax.named_scope("sum_layers"):
         others = [shift(value, "layer", LAYER, k + 1) for k, value in enumerate(sent)]

time: 131 us -> 112 us (0.85)
  waiting for transfers between devices: 47.8 us -> 31.3 us
  starting transfers between devices: 68.2 us -> 64.8 us
    ppermute x33 -> x31, waiting for transfers between devices: 44.3 us -> 21.3 us  [shift(): lax.ppermute(value, axis, [(i, (i + by) % size) for i in range(size)])]
    ppermute x4, starting transfers between devices: 16.6 us -> 10.1 us  [swap_core(): return lax.ppermute(value, 'core', [(0, 1), (1, 0)])]
    ppermute x2 -> x4, waiting for transfers between devices: 0.01 us -> 5.72 us  [swap_chip(): lax.ppermute(value, 'y', [pair for a, b in pairs for pair in ((a, b), (b,...]
    ppermute x33 -> x31, starting transfers between devices: 42.2 us -> 44.8 us  [shift(): lax.ppermute(value, axis, [(i, (i + by) % size) for i in range(size)])]
    ppermute x2 -> x4, starting transfers between devices: 4.11 us -> 4.6 us  [swap_chip(): lax.ppermute(value, 'y', [pair for a, b in pairs for pair in ((a, b), (b,...]
  transfers between devices with their start and end apart: 42 -> 42, of which waited for: 17 -> 15; matrix products, arithmetic and copies ran while one was open for 0% -> 1% of each run, Pallas kernels for 4% -> 7%
where the time goes in v2:
time: 112 us
  starting transfers between devices  64.8 us (58%)
  waiting for transfers between devices  31.3 us (28%)
  Pallas kernels  10.5 us (9%)
  local copies, waits for them, and re-layouts  4.16 us (4%)
    ppermute x31, starting transfers between devices, shift(): lax.ppermute(value, axis, [(i, (i + by) % size) for i in range(size)])  44.8 us
    ppermute x31, waiting for transfers between devices, shift(): lax.ppermute(value, axis, [(i, (i + by) % size) for i in range(size)])  21.3 us
    ppermute x4, starting transfers between devices, swap_core(): return lax.ppermute(value, 'core', [(0, 1), (1, 0)])  10.1 us
    ppermute x4, waiting for transfers between devices, swap_chip(): lax.ppermute(value, 'y', [pair for a, b in pairs for pair in ((a, b), (b,...  5.72 us
    ppermute x3, starting transfers between devices, per_device(): lax.ppermute(parts[k], ('y', 'core'), pairs[k - 1])  5.36 us
    ppermute x4, starting transfers between devices, swap_chip(): lax.ppermute(value, 'y', [pair for a, b in pairs for pair in ((a, b), (b,...  4.6 us
    ppermute x3, waiting for transfers between devices, per_device(): lax.ppermute(parts[k], ('y', 'core'), pairs[k - 1])  4.32 us
    pallas_call x2, Pallas kernels, score(): pl.pallas_call(lambda *refs: score_kernel(some, len(stored), before is No...  4.05 us
  transfers between devices with their start and end apart: 42, of which 15 were waited for; matrix products, arithmetic and copies ran while one was open for 1% of the time, Pallas kernels for 7%

profile of v2, /device:TPU:1, one launch (start us, length us, event | category | flops | bytes accessed | tf_op | source)
XLA Modules:
  0.0 111.9 jit_solution(8203835623761115680)
XLA Ops:
  0.0 3.6 %collective-permute-start.16 = (f32[64,4096]{1,0:T(8,128)}, f32[64,4096]{1,0:T(8,128)S(1)}, u32[]{:S(2)}, u32[]{:S(2)}) collective-permute-start(f32[64,4096]{1,0:T(8,128)} %bitcast.12), channel_id=1, source_target_pairs={{0,6},{6,0},{2,4},{4,2},{1,7},{7,1},{3,5},{5,3},{8,14},{14,8},{10,... | collective-permute-start | bytes 3145736 | tf_op jit(solution)/shard_map/swap_inverse/ppermute | solution.py:245
  3.6 0.7 broadcast_multiply_fusion
  4.5 0.1 mul.18
  4.8 1.6 %copy-done.1 = bf16[1,16,512,128]{3,2,1,0:T(8,128)(2,1)S(1)} copy-done((bf16[1,16,512,128]{3,2,1,0:T(8,128)(2,1)S(1)}, bf16[1,16,512,128]{3,2,1,0:T(8,128)(2,1)}, u32[]{:S(2)}) %copy-start.1) | copy-done | bytes 2097176
  6.4 0.7 copy-done.3
  7.1 2.1 %form_gradients.1 = bf16[16,64,64]{2,1,0:T(8,128)(2,1)S(1)} custom-call(s32[16]{0:T(128)S(1)} %copy-done.3, bf16[16,512,128]{2,1,0:T(8,128)(2,1)S(1)} %bitcast.11), custom_call_target="tpu_custom_call" | custom-call | flops 268435456 | bytes 2097152 | tf_op jit(solution)/shard_map/gradients/form_gradients/pallas_call | solution.py:41
  9.2 0.3 reshape.12.refs_1_
  9.5 0.1 collective-permute-start.7
  9.6 1.7 %collective-permute-start = (bf16[16,4096]{1,0:T(8,128)(2,1)S(1)}, bf16[16,4096]{1,0:T(8,128)(2,1)S(1)}, u32[]{:S(2)}, u32[]{:S(2)}) collective-permute-start(bf16[16,4096]{1,0:T(8,128)(2,1)S(1)} %reshape.12.refs_1_), channel_id=1, source_target_pairs={{0,8},{8,16},{16,24},{24,32},{32,40},{40,48},{48,56},{56,0},{1,9},... | collective-permute-start | bytes 393224 | tf_op jit(solution)/shard_map/gather_projected/ppermute | solution.py:202
  11.3 4.0 %collective-permute-start.1 = (bf16[16,4096]{1,0:T(8,128)(2,1)S(1)}, bf16[16,4096]{1,0:T(8,128)(2,1)S(1)}, u32[]{:S(2)}, u32[]{:S(2)}) collective-permute-start(bf16[16,4096]{1,0:T(8,128)(2,1)S(1)} %reshape.12.refs_1_), channel_id=1, source_target_pairs={{0,56},{8,0},{16,8},{24,16},{32,24},{40,32},{48,40},{56,48},{1,57}... | collective-permute-start | bytes 393224 | tf_op jit(solution)/shard_map/gather_projected/ppermute | solution.py:202
  15.3 2.8 %collective-permute-done.refs_2_ = bf16[16,4096]{1,0:T(8,128)(2,1)S(1)} collective-permute-done((bf16[16,4096]{1,0:T(8,128)(2,1)S(1)}, bf16[16,4096]{1,0:T(8,128)(2,1)S(1)}, u32[]{:S(2)}, u32[]{:S(2)}) %collective-permute-start) | collective-permute-done | bytes 131104 | tf_op jit(solution)/shard_map/gather_projected/ppermute | solution.py:202
  18.1 0.5 collective-permute-start.31
  18.6 2.7 %collective-permute-start.9 = (bf16[16,4096]{1,0:T(8,128)(2,1)S(1)}, bf16[16,4096]{1,0:T(8,128)(2,1)S(1)}, u32[]{:S(2)}, u32[]{:S(2)}) collective-permute-start(bf16[16,4096]{1,0:T(8,128)(2,1)S(1)} %collective-permute-done.7.refs_9_), channel_id=1, source_target_pairs={{0,56},{8,0},{16,8},{24,16},{32,24},{40,32},{48,40},{56,48},{1,57}... | collective-permute-start | bytes 393224 | tf_op jit(solution)/shard_map/gather_projected/ppermute | solution.py:202
  21.2 2.6 %collective-permute-done.8.refs_10_ = bf16[16,4096]{1,0:T(8,128)(2,1)S(1)} collective-permute-done((bf16[16,4096]{1,0:T(8,128)(2,1)S(1)}, bf16[16,4096]{1,0:T(8,128)(2,1)S(1)}, u32[]{:S(2)}, u32[]{:S(2)}) %collective-permute-start.8) | collective-permute-done | bytes 131104 | tf_op jit(solution)/shard_map/gather_projected/ppermute | solution.py:202
  23.9 1.5 %collective-permute-start.3 = (bf16[16,4096]{1,0:T(8,128)(2,1)S(1)}, bf16[16,4096]{1,0:T(8,128)(2,1)S(1)}, u32[]{:S(2)}, u32[]{:S(2)}) collective-permute-start(bf16[16,4096]{1,0:T(8,128)(2,1)S(1)} %collective-permute-done.1.refs_3_), channel_id=1, source_target_pairs={{0,56},{8,0},{16,8},{24,16},{32,24},{40,32},{48,40},{56,48},{1,57}... | collective-permute-start | bytes 393224 | tf_op jit(solution)/shard_map/gather_projected/ppermute | solution.py:202
  25.3 0.7 collective-permute-start.10
  26.1 1.8 %collective-permute-done.2.refs_4_ = bf16[16,4096]{1,0:T(8,128)(2,1)S(1)} collective-permute-done((bf16[16,4096]{1,0:T(8,128)(2,1)S(1)}, bf16[16,4096]{1,0:T(8,128)(2,1)S(1)}, u32[]{:S(2)}, u32[]{:S(2)}) %collective-permute-start.2) | collective-permute-done | bytes 131104 | tf_op jit(solution)/shard_map/gather_projected/ppermute | solution.py:202
  27.9 0.1 collective-permute-start.11
  28.0 5.8 %collective-permute-start.15 = (f32[64,4096]{1,0:T(8,128)}, f32[64,4096]{1,0:T(8,128)S(1)}, u32[]{:S(2)}, u32[]{:S(2)}) collective-permute-start(f32[64,4096]{1,0:T(8,128)} %bitcast.13), channel_id=1, source_target_pairs={{0,1},{1,0},{2,3},{3,2},{4,5},{5,4},{6,7},{7,6},{8,9},{9,8},{10,11... | collective-permute-start | bytes 3145736 | tf_op jit(solution)/shard_map/swap_inverse/ppermute | solution.py:210
  33.8 1.7 %collective-permute-start.17 = (f32[64,4096]{1,0:T(8,128)S(1)}, f32[64,4096]{1,0:T(8,128)S(1)}, u32[]{:S(2)}, u32[]{:S(2)}) collective-permute-start(f32[64,4096]{1,0:T(8,128)S(1)} %collective-permute-done.16.chip_ref), channel_id=1, source_target_pairs={{0,1},{1,0},{2,3},{3,2},{4,5},{5,4},{6,7},{7,6},{8,9},{9,8},{10,11... | collective-permute-start | bytes 3145736 | tf_op jit(solution)/shard_map/swap_inverse/ppermute | solution.py:210
  35.6 1.7 %collective-permute-start.4 = (bf16[16,4096]{1,0:T(8,128)(2,1)S(1)}, bf16[16,4096]{1,0:T(8,128)(2,1)S(1)}, u32[]{:S(2)}, u32[]{:S(2)}) collective-permute-start(bf16[16,4096]{1,0:T(8,128)(2,1)S(1)} %collective-permute-done.2.refs_4_), channel_id=1, source_target_pairs={{0,8},{8,16},{16,24},{24,32},{32,40},{40,48},{48,56},{56,0},{1,9},... | collective-permute-start | bytes 393224 | tf_op jit(solution)/shard_map/gather_projected/ppermute | solution.py:202
  37.3 1.0 collective-permute-start.13
  38.2 3.7 %collective-permute-done.4.refs_6_ = bf16[16,4096]{1,0:T(8,128)(2,1)S(1)} collective-permute-done((bf16[16,4096]{1,0:T(8,128)(2,1)S(1)}, bf16[16,4096]{1,0:T(8,128)(2,1)S(1)}, u32[]{:S(2)}, u32[]{:S(2)}) %collective-permute-start.4) | collective-permute-done | bytes 131104 | tf_op jit(solution)/shard_map/gather_projected/ppermute | solution.py:202
  41.9 1.3 %collective-permute-start.5 = (bf16[16,4096]{1,0:T(8,128)(2,1)S(1)}, bf16[16,4096]{1,0:T(8,128)(2,1)S(1)}, u32[]{:S(2)}, u32[]{:S(2)}) collective-permute-start(bf16[16,4096]{1,0:T(8,128)(2,1)S(1)} %collective-permute-done.3.refs_5_), channel_id=1, source_target_pairs={{0,56},{8,0},{16,8},{24,16},{32,24},{40,32},{48,40},{56,48},{1,57}... | collective-permute-start | bytes 393224 | tf_op jit(solution)/shard_map/gather_projected/ppermute | solution.py:202
  43.2 1.0 collective-permute-start.12
  44.2 1.1 %collective-permute-start.6 = (bf16[16,4096]{1,0:T(8,128)(2,1)S(1)}, bf16[16,4096]{1,0:T(8,128)(2,1)S(1)}, u32[]{:S(2)}, u32[]{:S(2)}) collective-permute-start(bf16[16,4096]{1,0:T(8,128)(2,1)S(1)} %collective-permute-done.4.refs_6_), channel_id=1, source_target_pairs={{0,8},{8,16},{16,24},{24,32},{32,40},{40,48},{48,56},{56,0},{1,9},... | collective-permute-start | bytes 393224 | tf_op jit(solution)/shard_map/gather_projected/ppermute | solution.py:202
  45.4 1.5 %collective-permute-start.14 = (bf16[16,4096]{1,0:T(8,128)(2,1)S(1)}, bf16[16,4096]{1,0:T(8,128)(2,1)S(1)}, u32[]{:S(2)}, u32[]{:S(2)}) collective-permute-start(bf16[16,4096]{1,0:T(8,128)(2,1)S(1)} %collective-permute-done.13.refs_15_), channel_id=1, source_target_pairs={{0,56},{8,0},{16,8},{24,16},{32,24},{40,32},{48,40},{56,48},{1,57}... | collective-permute-start | bytes 393224 | tf_op jit(solution)/shard_map/gather_projected/ppermute | solution.py:202
  46.9 1.2 %copy-done.2 = f32[1,64,4096]{2,1,0:T(8,128)S(1)} copy-done((f32[1,64,4096]{2,1,0:T(8,128)S(1)}, f32[1,64,4096]{2,1,0:T(8,128)}, u32[]{:S(2)}) %copy-start.2) | copy-done | bytes 1048600
  48.1 1.2 %split_inverse.1 = (bf16[256,4096]{1,0:T(8,128)(2,1)S(1)}, bf16[256,4096]{1,0:T(8,128)(2,1)S(1)}) custom-call(s32[50]{0:T(128)S(1)} %concatenate.3.where_ref.refs_0_, f32[64,4096]{1,0:T(8,128)S(1)} %bitcast.14, f32[64,4096]{1,0:T(8,128)S(1)} %collective-permute-done.15.core_ref, f32[64,4096]{1,0:T(8,128)S(1)} %collective-permute-done.16.chip_ref, ...), custom_call_target="tpu_custom_call" | custom-call | flops 2097152 | bytes 8388608 | tf_op jit(solution)/shard_map/split_inverse/split_inverse/pallas_call | solution.py:71
  49.4 1.8 %collective-permute-done.6.refs_8_ = bf16[16,4096]{1,0:T(8,128)(2,1)S(1)} collective-permute-done((bf16[16,4096]{1,0:T(8,128)(2,1)S(1)}, bf16[16,4096]{1,0:T(8,128)(2,1)S(1)}, u32[]{:S(2)}, u32[]{:S(2)}) %collective-permute-start.6) | collective-permute-done | bytes 131104 | tf_op jit(solution)/shard_map/gather_projected/ppermute | solution.py:202
  51.1 1.8 %precondition.1.refs_1_ = bf16[256,256]{1,0:T(8,128)(2,1)S(1)} custom-call(s32[50]{0:T(128)S(1)} %concatenate.3.where_ref.refs_0_, bf16[16,4096]{1,0:T(8,128)(2,1)S(1)} %reshape.12.refs_1_, bf16[16,4096]{1,0:T(8,128)(2,1)S(1)} %collective-permute-done.refs_2_, bf16[16,4096]{1,0:T(8,128)(2,1)S(1)} %collective-permute-done.1.refs_3_, ...), custom_call_target="tpu_custom_call" | custom-call | flops 1073741824 | bytes 6291456 | tf_op jit(solution)/shard_map/precondition/precondition/pallas_call | solution.py:97
  53.0 0.5 collective-permute-start.22
  53.5 0.2 collective-permute-start.18
  53.7 2.5 %collective-permute-start.32 = (bf16[256,256]{1,0:T(8,128)(2,1)S(1)}, bf16[256,256]{1,0:T(8,128)(2,1)S(1)}, u32[]{:S(2)}, u32[]{:S(2)}) collective-permute-start(bf16[256,256]{1,0:T(8,128)(2,1)S(1)} %precondition.1.refs_1_), channel_id=1, source_target_pairs={{0,56},{8,0},{16,8},{24,16},{32,24},{40,32},{48,40},{56,48},{1,57}... | collective-permute-start | bytes 393224 | tf_op jit(solution)/shard_map/gather_preconditioned/ppermute | solution.py:202
  56.1 1.0 collective-permute-done.22.refs_8_
  57.2 0.1 collective-permute-start.23
  57.3 2.5 %collective-permute-start.26 = (bf16[256,256]{1,0:T(8,128)(2,1)S(1)}, bf16[256,256]{1,0:T(8,128)(2,1)S(1)}, u32[]{:S(2)}, u32[]{:S(2)}) collective-permute-start(bf16[256,256]{1,0:T(8,128)(2,1)S(1)} %collective-permute-done.22.refs_8_), channel_id=1, source_target_pairs={{0,56},{8,0},{16,8},{24,16},{32,24},{40,32},{48,40},{56,48},{1,57}... | collective-permute-start | bytes 393224 | tf_op jit(solution)/shard_map/gather_preconditioned/ppermute | solution.py:202
  59.9 2.7 %collective-permute-start.33 = (bf16[256,256]{1,0:T(8,128)(2,1)S(1)}, bf16[256,256]{1,0:T(8,128)(2,1)S(1)}, u32[]{:S(2)}, u32[]{:S(2)}) collective-permute-start(bf16[256,256]{1,0:T(8,128)(2,1)S(1)} %collective-permute-done.32.refs_3_), channel_id=1, source_target_pairs={{0,56},{8,0},{16,8},{24,16},{32,24},{40,32},{48,40},{56,48},{1,57}... | collective-permute-start | bytes 393224 | tf_op jit(solution)/shard_map/gather_preconditioned/ppermute | solution.py:202
  62.5 0.4 collective-permute-done.23.refs_9_
  62.9 3.0 %collective-permute-start.27 = (bf16[256,256]{1,0:T(8,128)(2,1)S(1)}, bf16[256,256]{1,0:T(8,128)(2,1)S(1)}, u32[]{:S(2)}, u32[]{:S(2)}) collective-permute-start(bf16[256,256]{1,0:T(8,128)(2,1)S(1)} %collective-permute-done.26.refs_10_), channel_id=1, source_target_pairs={{0,56},{8,0},{16,8},{24,16},{32,24},{40,32},{48,40},{56,48},{1,57}... | collective-permute-start | bytes 393224 | tf_op jit(solution)/shard_map/gather_preconditioned/ppermute | solution.py:202
  65.9 4.7 %collective-permute-done.31.refs_15_.refs_7_ = bf16[256,4096]{1,0:T(8,128)(2,1)S(1)} collective-permute-done((bf16[256,4096]{1,0:T(8,128)(2,1)S(1)}, bf16[256,4096]{1,0:T(8,128)(2,1)S(1)}, u32[]{:S(2)}, u32[]{:S(2)}) %collective-permute-start.31) | collective-permute-done | bytes 2097184 | tf_op jit(solution)/shard_map/swap_stored/ppermute | solution.py:245
  70.5 2.3 %collective-permute-start.30 = (bf16[256,4096]{1,0:T(8,128)(2,1)S(1)}, bf16[256,4096]{1,0:T(8,128)(2,1)S(1)}, u32[]{:S(2)}, u32[]{:S(2)}) collective-permute-start(bf16[256,4096]{1,0:T(8,128)(2,1)S(1)} %bitcast.8), channel_id=1, source_target_pairs={{0,1},{1,0},{2,3},{3,2},{4,5},{5,4},{6,7},{7,6},{8,9},{9,8},{10,11... | collective-permute-start | bytes 6291464 | tf_op jit(solution)/shard_map/swap_stored/ppermute | solution.py:210
  72.9 0.3 collective-permute-start.34
  73.2 1.5 %collective-permute-start.20 = (bf16[256,256]{1,0:T(8,128)(2,1)S(1)}, bf16[256,256]{1,0:T(8,128)(2,1)S(1)}, u32[]{:S(2)}, u32[]{:S(2)}) collective-permute-start(bf16[256,256]{1,0:T(8,128)(2,1)S(1)} %collective-permute-done.19.refs_4_), channel_id=1, source_target_pairs={{0,8},{8,16},{16,24},{24,32},{32,40},{40,48},{48,56},{56,0},{1,9},... | collective-permute-start | bytes 393224 | tf_op jit(solution)/shard_map/gather_preconditioned/ppermute | solution.py:202
  74.7 4.3 %collective-permute-start.35 = (bf16[256,256]{1,0:T(8,128)(2,1)S(1)}, bf16[256,256]{1,0:T(8,128)(2,1)S(1)}, u32[]{:S(2)}, u32[]{:S(2)}) collective-permute-start(bf16[256,256]{1,0:T(8,128)(2,1)S(1)} %collective-permute-done.33.refs_5_), channel_id=1, source_target_pairs={{0,56},{8,0},{16,8},{24,16},{32,24},{40,32},{48,40},{56,48},{1,57}... | collective-permute-start | bytes 393224 | tf_op jit(solution)/shard_map/gather_preconditioned/ppermute | solution.py:202
  78.9 1.1 %collective-permute-start.28 = (bf16[256,256]{1,0:T(8,128)(2,1)S(1)}, bf16[256,256]{1,0:T(8,128)(2,1)S(1)}, u32[]{:S(2)}, u32[]{:S(2)}) collective-permute-start(bf16[256,256]{1,0:T(8,128)(2,1)S(1)} %collective-permute-done.27.refs_12_), channel_id=1, source_target_pairs={{0,56},{8,0},{16,8},{24,16},{32,24},{40,32},{48,40},{56,48},{1,57}... | collective-permute-start | bytes 393224 | tf_op jit(solution)/shard_map/gather_preconditioned/ppermute | solution.py:202
  80.1 2.1 %collective-permute-done.20.refs_6_ = bf16[256,256]{1,0:T(8,128)(2,1)S(1)} collective-permute-done((bf16[256,256]{1,0:T(8,128)(2,1)S(1)}, bf16[256,256]{1,0:T(8,128)(2,1)S(1)}, u32[]{:S(2)}, u32[]{:S(2)}) %collective-permute-start.20) | collective-permute-done | bytes 131104 | tf_op jit(solution)/shard_map/gather_preconditioned/ppermute | solution.py:202
  82.1 0.2 collective-permute-start.21
  82.3 2.3 %collective-permute-done.28.refs_3_ = bf16[256,256]{1,0:T(8,128)(2,1)S(1)} collective-permute-done((bf16[256,256]{1,0:T(8,128)(2,1)S(1)}, bf16[256,256]{1,0:T(8,128)(2,1)S(1)}, u32[]{:S(2)}, u32[]{:S(2)}) %collective-permute-start.28) | collective-permute-done | bytes 131104 | tf_op jit(solution)/shard_map/gather_preconditioned/ppermute | solution.py:202
  84.6 3.4 %collective-permute-start.29 = (bf16[256,256]{1,0:T(8,128)(2,1)S(1)}, bf16[256,256]{1,0:T(8,128)(2,1)S(1)}, u32[]{:S(2)}, u32[]{:S(2)}) collective-permute-start(bf16[256,256]{1,0:T(8,128)(2,1)S(1)} %collective-permute-done.28.refs_3_), channel_id=1, source_target_pairs={{0,56},{8,0},{16,8},{24,16},{32,24},{40,32},{48,40},{56,48},{1,57}... | collective-permute-start | bytes 393224 | tf_op jit(solution)/shard_map/gather_preconditioned/ppermute | solution.py:202
  88.0 2.5 %score.2.refs_9_ = f32[256,1024]{1,0:T(8,128)S(1)} custom-call(s32[50]{0:T(128)S(1)} %concatenate.3.where_ref.refs_0_, bf16[256,256]{1,0:T(8,128)(2,1)S(1)} %precondition.1.refs_1_, bf16[256,256]{1,0:T(8,128)(2,1)S(1)} %collective-permute-done.18.refs_2_, bf16[256,256]{1,0:T(8,128)(2,1)S(1)} %collective-permute-done.32.refs_3_, ...), custom_call_target="tpu_custom_call" | custom-call | flops 1610612736 | bytes 7864320 | tf_op jit(solution)/shard_map/score/score/pallas_call | solution.py:144
  90.6 1.5 %score.3 = (f32[64,1024]{1,0:T(8,128)S(1)}, bf16[64,1024]{1,0:T(8,128)(2,1)S(1)}, bf16[64,1024]{1,0:T(8,128)(2,1)S(1)}, bf16[64,1024]{1,0:T(8,128)(2,1)S(1)}) custom-call(s32[50]{0:T(128)S(1)} %concatenate.3.where_ref.refs_0_, bf16[256,256]{1,0:T(8,128)(2,1)S(1)} %collective-permute-done.21.refs_1_, bf16[256,256]{1,0:T(8,128)(2,1)S(1)} %collective-permute-done.25.refs_2_, ...), custom_call_target="tpu_custom_call" | custom-call | flops 536870912 | bytes 2621440 | tf_op jit(solution)/shard_map/score/score/pallas_call | solution.py:144
  92.1 1.3 %collective-permute-start.36 = (bf16[64,1024]{1,0:T(8,128)(2,1)S(1)}, bf16[64,1024]{1,0:T(8,128)(2,1)S(1)}, u32[]{:S(2)}, u32[]{:S(2)}) collective-permute-start(bf16[64,1024]{1,0:T(8,128)(2,1)S(1)} %get-tuple-element.28), channel_id=1, source_target_pairs={{0,64},{64,128},{128,192},{192,0},{1,65},{65,129},{129,193},{193,1... | collective-permute-start | bytes 393224 | tf_op jit(solution)/shard_map/sum_layers/ppermute | solution.py:202
  93.4 2.4 %collective-permute-start.37 = (bf16[64,1024]{1,0:T(8,128)(2,1)S(1)}, bf16[64,1024]{1,0:T(8,128)(2,1)S(1)}, u32[]{:S(2)}, u32[]{:S(2)}) collective-permute-start(bf16[64,1024]{1,0:T(8,128)(2,1)S(1)} %get-tuple-element.29), channel_id=1, source_target_pairs={{0,128},{64,192},{128,0},{192,64},{1,129},{65,193},{129,1},{193,65... | collective-permute-start | bytes 393224 | tf_op jit(solution)/shard_map/sum_layers/ppermute | solution.py:202
  95.9 1.2 %collective-permute-start.38 = (bf16[64,1024]{1,0:T(8,128)(2,1)S(1)}, bf16[64,1024]{1,0:T(8,128)(2,1)S(1)}, u32[]{:S(2)}, u32[]{:S(2)}) collective-permute-start(bf16[64,1024]{1,0:T(8,128)(2,1)S(1)} %get-tuple-element.30), channel_id=1, source_target_pairs={{0,192},{64,0},{128,64},{192,128},{1,193},{65,1},{129,65},{193,129... | collective-permute-start | bytes 393224 | tf_op jit(solution)/shard_map/sum_layers/ppermute | solution.py:202
  97.0 0.2 collective-permute-done.36.a_ref
  97.2 3.2 %collective-permute-done.37.b_ref = bf16[64,1024]{1,0:T(8,128)(2,1)S(1)} collective-permute-done((bf16[64,1024]{1,0:T(8,128)(2,1)S(1)}, bf16[64,1024]{1,0:T(8,128)(2,1)S(1)}, u32[]{:S(2)}, u32[]{:S(2)}) %collective-permute-start.37) | collective-permute-done | bytes 131104 | tf_op jit(solution)/shard_map/sum_layers/ppermute | solution.py:202
  100.4 0.4 collective-permute-done.38.c_ref
  100.9 2.4 %collective-permute-start.39 = (bf16[64,256]{1,0:T(8,128)(2,1)S(1)}, bf16[64,256]{1,0:T(8,128)(2,1)S(1)}, u32[]{:S(2)}, u32[]{:S(2)}) collective-permute-start(bf16[64,256]{1,0:T(8,128)(2,1)S(1)} %get-tuple-element.32), channel_id=1, source_target_pairs={{0,1},{1,0},{2,3},{3,2},{4,5},{5,4},{6,7},{7,6},{8,9},{9,8},{10,11... | collective-permute-start | bytes 98312 | tf_op jit(solution)/shard_map/exchange_examples/ppermute | solution.py:281
  103.3 2.7 %collective-permute-start.40 = (bf16[64,256]{1,0:T(8,128)(2,1)S(1)}, bf16[64,256]{1,0:T(8,128)(2,1)S(1)}, u32[]{:S(2)}, u32[]{:S(2)}) collective-permute-start(bf16[64,256]{1,0:T(8,128)(2,1)S(1)} %get-tuple-element.33), channel_id=1, source_target_pairs={{0,6},{1,7},{2,4},{3,5},{4,2},{5,3},{6,0},{7,1},{8,14},{9,15},{10,... | collective-permute-start | bytes 98312 | tf_op jit(solution)/shard_map/exchange_examples/ppermute | solution.py:281
  106.0 0.3 collective-permute-start.41
  106.3 1.0 collective-permute-done.40.refs_2_
  107.3 3.3 %collective-permute-done.41.refs_3_ = bf16[64,256]{1,0:T(8,128)(2,1)S(1)} collective-permute-done((bf16[64,256]{1,0:T(8,128)(2,1)S(1)}, bf16[64,256]{1,0:T(8,128)(2,1)S(1)}, u32[]{:S(2)}, u32[]{:S(2)}) %collective-permute-start.41) | collective-permute-done | bytes 32800 | tf_op jit(solution)/shard_map/exchange_examples/ppermute | solution.py:281
  110.6 1.3 %place_parts.1 = f32[256,256]{1,0:T(8,128)} custom-call(s32[50]{0:T(128)S(1)} %concatenate.3.where_ref.refs_0_, f32[64,256]{1,0:T(8,128)S(1)} %get-tuple-element.31.refs_0_, bf16[64,256]{1,0:T(8,128)(2,1)S(1)} %collective-permute-done.39.refs_1_, bf16[64,256]{1,0:T(8,128)(2,1)S(1)} %collective-permute-done.40.refs_2_, ...), custom_call_target="tpu_custom_call" | custom-call | flops 65536 | bytes 524288 | tf_op jit(solution)/shard_map/exchange_examples/place_parts/pallas_call | solution.py:190
  (47 shorter events, 0.7 us)
Async XLA Ops:
  0.0 18.1 %copy-start = (bf16[1,256,4096]{2,1,0:T(8,128)(2,1)S(1)}, bf16[1,256,4096]{2,1,0:T(8,128)(2,1)}, u32[]{:S(2)}) copy-start(bf16[1,256,4096]{2,1,0:T(8,128)(2,1)} %param.8) | copy-start | bytes 6291460
  0.0 33.8 %collective-permute-start.16 = (f32[64,4096]{1,0:T(8,128)}, f32[64,4096]{1,0:T(8,128)S(1)}, u32[]{:S(2)}, u32[]{:S(2)}) collective-permute-start(f32[64,4096]{1,0:T(8,128)} %bitcast.12), channel_id=1, source_target_pairs={{0,6},{6,0},{2,4},{4,2},{1,7},{7,1},{3,5},{5,3},{8,14},{14,8},{10,... | collective-permute-start | bytes 3145736 | tf_op jit(solution)/shard_map/swap_inverse/ppermute | solution.py:245
  4.8 1.6 %copy-start.1 = (bf16[1,16,512,128]{3,2,1,0:T(8,128)(2,1)S(1)}, bf16[1,16,512,128]{3,2,1,0:T(8,128)(2,1)}, u32[]{:S(2)}) copy-start(bf16[1,16,512,128]{3,2,1,0:T(8,128)(2,1)} %param.5) | copy-start | bytes 6291460
  6.4 0.7 copy-start.3
  9.5 5.8 %collective-permute-start.7 = (bf16[16,4096]{1,0:T(8,128)(2,1)S(1)}, bf16[16,4096]{1,0:T(8,128)(2,1)S(1)}, u32[]{:S(2)}, u32[]{:S(2)}) collective-permute-start(bf16[16,4096]{1,0:T(8,128)(2,1)S(1)} %reshape.12.refs_1_), channel_id=1, source_target_pairs={{0,2},{2,0},{4,6},{6,4},{1,3},{3,1},{5,7},{7,5},{8,10},{10,8},{12,... | collective-permute-start | bytes 393224 | tf_op jit(solution)/shard_map/gather_projected/ppermute | solution.py:245
  9.6 8.5 %collective-permute-start = (bf16[16,4096]{1,0:T(8,128)(2,1)S(1)}, bf16[16,4096]{1,0:T(8,128)(2,1)S(1)}, u32[]{:S(2)}, u32[]{:S(2)}) collective-permute-start(bf16[16,4096]{1,0:T(8,128)(2,1)S(1)} %reshape.12.refs_1_), channel_id=1, source_target_pairs={{0,8},{8,16},{16,24},{24,32},{32,40},{40,48},{48,56},{56,0},{1,9},... | collective-permute-start | bytes 393224 | tf_op jit(solution)/shard_map/gather_projected/ppermute | solution.py:202
  11.3 6.8 %collective-permute-start.1 = (bf16[16,4096]{1,0:T(8,128)(2,1)S(1)}, bf16[16,4096]{1,0:T(8,128)(2,1)S(1)}, u32[]{:S(2)}, u32[]{:S(2)}) collective-permute-start(bf16[16,4096]{1,0:T(8,128)(2,1)S(1)} %reshape.12.refs_1_), channel_id=1, source_target_pairs={{0,56},{8,0},{16,8},{24,16},{32,24},{40,32},{48,40},{56,48},{1,57}... | collective-permute-start | bytes 393224 | tf_op jit(solution)/shard_map/gather_projected/ppermute | solution.py:202
  18.1 52.5 %collective-permute-start.31 = (bf16[256,4096]{1,0:T(8,128)(2,1)S(1)}, bf16[256,4096]{1,0:T(8,128)(2,1)S(1)}, u32[]{:S(2)}, u32[]{:S(2)}) collective-permute-start(bf16[256,4096]{1,0:T(8,128)(2,1)S(1)} %bitcast.7), channel_id=1, source_target_pairs={{0,6},{6,0},{2,4},{4,2},{1,7},{7,1},{3,5},{5,3},{8,14},{14,8},{10,... | collective-permute-start | bytes 6291464 | tf_op jit(solution)/shard_map/swap_stored/ppermute | solution.py:245
  18.6 5.3 %collective-permute-start.8 = (bf16[16,4096]{1,0:T(8,128)(2,1)S(1)}, bf16[16,4096]{1,0:T(8,128)(2,1)S(1)}, u32[]{:S(2)}, u32[]{:S(2)}) collective-permute-start(bf16[16,4096]{1,0:T(8,128)(2,1)S(1)} %collective-permute-done.7.refs_9_), channel_id=1, source_target_pairs={{0,8},{8,16},{16,24},{24,32},{32,40},{40,48},{48,56},{56,0},{1,9},... | collective-permute-start | bytes 393224 | tf_op jit(solution)/shard_map/gather_projected/ppermute | solution.py:202
  18.6 6.8 %collective-permute-start.9 = (bf16[16,4096]{1,0:T(8,128)(2,1)S(1)}, bf16[16,4096]{1,0:T(8,128)(2,1)S(1)}, u32[]{:S(2)}, u32[]{:S(2)}) collective-permute-start(bf16[16,4096]{1,0:T(8,128)(2,1)S(1)} %collective-permute-done.7.refs_9_), channel_id=1, source_target_pairs={{0,56},{8,0},{16,8},{24,16},{32,24},{40,32},{48,40},{56,48},{1,57}... | collective-permute-start | bytes 393224 | tf_op jit(solution)/shard_map/gather_projected/ppermute | solution.py:202
  21.2 6.7 %collective-permute-start.2 = (bf16[16,4096]{1,0:T(8,128)(2,1)S(1)}, bf16[16,4096]{1,0:T(8,128)(2,1)S(1)}, u32[]{:S(2)}, u32[]{:S(2)}) collective-permute-start(bf16[16,4096]{1,0:T(8,128)(2,1)S(1)} %collective-permute-done.refs_2_), channel_id=1, source_target_pairs={{0,8},{8,16},{16,24},{24,32},{32,40},{40,48},{48,56},{56,0},{1,9},... | collective-permute-start | bytes 393224 | tf_op jit(solution)/shard_map/gather_projected/ppermute | solution.py:202
  23.9 4.2 %collective-permute-start.3 = (bf16[16,4096]{1,0:T(8,128)(2,1)S(1)}, bf16[16,4096]{1,0:T(8,128)(2,1)S(1)}, u32[]{:S(2)}, u32[]{:S(2)}) collective-permute-start(bf16[16,4096]{1,0:T(8,128)(2,1)S(1)} %collective-permute-done.1.refs_3_), channel_id=1, source_target_pairs={{0,56},{8,0},{16,8},{24,16},{32,24},{40,32},{48,40},{56,48},{1,57}... | collective-permute-start | bytes 393224 | tf_op jit(solution)/shard_map/gather_projected/ppermute | solution.py:202
  25.3 8.5 %collective-permute-start.10 = (bf16[16,4096]{1,0:T(8,128)(2,1)S(1)}, bf16[16,4096]{1,0:T(8,128)(2,1)S(1)}, u32[]{:S(2)}, u32[]{:S(2)}) collective-permute-start(bf16[16,4096]{1,0:T(8,128)(2,1)S(1)} %collective-permute-done.8.refs_10_), channel_id=1, source_target_pairs={{0,8},{8,16},{16,24},{24,32},{32,40},{40,48},{48,56},{56,0},{1,9},... | collective-permute-start | bytes 393224 | tf_op jit(solution)/shard_map/gather_projected/ppermute | solution.py:202
  27.9 5.9 %collective-permute-start.11 = (bf16[16,4096]{1,0:T(8,128)(2,1)S(1)}, bf16[16,4096]{1,0:T(8,128)(2,1)S(1)}, u32[]{:S(2)}, u32[]{:S(2)}) collective-permute-start(bf16[16,4096]{1,0:T(8,128)(2,1)S(1)} %collective-permute-done.9.refs_11_), channel_id=1, source_target_pairs={{0,56},{8,0},{16,8},{24,16},{32,24},{40,32},{48,40},{56,48},{1,57}... | collective-permute-start | bytes 393224 | tf_op jit(solution)/shard_map/gather_projected/ppermute | solution.py:202
  28.0 16.2 %collective-permute-start.15 = (f32[64,4096]{1,0:T(8,128)}, f32[64,4096]{1,0:T(8,128)S(1)}, u32[]{:S(2)}, u32[]{:S(2)}) collective-permute-start(f32[64,4096]{1,0:T(8,128)} %bitcast.13), channel_id=1, source_target_pairs={{0,1},{1,0},{2,3},{3,2},{4,5},{5,4},{6,7},{7,6},{8,9},{9,8},{10,11... | collective-permute-start | bytes 3145736 | tf_op jit(solution)/shard_map/swap_inverse/ppermute | solution.py:210
  33.8 11.6 %collective-permute-start.17 = (f32[64,4096]{1,0:T(8,128)S(1)}, f32[64,4096]{1,0:T(8,128)S(1)}, u32[]{:S(2)}, u32[]{:S(2)}) collective-permute-start(f32[64,4096]{1,0:T(8,128)S(1)} %collective-permute-done.16.chip_ref), channel_id=1, source_target_pairs={{0,1},{1,0},{2,3},{3,2},{4,5},{5,4},{6,7},{7,6},{8,9},{9,8},{10,11... | collective-permute-start | bytes 3145736 | tf_op jit(solution)/shard_map/swap_inverse/ppermute | solution.py:210
  35.6 6.3 %collective-permute-start.4 = (bf16[16,4096]{1,0:T(8,128)(2,1)S(1)}, bf16[16,4096]{1,0:T(8,128)(2,1)S(1)}, u32[]{:S(2)}, u32[]{:S(2)}) collective-permute-start(bf16[16,4096]{1,0:T(8,128)(2,1)S(1)} %collective-permute-done.2.refs_4_), channel_id=1, source_target_pairs={{0,8},{8,16},{16,24},{24,32},{32,40},{40,48},{48,56},{56,0},{1,9},... | collective-permute-start | bytes 393224 | tf_op jit(solution)/shard_map/gather_projected/ppermute | solution.py:202
  37.3 5.9 %collective-permute-start.13 = (bf16[16,4096]{1,0:T(8,128)(2,1)S(1)}, bf16[16,4096]{1,0:T(8,128)(2,1)S(1)}, u32[]{:S(2)}, u32[]{:S(2)}) collective-permute-start(bf16[16,4096]{1,0:T(8,128)(2,1)S(1)} %collective-permute-done.11.refs_13_), channel_id=1, source_target_pairs={{0,56},{8,0},{16,8},{24,16},{32,24},{40,32},{48,40},{56,48},{1,57}... | collective-permute-start | bytes 393224 | tf_op jit(solution)/shard_map/gather_projected/ppermute | solution.py:202
  41.9 7.4 %collective-permute-start.5 = (bf16[16,4096]{1,0:T(8,128)(2,1)S(1)}, bf16[16,4096]{1,0:T(8,128)(2,1)S(1)}, u32[]{:S(2)}, u32[]{:S(2)}) collective-permute-start(bf16[16,4096]{1,0:T(8,128)(2,1)S(1)} %collective-permute-done.3.refs_5_), channel_id=1, source_target_pairs={{0,56},{8,0},{16,8},{24,16},{32,24},{40,32},{48,40},{56,48},{1,57}... | collective-permute-start | bytes 393224 | tf_op jit(solution)/shard_map/gather_projected/ppermute | solution.py:202
  43.2 6.2 %collective-permute-start.12 = (bf16[16,4096]{1,0:T(8,128)(2,1)S(1)}, bf16[16,4096]{1,0:T(8,128)(2,1)S(1)}, u32[]{:S(2)}, u32[]{:S(2)}) collective-permute-start(bf16[16,4096]{1,0:T(8,128)(2,1)S(1)} %collective-permute-done.10.refs_12_), channel_id=1, source_target_pairs={{0,8},{8,16},{16,24},{24,32},{32,40},{40,48},{48,56},{56,0},{1,9},... | collective-permute-start | bytes 393224 | tf_op jit(solution)/shard_map/gather_projected/ppermute | solution.py:202
  44.2 6.9 %collective-permute-start.6 = (bf16[16,4096]{1,0:T(8,128)(2,1)S(1)}, bf16[16,4096]{1,0:T(8,128)(2,1)S(1)}, u32[]{:S(2)}, u32[]{:S(2)}) collective-permute-start(bf16[16,4096]{1,0:T(8,128)(2,1)S(1)} %collective-permute-done.4.refs_6_), channel_id=1, source_target_pairs={{0,8},{8,16},{16,24},{24,32},{32,40},{40,48},{48,56},{56,0},{1,9},... | collective-permute-start | bytes 393224 | tf_op jit(solution)/shard_map/gather_projected/ppermute | solution.py:202
  45.4 5.8 %collective-permute-start.14 = (bf16[16,4096]{1,0:T(8,128)(2,1)S(1)}, bf16[16,4096]{1,0:T(8,128)(2,1)S(1)}, u32[]{:S(2)}, u32[]{:S(2)}) collective-permute-start(bf16[16,4096]{1,0:T(8,128)(2,1)S(1)} %collective-permute-done.13.refs_15_), channel_id=1, source_target_pairs={{0,56},{8,0},{16,8},{24,16},{32,24},{40,32},{48,40},{56,48},{1,57}... | collective-permute-start | bytes 393224 | tf_op jit(solution)/shard_map/gather_projected/ppermute | solution.py:202
  46.9 1.2 %copy-start.2 = (f32[1,64,4096]{2,1,0:T(8,128)S(1)}, f32[1,64,4096]{2,1,0:T(8,128)}, u32[]{:S(2)}) copy-start(f32[1,64,4096]{2,1,0:T(8,128)} %param.7) | copy-start | bytes 3145732
  53.0 4.2 %collective-permute-start.22 = (bf16[256,256]{1,0:T(8,128)(2,1)S(1)}, bf16[256,256]{1,0:T(8,128)(2,1)S(1)}, u32[]{:S(2)}, u32[]{:S(2)}) collective-permute-start(bf16[256,256]{1,0:T(8,128)(2,1)S(1)} %precondition.1.refs_1_), channel_id=1, source_target_pairs={{0,2},{2,0},{4,6},{6,4},{1,3},{3,1},{5,7},{7,5},{8,10},{10,8},{12,... | collective-permute-start | bytes 393224 | tf_op jit(solution)/shard_map/gather_preconditioned/ppermute | solution.py:245
  53.5 6.4 %collective-permute-start.18 = (bf16[256,256]{1,0:T(8,128)(2,1)S(1)}, bf16[256,256]{1,0:T(8,128)(2,1)S(1)}, u32[]{:S(2)}, u32[]{:S(2)}) collective-permute-start(bf16[256,256]{1,0:T(8,128)(2,1)S(1)} %precondition.1.refs_1_), channel_id=1, source_target_pairs={{0,8},{8,16},{16,24},{24,32},{32,40},{40,48},{48,56},{56,0},{1,9},... | collective-permute-start | bytes 393224 | tf_op jit(solution)/shard_map/gather_preconditioned/ppermute | solution.py:202
  53.7 6.2 %collective-permute-start.32 = (bf16[256,256]{1,0:T(8,128)(2,1)S(1)}, bf16[256,256]{1,0:T(8,128)(2,1)S(1)}, u32[]{:S(2)}, u32[]{:S(2)}) collective-permute-start(bf16[256,256]{1,0:T(8,128)(2,1)S(1)} %precondition.1.refs_1_), channel_id=1, source_target_pairs={{0,56},{8,0},{16,8},{24,16},{32,24},{40,32},{48,40},{56,48},{1,57}... | collective-permute-start | bytes 393224 | tf_op jit(solution)/shard_map/gather_preconditioned/ppermute | solution.py:202
  57.2 5.7 %collective-permute-start.23 = (bf16[256,256]{1,0:T(8,128)(2,1)S(1)}, bf16[256,256]{1,0:T(8,128)(2,1)S(1)}, u32[]{:S(2)}, u32[]{:S(2)}) collective-permute-start(bf16[256,256]{1,0:T(8,128)(2,1)S(1)} %collective-permute-done.22.refs_8_), channel_id=1, source_target_pairs={{0,8},{8,16},{16,24},{24,32},{32,40},{40,48},{48,56},{56,0},{1,9},... | collective-permute-start | bytes 393224 | tf_op jit(solution)/shard_map/gather_preconditioned/ppermute | solution.py:202
  57.3 5.6 %collective-permute-start.26 = (bf16[256,256]{1,0:T(8,128)(2,1)S(1)}, bf16[256,256]{1,0:T(8,128)(2,1)S(1)}, u32[]{:S(2)}, u32[]{:S(2)}) collective-permute-start(bf16[256,256]{1,0:T(8,128)(2,1)S(1)} %collective-permute-done.22.refs_8_), channel_id=1, source_target_pairs={{0,56},{8,0},{16,8},{24,16},{32,24},{40,32},{48,40},{56,48},{1,57}... | collective-permute-start | bytes 393224 | tf_op jit(solution)/shard_map/gather_preconditioned/ppermute | solution.py:202
  59.8 13.0 %collective-permute-start.19 = (bf16[256,256]{1,0:T(8,128)(2,1)S(1)}, bf16[256,256]{1,0:T(8,128)(2,1)S(1)}, u32[]{:S(2)}, u32[]{:S(2)}) collective-permute-start(bf16[256,256]{1,0:T(8,128)(2,1)S(1)} %collective-permute-done.18.refs_2_), channel_id=1, source_target_pairs={{0,8},{8,16},{16,24},{24,32},{32,40},{40,48},{48,56},{56,0},{1,9},... | collective-permute-start | bytes 393224 | tf_op jit(solution)/shard_map/gather_preconditioned/ppermute | solution.py:202
  59.9 13.0 %collective-permute-start.33 = (bf16[256,256]{1,0:T(8,128)(2,1)S(1)}, bf16[256,256]{1,0:T(8,128)(2,1)S(1)}, u32[]{:S(2)}, u32[]{:S(2)}) collective-permute-start(bf16[256,256]{1,0:T(8,128)(2,1)S(1)} %collective-permute-done.32.refs_3_), channel_id=1, source_target_pairs={{0,56},{8,0},{16,8},{24,16},{32,24},{40,32},{48,40},{56,48},{1,57}... | collective-permute-start | bytes 393224 | tf_op jit(solution)/shard_map/gather_preconditioned/ppermute | solution.py:202
  62.9 9.9 %collective-permute-start.24 = (bf16[256,256]{1,0:T(8,128)(2,1)S(1)}, bf16[256,256]{1,0:T(8,128)(2,1)S(1)}, u32[]{:S(2)}, u32[]{:S(2)}) collective-permute-start(bf16[256,256]{1,0:T(8,128)(2,1)S(1)} %collective-permute-done.23.refs_9_), channel_id=1, source_target_pairs={{0,8},{8,16},{16,24},{24,32},{32,40},{40,48},{48,56},{56,0},{1,9},... | collective-permute-start | bytes 393224 | tf_op jit(solution)/shard_map/gather_preconditioned/ppermute | solution.py:202
  62.9 9.9 %collective-permute-start.27 = (bf16[256,256]{1,0:T(8,128)(2,1)S(1)}, bf16[256,256]{1,0:T(8,128)(2,1)S(1)}, u32[]{:S(2)}, u32[]{:S(2)}) collective-permute-start(bf16[256,256]{1,0:T(8,128)(2,1)S(1)} %collective-permute-done.26.refs_10_), channel_id=1, source_target_pairs={{0,56},{8,0},{16,8},{24,16},{32,24},{40,32},{48,40},{56,48},{1,57}... | collective-permute-start | bytes 393224 | tf_op jit(solution)/shard_map/gather_preconditioned/ppermute | solution.py:202
  70.5 17.5 %collective-permute-start.30 = (bf16[256,4096]{1,0:T(8,128)(2,1)S(1)}, bf16[256,4096]{1,0:T(8,128)(2,1)S(1)}, u32[]{:S(2)}, u32[]{:S(2)}) collective-permute-start(bf16[256,4096]{1,0:T(8,128)(2,1)S(1)} %bitcast.8), channel_id=1, source_target_pairs={{0,1},{1,0},{2,3},{3,2},{4,5},{5,4},{6,7},{7,6},{8,9},{9,8},{10,11... | collective-permute-start | bytes 6291464 | tf_op jit(solution)/shard_map/swap_stored/ppermute | solution.py:210
  72.9 15.2 %collective-permute-start.34 = (bf16[256,4096]{1,0:T(8,128)(2,1)S(1)}, bf16[256,4096]{1,0:T(8,128)(2,1)S(1)}, u32[]{:S(2)}, u32[]{:S(2)}) collective-permute-start(bf16[256,4096]{1,0:T(8,128)(2,1)S(1)} %collective-permute-done.31.refs_15_.refs_7_), channel_id=1, source_target_pairs={{0,1},{1,0},{2,3},{3,2},{4,5},{5,4},{6,7},{7,6},{8,9},{9,8},{10,11... | collective-permute-start | bytes 6291464 | tf_op jit(solution)/shard_map/swap_stored/ppermute | solution.py:210
  73.2 9.0 %collective-permute-start.20 = (bf16[256,256]{1,0:T(8,128)(2,1)S(1)}, bf16[256,256]{1,0:T(8,128)(2,1)S(1)}, u32[]{:S(2)}, u32[]{:S(2)}) collective-permute-start(bf16[256,256]{1,0:T(8,128)(2,1)S(1)} %collective-permute-done.19.refs_4_), channel_id=1, source_target_pairs={{0,8},{8,16},{16,24},{24,32},{32,40},{40,48},{48,56},{56,0},{1,9},... | collective-permute-start | bytes 393224 | tf_op jit(solution)/shard_map/gather_preconditioned/ppermute | solution.py:202
  74.7 7.5 %collective-permute-start.35 = (bf16[256,256]{1,0:T(8,128)(2,1)S(1)}, bf16[256,256]{1,0:T(8,128)(2,1)S(1)}, u32[]{:S(2)}, u32[]{:S(2)}) collective-permute-start(bf16[256,256]{1,0:T(8,128)(2,1)S(1)} %collective-permute-done.33.refs_5_), channel_id=1, source_target_pairs={{0,56},{8,0},{16,8},{24,16},{32,24},{40,32},{48,40},{56,48},{1,57}... | collective-permute-start | bytes 393224 | tf_op jit(solution)/shard_map/gather_preconditioned/ppermute | solution.py:202
  78.9 5.6 %collective-permute-start.28 = (bf16[256,256]{1,0:T(8,128)(2,1)S(1)}, bf16[256,256]{1,0:T(8,128)(2,1)S(1)}, u32[]{:S(2)}, u32[]{:S(2)}) collective-permute-start(bf16[256,256]{1,0:T(8,128)(2,1)S(1)} %collective-permute-done.27.refs_12_), channel_id=1, source_target_pairs={{0,56},{8,0},{16,8},{24,16},{32,24},{40,32},{48,40},{56,48},{1,57}... | collective-permute-start | bytes 393224 | tf_op jit(solution)/shard_map/gather_preconditioned/ppermute | solution.py:202
  82.1 8.4 %collective-permute-start.25 = (bf16[256,256]{1,0:T(8,128)(2,1)S(1)}, bf16[256,256]{1,0:T(8,128)(2,1)S(1)}, u32[]{:S(2)}, u32[]{:S(2)}) collective-permute-start(bf16[256,256]{1,0:T(8,128)(2,1)S(1)} %collective-permute-done.24.refs_11_), channel_id=1, source_target_pairs={{0,8},{8,16},{16,24},{24,32},{32,40},{40,48},{48,56},{56,0},{1,9},... | collective-permute-start | bytes 393224 | tf_op jit(solution)/shard_map/gather_preconditioned/ppermute | solution.py:202
  82.1 8.4 %collective-permute-start.21 = (bf16[256,256]{1,0:T(8,128)(2,1)S(1)}, bf16[256,256]{1,0:T(8,128)(2,1)S(1)}, u32[]{:S(2)}, u32[]{:S(2)}) collective-permute-start(bf16[256,256]{1,0:T(8,128)(2,1)S(1)} %collective-permute-done.20.refs_6_), channel_id=1, source_target_pairs={{0,8},{8,16},{16,24},{24,32},{32,40},{40,48},{48,56},{56,0},{1,9},... | collective-permute-start | bytes 393224 | tf_op jit(solution)/shard_map/gather_preconditioned/ppermute | solution.py:202
  84.6 6.0 %collective-permute-start.29 = (bf16[256,256]{1,0:T(8,128)(2,1)S(1)}, bf16[256,256]{1,0:T(8,128)(2,1)S(1)}, u32[]{:S(2)}, u32[]{:S(2)}) collective-permute-start(bf16[256,256]{1,0:T(8,128)(2,1)S(1)} %collective-permute-done.28.refs_3_), channel_id=1, source_target_pairs={{0,56},{8,0},{16,8},{24,16},{32,24},{40,32},{48,40},{56,48},{1,57}... | collective-permute-start | bytes 393224 | tf_op jit(solution)/shard_map/gather_preconditioned/ppermute | solution.py:202
  92.1 5.1 %collective-permute-start.36 = (bf16[64,1024]{1,0:T(8,128)(2,1)S(1)}, bf16[64,1024]{1,0:T(8,128)(2,1)S(1)}, u32[]{:S(2)}, u32[]{:S(2)}) collective-permute-start(bf16[64,1024]{1,0:T(8,128)(2,1)S(1)} %get-tuple-element.28), channel_id=1, source_target_pairs={{0,64},{64,128},{128,192},{192,0},{1,65},{65,129},{129,193},{193,1... | collective-permute-start | bytes 393224 | tf_op jit(solution)/shard_map/sum_layers/ppermute | solution.py:202
  93.4 7.0 %collective-permute-start.37 = (bf16[64,1024]{1,0:T(8,128)(2,1)S(1)}, bf16[64,1024]{1,0:T(8,128)(2,1)S(1)}, u32[]{:S(2)}, u32[]{:S(2)}) collective-permute-start(bf16[64,1024]{1,0:T(8,128)(2,1)S(1)} %get-tuple-element.29), channel_id=1, source_target_pairs={{0,128},{64,192},{128,0},{192,64},{1,129},{65,193},{129,1},{193,65... | collective-permute-start | bytes 393224 | tf_op jit(solution)/shard_map/sum_layers/ppermute | solution.py:202
  95.9 5.0 %collective-permute-start.38 = (bf16[64,1024]{1,0:T(8,128)(2,1)S(1)}, bf16[64,1024]{1,0:T(8,128)(2,1)S(1)}, u32[]{:S(2)}, u32[]{:S(2)}) collective-permute-start(bf16[64,1024]{1,0:T(8,128)(2,1)S(1)} %get-tuple-element.30), channel_id=1, source_target_pairs={{0,192},{64,0},{128,64},{192,128},{1,193},{65,1},{129,65},{193,129... | collective-permute-start | bytes 393224 | tf_op jit(solution)/shard_map/sum_layers/ppermute | solution.py:202
  100.9 5.4 %collective-permute-start.39 = (bf16[64,256]{1,0:T(8,128)(2,1)S(1)}, bf16[64,256]{1,0:T(8,128)(2,1)S(1)}, u32[]{:S(2)}, u32[]{:S(2)}) collective-permute-start(bf16[64,256]{1,0:T(8,128)(2,1)S(1)} %get-tuple-element.32), channel_id=1, source_target_pairs={{0,1},{1,0},{2,3},{3,2},{4,5},{5,4},{6,7},{7,6},{8,9},{9,8},{10,11... | collective-permute-start | bytes 98312 | tf_op jit(solution)/shard_map/exchange_examples/ppermute | solution.py:281
  103.3 4.0 %collective-permute-start.40 = (bf16[64,256]{1,0:T(8,128)(2,1)S(1)}, bf16[64,256]{1,0:T(8,128)(2,1)S(1)}, u32[]{:S(2)}, u32[]{:S(2)}) collective-permute-start(bf16[64,256]{1,0:T(8,128)(2,1)S(1)} %get-tuple-element.33), channel_id=1, source_target_pairs={{0,6},{1,7},{2,4},{3,5},{4,2},{5,3},{6,0},{7,1},{8,14},{9,15},{10,... | collective-permute-start | bytes 98312 | tf_op jit(solution)/shard_map/exchange_examples/ppermute | solution.py:281
  106.0 4.6 %collective-permute-start.41 = (bf16[64,256]{1,0:T(8,128)(2,1)S(1)}, bf16[64,256]{1,0:T(8,128)(2,1)S(1)}, u32[]{:S(2)}, u32[]{:S(2)}) collective-permute-start(bf16[64,256]{1,0:T(8,128)(2,1)S(1)} %get-tuple-element.34), channel_id=1, source_target_pairs={{0,7},{1,6},{2,5},{3,4},{4,3},{5,2},{6,1},{7,0},{8,15},{9,14},{10,... | collective-permute-start | bytes 98312 | tf_op jit(solution)/shard_map/exchange_examples/ppermute | solution.py:281

commit v3 on v2

--- a/solution.py
+++ b/solution.py
@@ -262,7 +262,7 @@
         pieces = gather(own, swap_chip(own, (0, 1), (2, 3)))
     with jax.named_scope("swap_stored"):
         core_stored = swap_core(after(stored_rows, own))
-        both_stored = swap_core(after(chip_stored, some(pieces, (2, 0), (-2, 0), (2, 1), (-2, 1))))
+        both_stored = swap_core(after(chip_stored, some(pieces, (3, 0), (-3, 0), (3, 1), (-3, 1))))
     with jax.named_scope("score"):
         late = [k for k, (dz, side, _) in enumerate(pieces) if abs(dz) == 4 or (side and abs(dz) == 3)]
         soon = [k for k in range(len(pieces)) if k not in late]

time: 112 us -> 107 us (0.955)
  waiting for transfers between devices: 31.3 us -> 24.6 us
  starting transfers between devices: 64.8 us -> 67.1 us
    ppermute x4, starting transfers between devices: 10.1 us -> 15.3 us  [swap_core(): return lax.ppermute(value, 'core', [(0, 1), (1, 0)])]
    ppermute x4, waiting for transfers between devices: 5.72 us -> 1.1 us  [swap_chip(): lax.ppermute(value, 'y', [pair for a, b in pairs for pair in ((a, b), (b,...]
    ppermute x31, waiting for transfers between devices: 21.3 us -> 18.7 us  [shift(): lax.ppermute(value, axis, [(i, (i + by) % size) for i in range(size)])]
    ppermute x31, starting transfers between devices: 44.8 us -> 42.5 us  [shift(): lax.ppermute(value, axis, [(i, (i + by) % size) for i in range(size)])]
where the time goes in v3:
time: 107 us
  starting transfers between devices  67.1 us (63%)
  waiting for transfers between devices  24.6 us (23%)
  Pallas kernels  10.5 us (10%)
  local copies, waits for them, and re-layouts  4.16 us (4%)
    ppermute x31, starting transfers between devices, shift(): lax.ppermute(value, axis, [(i, (i + by) % size) for i in range(size)])  42.5 us
    ppermute x31, waiting for transfers between devices, shift(): lax.ppermute(value, axis, [(i, (i + by) % size) for i in range(size)])  18.7 us
    ppermute x4, starting transfers between devices, swap_core(): return lax.ppermute(value, 'core', [(0, 1), (1, 0)])  15.3 us
    ppermute x4, starting transfers between devices, swap_chip(): lax.ppermute(value, 'y', [pair for a, b in pairs for pair in ((a, b), (b,...  4.79 us
    ppermute x3, starting transfers between devices, per_device(): lax.ppermute(parts[k], ('y', 'core'), pairs[k - 1])  4.47 us
    pallas_call x2, Pallas kernels, score(): pl.pallas_call(lambda *refs: score_kernel(some, len(stored), before is No...  4.04 us
    ppermute x3, waiting for transfers between devices, per_device(): lax.ppermute(parts[k], ('y', 'core'), pairs[k - 1])  3.85 us
    unnamed x8, local copies, waits for them, and re-layouts  3.47 us
  transfers between devices with their start and end apart: 42, of which 15 were waited for; matrix products, arithmetic and copies ran while one was open for 1% of the time, Pallas kernels for 7%

profile of v3, /device:TPU:1, one launch (start us, length us, event | category | flops | bytes accessed | tf_op | source)
XLA Modules:
  0.0 107.3 jit_solution(8134429814680249066)
XLA Ops:
  0.0 3.6 %collective-permute-start.16 = (f32[64,4096]{1,0:T(8,128)}, f32[64,4096]{1,0:T(8,128)S(1)}, u32[]{:S(2)}, u32[]{:S(2)}) collective-permute-start(f32[64,4096]{1,0:T(8,128)} %bitcast.12), channel_id=1, source_target_pairs={{0,6},{6,0},{2,4},{4,2},{1,7},{7,1},{3,5},{5,3},{8,14},{14,8},{10,... | collective-permute-start | bytes 3145736 | tf_op jit(solution)/shard_map/swap_inverse/ppermute | solution.py:245
  3.7 0.1 xor.12
  3.8 0.7 broadcast_multiply_fusion
  4.5 0.1 mul.18
  4.6 0.1 add.39
  4.7 0.1 concatenate.3.where_ref.refs_0_
  4.8 1.6 %copy-done.1 = bf16[1,16,512,128]{3,2,1,0:T(8,128)(2,1)S(1)} copy-done((bf16[1,16,512,128]{3,2,1,0:T(8,128)(2,1)S(1)}, bf16[1,16,512,128]{3,2,1,0:T(8,128)(2,1)}, u32[]{:S(2)}) %copy-start.1) | copy-done | bytes 2097176
  6.4 0.7 copy-done.3
  7.1 2.1 %form_gradients.1 = bf16[16,64,64]{2,1,0:T(8,128)(2,1)S(1)} custom-call(s32[16]{0:T(128)S(1)} %copy-done.3, bf16[16,512,128]{2,1,0:T(8,128)(2,1)S(1)} %bitcast.11), custom_call_target="tpu_custom_call" | custom-call | flops 268435456 | bytes 2097152 | tf_op jit(solution)/shard_map/gradients/form_gradients/pallas_call | solution.py:41
  9.2 0.3 reshape.12.refs_1_
  9.5 0.1 collective-permute-start.7
  9.6 1.7 %collective-permute-start = (bf16[16,4096]{1,0:T(8,128)(2,1)S(1)}, bf16[16,4096]{1,0:T(8,128)(2,1)S(1)}, u32[]{:S(2)}, u32[]{:S(2)}) collective-permute-start(bf16[16,4096]{1,0:T(8,128)(2,1)S(1)} %reshape.12.refs_1_), channel_id=1, source_target_pairs={{0,8},{8,16},{16,24},{24,32},{32,40},{40,48},{48,56},{56,0},{1,9},... | collective-permute-start | bytes 393224 | tf_op jit(solution)/shard_map/gather_projected/ppermute | solution.py:202
  11.3 4.0 %collective-permute-start.1 = (bf16[16,4096]{1,0:T(8,128)(2,1)S(1)}, bf16[16,4096]{1,0:T(8,128)(2,1)S(1)}, u32[]{:S(2)}, u32[]{:S(2)}) collective-permute-start(bf16[16,4096]{1,0:T(8,128)(2,1)S(1)} %reshape.12.refs_1_), channel_id=1, source_target_pairs={{0,56},{8,0},{16,8},{24,16},{32,24},{40,32},{48,40},{56,48},{1,57}... | collective-permute-start | bytes 393224 | tf_op jit(solution)/shard_map/gather_projected/ppermute | solution.py:202
  15.3 2.8 %collective-permute-done.refs_2_ = bf16[16,4096]{1,0:T(8,128)(2,1)S(1)} collective-permute-done((bf16[16,4096]{1,0:T(8,128)(2,1)S(1)}, bf16[16,4096]{1,0:T(8,128)(2,1)S(1)}, u32[]{:S(2)}, u32[]{:S(2)}) %collective-permute-start) | collective-permute-done | bytes 131104 | tf_op jit(solution)/shard_map/gather_projected/ppermute | solution.py:202
  18.1 0.7 collective-permute-start.31
  18.8 2.7 %collective-permute-start.9 = (bf16[16,4096]{1,0:T(8,128)(2,1)S(1)}, bf16[16,4096]{1,0:T(8,128)(2,1)S(1)}, u32[]{:S(2)}, u32[]{:S(2)}) collective-permute-start(bf16[16,4096]{1,0:T(8,128)(2,1)S(1)} %collective-permute-done.7.refs_9_), channel_id=1, source_target_pairs={{0,56},{8,0},{16,8},{24,16},{32,24},{40,32},{48,40},{56,48},{1,57}... | collective-permute-start | bytes 393224 | tf_op jit(solution)/shard_map/gather_projected/ppermute | solution.py:202
  21.5 2.6 %collective-permute-done.8.refs_10_ = bf16[16,4096]{1,0:T(8,128)(2,1)S(1)} collective-permute-done((bf16[16,4096]{1,0:T(8,128)(2,1)S(1)}, bf16[16,4096]{1,0:T(8,128)(2,1)S(1)}, u32[]{:S(2)}, u32[]{:S(2)}) %collective-permute-start.8) | collective-permute-done | bytes 131104 | tf_op jit(solution)/shard_map/gather_projected/ppermute | solution.py:202
  24.1 1.3 %collective-permute-start.3 = (bf16[16,4096]{1,0:T(8,128)(2,1)S(1)}, bf16[16,4096]{1,0:T(8,128)(2,1)S(1)}, u32[]{:S(2)}, u32[]{:S(2)}) collective-permute-start(bf16[16,4096]{1,0:T(8,128)(2,1)S(1)} %collective-permute-done.1.refs_3_), channel_id=1, source_target_pairs={{0,56},{8,0},{16,8},{24,16},{32,24},{40,32},{48,40},{56,48},{1,57}... | collective-permute-start | bytes 393224 | tf_op jit(solution)/shard_map/gather_projected/ppermute | solution.py:202
  25.4 0.7 collective-permute-start.10
  26.1 1.8 %collective-permute-done.2.refs_4_ = bf16[16,4096]{1,0:T(8,128)(2,1)S(1)} collective-permute-done((bf16[16,4096]{1,0:T(8,128)(2,1)S(1)}, bf16[16,4096]{1,0:T(8,128)(2,1)S(1)}, u32[]{:S(2)}, u32[]{:S(2)}) %collective-permute-start.2) | collective-permute-done | bytes 131104 | tf_op jit(solution)/shard_map/gather_projected/ppermute | solution.py:202
  27.9 0.2 collective-permute-start.11
  28.1 0.1 collective-permute-done.3.refs_5_
  28.2 5.6 %collective-permute-start.15 = (f32[64,4096]{1,0:T(8,128)}, f32[64,4096]{1,0:T(8,128)S(1)}, u32[]{:S(2)}, u32[]{:S(2)}) collective-permute-start(f32[64,4096]{1,0:T(8,128)} %bitcast.13), channel_id=1, source_target_pairs={{0,1},{1,0},{2,3},{3,2},{4,5},{5,4},{6,7},{7,6},{8,9},{9,8},{10,11... | collective-permute-start | bytes 3145736 | tf_op jit(solution)/shard_map/swap_inverse/ppermute | solution.py:210
  33.8 1.7 %collective-permute-start.17 = (f32[64,4096]{1,0:T(8,128)S(1)}, f32[64,4096]{1,0:T(8,128)S(1)}, u32[]{:S(2)}, u32[]{:S(2)}) collective-permute-start(f32[64,4096]{1,0:T(8,128)S(1)} %collective-permute-done.16.chip_ref), channel_id=1, source_target_pairs={{0,1},{1,0},{2,3},{3,2},{4,5},{5,4},{6,7},{7,6},{8,9},{9,8},{10,11... | collective-permute-start | bytes 3145736 | tf_op jit(solution)/shard_map/swap_inverse/ppermute | solution.py:210
  35.6 1.7 %collective-permute-start.4 = (bf16[16,4096]{1,0:T(8,128)(2,1)S(1)}, bf16[16,4096]{1,0:T(8,128)(2,1)S(1)}, u32[]{:S(2)}, u32[]{:S(2)}) collective-permute-start(bf16[16,4096]{1,0:T(8,128)(2,1)S(1)} %collective-permute-done.2.refs_4_), channel_id=1, source_target_pairs={{0,8},{8,16},{16,24},{24,32},{32,40},{40,48},{48,56},{56,0},{1,9},... | collective-permute-start | bytes 393224 | tf_op jit(solution)/shard_map/gather_projected/ppermute | solution.py:202
  37.3 0.9 collective-permute-start.13
  38.2 3.7 %collective-permute-done.4.refs_6_ = bf16[16,4096]{1,0:T(8,128)(2,1)S(1)} collective-permute-done((bf16[16,4096]{1,0:T(8,128)(2,1)S(1)}, bf16[16,4096]{1,0:T(8,128)(2,1)S(1)}, u32[]{:S(2)}, u32[]{:S(2)}) %collective-permute-start.4) | collective-permute-done | bytes 131104 | tf_op jit(solution)/shard_map/gather_projected/ppermute | solution.py:202
  41.9 1.3 %collective-permute-start.5 = (bf16[16,4096]{1,0:T(8,128)(2,1)S(1)}, bf16[16,4096]{1,0:T(8,128)(2,1)S(1)}, u32[]{:S(2)}, u32[]{:S(2)}) collective-permute-start(bf16[16,4096]{1,0:T(8,128)(2,1)S(1)} %collective-permute-done.3.refs_5_), channel_id=1, source_target_pairs={{0,56},{8,0},{16,8},{24,16},{32,24},{40,32},{48,40},{56,48},{1,57}... | collective-permute-start | bytes 393224 | tf_op jit(solution)/shard_map/gather_projected/ppermute | solution.py:202
  43.2 0.8 collective-permute-start.12
  44.0 1.1 %collective-permute-start.6 = (bf16[16,4096]{1,0:T(8,128)(2,1)S(1)}, bf16[16,4096]{1,0:T(8,128)(2,1)S(1)}, u32[]{:S(2)}, u32[]{:S(2)}) collective-permute-start(bf16[16,4096]{1,0:T(8,128)(2,1)S(1)} %collective-permute-done.4.refs_6_), channel_id=1, source_target_pairs={{0,8},{8,16},{16,24},{24,32},{32,40},{40,48},{48,56},{56,0},{1,9},... | collective-permute-start | bytes 393224 | tf_op jit(solution)/shard_map/gather_projected/ppermute | solution.py:202
  45.2 1.5 %collective-permute-start.14 = (bf16[16,4096]{1,0:T(8,128)(2,1)S(1)}, bf16[16,4096]{1,0:T(8,128)(2,1)S(1)}, u32[]{:S(2)}, u32[]{:S(2)}) collective-permute-start(bf16[16,4096]{1,0:T(8,128)(2,1)S(1)} %collective-permute-done.13.refs_15_), channel_id=1, source_target_pairs={{0,56},{8,0},{16,8},{24,16},{32,24},{40,32},{48,40},{56,48},{1,57}... | collective-permute-start | bytes 393224 | tf_op jit(solution)/shard_map/gather_projected/ppermute | solution.py:202
  46.7 1.2 %copy-done.2 = f32[1,64,4096]{2,1,0:T(8,128)S(1)} copy-done((f32[1,64,4096]{2,1,0:T(8,128)S(1)}, f32[1,64,4096]{2,1,0:T(8,128)}, u32[]{:S(2)}) %copy-start.2) | copy-done | bytes 1048600
  47.9 1.2 %split_inverse.1 = (bf16[256,4096]{1,0:T(8,128)(2,1)S(1)}, bf16[256,4096]{1,0:T(8,128)(2,1)S(1)}) custom-call(s32[50]{0:T(128)S(1)} %concatenate.3.where_ref.refs_0_, f32[64,4096]{1,0:T(8,128)S(1)} %bitcast.14, f32[64,4096]{1,0:T(8,128)S(1)} %collective-permute-done.15.core_ref, f32[64,4096]{1,0:T(8,128)S(1)} %collective-permute-done.16.chip_ref, ...), custom_call_target="tpu_custom_call" | custom-call | flops 2097152 | bytes 8388608 | tf_op jit(solution)/shard_map/split_inverse/split_inverse/pallas_call | solution.py:71
  49.1 2.1 %collective-permute-done.6.refs_8_ = bf16[16,4096]{1,0:T(8,128)(2,1)S(1)} collective-permute-done((bf16[16,4096]{1,0:T(8,128)(2,1)S(1)}, bf16[16,4096]{1,0:T(8,128)(2,1)S(1)}, u32[]{:S(2)}, u32[]{:S(2)}) %collective-permute-start.6) | collective-permute-done | bytes 131104 | tf_op jit(solution)/shard_map/gather_projected/ppermute | solution.py:202
  51.2 1.8 %precondition.1.refs_1_ = bf16[256,256]{1,0:T(8,128)(2,1)S(1)} custom-call(s32[50]{0:T(128)S(1)} %concatenate.3.where_ref.refs_0_, bf16[16,4096]{1,0:T(8,128)(2,1)S(1)} %reshape.12.refs_1_, bf16[16,4096]{1,0:T(8,128)(2,1)S(1)} %collective-permute-done.refs_2_, bf16[16,4096]{1,0:T(8,128)(2,1)S(1)} %collective-permute-done.1.refs_3_, ...), custom_call_target="tpu_custom_call" | custom-call | flops 1073741824 | bytes 6291456 | tf_op jit(solution)/shard_map/precondition/precondition/pallas_call | solution.py:97
  53.0 0.4 collective-permute-start.22
  53.4 0.2 collective-permute-start.18
  53.7 2.5 %collective-permute-start.32 = (bf16[256,256]{1,0:T(8,128)(2,1)S(1)}, bf16[256,256]{1,0:T(8,128)(2,1)S(1)}, u32[]{:S(2)}, u32[]{:S(2)}) collective-permute-start(bf16[256,256]{1,0:T(8,128)(2,1)S(1)} %precondition.1.refs_1_), channel_id=1, source_target_pairs={{0,56},{8,0},{16,8},{24,16},{32,24},{40,32},{48,40},{56,48},{1,57}... | collective-permute-start | bytes 393224 | tf_op jit(solution)/shard_map/gather_preconditioned/ppermute | solution.py:202
  56.1 1.1 %collective-permute-done.22.refs_8_ = bf16[256,256]{1,0:T(8,128)(2,1)S(1)} collective-permute-done((bf16[256,256]{1,0:T(8,128)(2,1)S(1)}, bf16[256,256]{1,0:T(8,128)(2,1)S(1)}, u32[]{:S(2)}, u32[]{:S(2)}) %collective-permute-start.22) | collective-permute-done | bytes 131104 | tf_op jit(solution)/shard_map/gather_preconditioned/ppermute | solution.py:245
  57.2 2.7 %collective-permute-start.26 = (bf16[256,256]{1,0:T(8,128)(2,1)S(1)}, bf16[256,256]{1,0:T(8,128)(2,1)S(1)}, u32[]{:S(2)}, u32[]{:S(2)}) collective-permute-start(bf16[256,256]{1,0:T(8,128)(2,1)S(1)} %collective-permute-done.22.refs_8_), channel_id=1, source_target_pairs={{0,56},{8,0},{16,8},{24,16},{32,24},{40,32},{48,40},{56,48},{1,57}... | collective-permute-start | bytes 393224 | tf_op jit(solution)/shard_map/gather_preconditioned/ppermute | solution.py:202
  59.9 2.7 %collective-permute-start.33 = (bf16[256,256]{1,0:T(8,128)(2,1)S(1)}, bf16[256,256]{1,0:T(8,128)(2,1)S(1)}, u32[]{:S(2)}, u32[]{:S(2)}) collective-permute-start(bf16[256,256]{1,0:T(8,128)(2,1)S(1)} %collective-permute-done.32.refs_3_), channel_id=1, source_target_pairs={{0,56},{8,0},{16,8},{24,16},{32,24},{40,32},{48,40},{56,48},{1,57}... | collective-permute-start | bytes 393224 | tf_op jit(solution)/shard_map/gather_preconditioned/ppermute | solution.py:202
  62.6 0.3 collective-permute-done.23.refs_9_
  62.9 3.0 %collective-permute-start.27 = (bf16[256,256]{1,0:T(8,128)(2,1)S(1)}, bf16[256,256]{1,0:T(8,128)(2,1)S(1)}, u32[]{:S(2)}, u32[]{:S(2)}) collective-permute-start(bf16[256,256]{1,0:T(8,128)(2,1)S(1)} %collective-permute-done.26.refs_10_), channel_id=1, source_target_pairs={{0,56},{8,0},{16,8},{24,16},{32,24},{40,32},{48,40},{56,48},{1,57}... | collective-permute-start | bytes 393224 | tf_op jit(solution)/shard_map/gather_preconditioned/ppermute | solution.py:202
  65.9 0.2 collective-permute-done.19.refs_4_
  66.1 2.7 %collective-permute-start.34 = (bf16[256,256]{1,0:T(8,128)(2,1)S(1)}, bf16[256,256]{1,0:T(8,128)(2,1)S(1)}, u32[]{:S(2)}, u32[]{:S(2)}) collective-permute-start(bf16[256,256]{1,0:T(8,128)(2,1)S(1)} %collective-permute-done.33.refs_5_), channel_id=1, source_target_pairs={{0,56},{8,0},{16,8},{24,16},{32,24},{40,32},{48,40},{56,48},{1,57}... | collective-permute-start | bytes 393224 | tf_op jit(solution)/shard_map/gather_preconditioned/ppermute | solution.py:202
  68.8 2.9 %collective-permute-start.28 = (bf16[256,256]{1,0:T(8,128)(2,1)S(1)}, bf16[256,256]{1,0:T(8,128)(2,1)S(1)}, u32[]{:S(2)}, u32[]{:S(2)}) collective-permute-start(bf16[256,256]{1,0:T(8,128)(2,1)S(1)} %collective-permute-done.27.refs_12_), channel_id=1, source_target_pairs={{0,56},{8,0},{16,8},{24,16},{32,24},{40,32},{48,40},{56,48},{1,57}... | collective-permute-start | bytes 393224 | tf_op jit(solution)/shard_map/gather_preconditioned/ppermute | solution.py:202
  71.7 5.0 %collective-permute-start.30 = (bf16[256,4096]{1,0:T(8,128)(2,1)S(1)}, bf16[256,4096]{1,0:T(8,128)(2,1)S(1)}, u32[]{:S(2)}, u32[]{:S(2)}) collective-permute-start(bf16[256,4096]{1,0:T(8,128)(2,1)S(1)} %bitcast.8), channel_id=1, source_target_pairs={{0,1},{1,0},{2,3},{3,2},{4,5},{5,4},{6,7},{7,6},{8,9},{9,8},{10,11... | collective-permute-start | bytes 6291464 | tf_op jit(solution)/shard_map/swap_stored/ppermute | solution.py:210
  76.8 2.9 %collective-permute-start.35 = (bf16[256,4096]{1,0:T(8,128)(2,1)S(1)}, bf16[256,4096]{1,0:T(8,128)(2,1)S(1)}, u32[]{:S(2)}, u32[]{:S(2)}) collective-permute-start(bf16[256,4096]{1,0:T(8,128)(2,1)S(1)} %collective-permute-done.31.refs_15_.refs_7_), channel_id=1, source_target_pairs={{0,1},{1,0},{2,3},{3,2},{4,5},{5,4},{6,7},{7,6},{8,9},{9,8},{10,11... | collective-permute-start | bytes 6291464 | tf_op jit(solution)/shard_map/swap_stored/ppermute | solution.py:210
  79.7 3.0 %collective-permute-start.29 = (bf16[256,256]{1,0:T(8,128)(2,1)S(1)}, bf16[256,256]{1,0:T(8,128)(2,1)S(1)}, u32[]{:S(2)}, u32[]{:S(2)}) collective-permute-start(bf16[256,256]{1,0:T(8,128)(2,1)S(1)} %collective-permute-done.28.refs_3_), channel_id=1, source_target_pairs={{0,56},{8,0},{16,8},{24,16},{32,24},{40,32},{48,40},{56,48},{1,57}... | collective-permute-start | bytes 393224 | tf_op jit(solution)/shard_map/gather_preconditioned/ppermute | solution.py:202
  82.7 0.9 collective-permute-done.35.refs_16_.refs_8_
  83.5 2.5 %score.2.refs_9_ = f32[256,1024]{1,0:T(8,128)S(1)} custom-call(s32[50]{0:T(128)S(1)} %concatenate.3.where_ref.refs_0_, bf16[256,256]{1,0:T(8,128)(2,1)S(1)} %precondition.1.refs_1_, bf16[256,256]{1,0:T(8,128)(2,1)S(1)} %collective-permute-done.18.refs_2_, bf16[256,256]{1,0:T(8,128)(2,1)S(1)} %collective-permute-done.32.refs_3_, ...), custom_call_target="tpu_custom_call" | custom-call | flops 1610612736 | bytes 7864320 | tf_op jit(solution)/shard_map/score/score/pallas_call | solution.py:144
  86.1 0.4 collective-permute-done.21.refs_1_
  86.5 1.5 %score.3 = (f32[64,1024]{1,0:T(8,128)S(1)}, bf16[64,1024]{1,0:T(8,128)(2,1)S(1)}, bf16[64,1024]{1,0:T(8,128)(2,1)S(1)}, bf16[64,1024]{1,0:T(8,128)(2,1)S(1)}) custom-call(s32[50]{0:T(128)S(1)} %concatenate.3.where_ref.refs_0_, bf16[256,256]{1,0:T(8,128)(2,1)S(1)} %collective-permute-done.21.refs_1_, bf16[256,256]{1,0:T(8,128)(2,1)S(1)} %collective-permute-done.25.refs_2_, ...), custom_call_target="tpu_custom_call" | custom-call | flops 536870912 | bytes 2621440 | tf_op jit(solution)/shard_map/score/score/pallas_call | solution.py:144
  88.0 1.3 %collective-permute-start.36 = (bf16[64,1024]{1,0:T(8,128)(2,1)S(1)}, bf16[64,1024]{1,0:T(8,128)(2,1)S(1)}, u32[]{:S(2)}, u32[]{:S(2)}) collective-permute-start(bf16[64,1024]{1,0:T(8,128)(2,1)S(1)} %get-tuple-element.28), channel_id=1, source_target_pairs={{0,64},{64,128},{128,192},{192,0},{1,65},{65,129},{129,193},{193,1... | collective-permute-start | bytes 393224 | tf_op jit(solution)/shard_map/sum_layers/ppermute | solution.py:202
  89.3 2.5 %collective-permute-start.37 = (bf16[64,1024]{1,0:T(8,128)(2,1)S(1)}, bf16[64,1024]{1,0:T(8,128)(2,1)S(1)}, u32[]{:S(2)}, u32[]{:S(2)}) collective-permute-start(bf16[64,1024]{1,0:T(8,128)(2,1)S(1)} %get-tuple-element.29), channel_id=1, source_target_pairs={{0,128},{64,192},{128,0},{192,64},{1,129},{65,193},{129,1},{193,65... | collective-permute-start | bytes 393224 | tf_op jit(solution)/shard_map/sum_layers/ppermute | solution.py:202
  91.8 1.2 %collective-permute-start.38 = (bf16[64,1024]{1,0:T(8,128)(2,1)S(1)}, bf16[64,1024]{1,0:T(8,128)(2,1)S(1)}, u32[]{:S(2)}, u32[]{:S(2)}) collective-permute-start(bf16[64,1024]{1,0:T(8,128)(2,1)S(1)} %get-tuple-element.30), channel_id=1, source_target_pairs={{0,192},{64,0},{128,64},{192,128},{1,193},{65,1},{129,65},{193,129... | collective-permute-start | bytes 393224 | tf_op jit(solution)/shard_map/sum_layers/ppermute | solution.py:202
  92.9 0.9 collective-permute-done.36.a_ref
  93.8 3.8 %collective-permute-done.37.b_ref = bf16[64,1024]{1,0:T(8,128)(2,1)S(1)} collective-permute-done((bf16[64,1024]{1,0:T(8,128)(2,1)S(1)}, bf16[64,1024]{1,0:T(8,128)(2,1)S(1)}, u32[]{:S(2)}, u32[]{:S(2)}) %collective-permute-start.37) | collective-permute-done | bytes 131104 | tf_op jit(solution)/shard_map/sum_layers/ppermute | solution.py:202
  97.7 1.5 %collective-permute-start.39 = (bf16[64,256]{1,0:T(8,128)(2,1)S(1)}, bf16[64,256]{1,0:T(8,128)(2,1)S(1)}, u32[]{:S(2)}, u32[]{:S(2)}) collective-permute-start(bf16[64,256]{1,0:T(8,128)(2,1)S(1)} %get-tuple-element.32), channel_id=1, source_target_pairs={{0,1},{1,0},{2,3},{3,2},{4,5},{5,4},{6,7},{7,6},{8,9},{9,8},{10,11... | collective-permute-start | bytes 98312 | tf_op jit(solution)/shard_map/exchange_examples/ppermute | solution.py:281
  99.2 2.2 %collective-permute-start.40 = (bf16[64,256]{1,0:T(8,128)(2,1)S(1)}, bf16[64,256]{1,0:T(8,128)(2,1)S(1)}, u32[]{:S(2)}, u32[]{:S(2)}) collective-permute-start(bf16[64,256]{1,0:T(8,128)(2,1)S(1)} %get-tuple-element.33), channel_id=1, source_target_pairs={{0,6},{1,7},{2,4},{3,5},{4,2},{5,3},{6,0},{7,1},{8,14},{9,15},{10,... | collective-permute-start | bytes 98312 | tf_op jit(solution)/shard_map/exchange_examples/ppermute | solution.py:281
  101.4 0.7 collective-permute-start.41
  102.1 1.0 collective-permute-done.40.refs_2_
  103.2 2.8 %collective-permute-done.41.refs_3_ = bf16[64,256]{1,0:T(8,128)(2,1)S(1)} collective-permute-done((bf16[64,256]{1,0:T(8,128)(2,1)S(1)}, bf16[64,256]{1,0:T(8,128)(2,1)S(1)}, u32[]{:S(2)}, u32[]{:S(2)}) %collective-permute-start.41) | collective-permute-done | bytes 32800 | tf_op jit(solution)/shard_map/exchange_examples/ppermute | solution.py:281
  106.0 1.3 %place_parts.1 = f32[256,256]{1,0:T(8,128)} custom-call(s32[50]{0:T(128)S(1)} %concatenate.3.where_ref.refs_0_, f32[64,256]{1,0:T(8,128)S(1)} %get-tuple-element.31.refs_0_, bf16[64,256]{1,0:T(8,128)(2,1)S(1)} %collective-permute-done.39.refs_1_, bf16[64,256]{1,0:T(8,128)(2,1)S(1)} %collective-permute-done.40.refs_2_, ...), custom_call_target="tpu_custom_call" | custom-call | flops 65536 | bytes 524288 | tf_op jit(solution)/shard_map/exchange_examples/place_parts/pallas_call | solution.py:190
  (47 shorter events, 0.4 us)
Async XLA Ops:
  0.0 18.1 %copy-start = (bf16[1,256,4096]{2,1,0:T(8,128)(2,1)S(1)}, bf16[1,256,4096]{2,1,0:T(8,128)(2,1)}, u32[]{:S(2)}) copy-start(bf16[1,256,4096]{2,1,0:T(8,128)(2,1)} %param.8) | copy-start | bytes 6291460
  0.0 33.8 %collective-permute-start.16 = (f32[64,4096]{1,0:T(8,128)}, f32[64,4096]{1,0:T(8,128)S(1)}, u32[]{:S(2)}, u32[]{:S(2)}) collective-permute-start(f32[64,4096]{1,0:T(8,128)} %bitcast.12), channel_id=1, source_target_pairs={{0,6},{6,0},{2,4},{4,2},{1,7},{7,1},{3,5},{5,3},{8,14},{14,8},{10,... | collective-permute-start | bytes 3145736 | tf_op jit(solution)/shard_map/swap_inverse/ppermute | solution.py:245
  4.8 1.6 %copy-start.1 = (bf16[1,16,512,128]{3,2,1,0:T(8,128)(2,1)S(1)}, bf16[1,16,512,128]{3,2,1,0:T(8,128)(2,1)}, u32[]{:S(2)}) copy-start(bf16[1,16,512,128]{3,2,1,0:T(8,128)(2,1)} %param.5) | copy-start | bytes 6291460
  6.4 0.7 copy-start.3
  9.5 5.8 %collective-permute-start.7 = (bf16[16,4096]{1,0:T(8,128)(2,1)S(1)}, bf16[16,4096]{1,0:T(8,128)(2,1)S(1)}, u32[]{:S(2)}, u32[]{:S(2)}) collective-permute-start(bf16[16,4096]{1,0:T(8,128)(2,1)S(1)} %reshape.12.refs_1_), channel_id=1, source_target_pairs={{0,2},{2,0},{4,6},{6,4},{1,3},{3,1},{5,7},{7,5},{8,10},{10,8},{12,... | collective-permute-start | bytes 393224 | tf_op jit(solution)/shard_map/gather_projected/ppermute | solution.py:245
  9.6 8.5 %collective-permute-start = (bf16[16,4096]{1,0:T(8,128)(2,1)S(1)}, bf16[16,4096]{1,0:T(8,128)(2,1)S(1)}, u32[]{:S(2)}, u32[]{:S(2)}) collective-permute-start(bf16[16,4096]{1,0:T(8,128)(2,1)S(1)} %reshape.12.refs_1_), channel_id=1, source_target_pairs={{0,8},{8,16},{16,24},{24,32},{32,40},{40,48},{48,56},{56,0},{1,9},... | collective-permute-start | bytes 393224 | tf_op jit(solution)/shard_map/gather_projected/ppermute | solution.py:202
  11.3 6.8 %collective-permute-start.1 = (bf16[16,4096]{1,0:T(8,128)(2,1)S(1)}, bf16[16,4096]{1,0:T(8,128)(2,1)S(1)}, u32[]{:S(2)}, u32[]{:S(2)}) collective-permute-start(bf16[16,4096]{1,0:T(8,128)(2,1)S(1)} %reshape.12.refs_1_), channel_id=1, source_target_pairs={{0,56},{8,0},{16,8},{24,16},{32,24},{40,32},{48,40},{56,48},{1,57}... | collective-permute-start | bytes 393224 | tf_op jit(solution)/shard_map/gather_projected/ppermute | solution.py:202
  18.1 53.7 %collective-permute-start.31 = (bf16[256,4096]{1,0:T(8,128)(2,1)S(1)}, bf16[256,4096]{1,0:T(8,128)(2,1)S(1)}, u32[]{:S(2)}, u32[]{:S(2)}) collective-permute-start(bf16[256,4096]{1,0:T(8,128)(2,1)S(1)} %bitcast.7), channel_id=1, source_target_pairs={{0,6},{6,0},{2,4},{4,2},{1,7},{7,1},{3,5},{5,3},{8,14},{14,8},{10,... | collective-permute-start | bytes 6291464 | tf_op jit(solution)/shard_map/swap_stored/ppermute | solution.py:245
  18.8 5.3 %collective-permute-start.8 = (bf16[16,4096]{1,0:T(8,128)(2,1)S(1)}, bf16[16,4096]{1,0:T(8,128)(2,1)S(1)}, u32[]{:S(2)}, u32[]{:S(2)}) collective-permute-start(bf16[16,4096]{1,0:T(8,128)(2,1)S(1)} %collective-permute-done.7.refs_9_), channel_id=1, source_target_pairs={{0,8},{8,16},{16,24},{24,32},{32,40},{40,48},{48,56},{56,0},{1,9},... | collective-permute-start | bytes 393224 | tf_op jit(solution)/shard_map/gather_projected/ppermute | solution.py:202
  18.8 6.6 %collective-permute-start.9 = (bf16[16,4096]{1,0:T(8,128)(2,1)S(1)}, bf16[16,4096]{1,0:T(8,128)(2,1)S(1)}, u32[]{:S(2)}, u32[]{:S(2)}) collective-permute-start(bf16[16,4096]{1,0:T(8,128)(2,1)S(1)} %collective-permute-done.7.refs_9_), channel_id=1, source_target_pairs={{0,56},{8,0},{16,8},{24,16},{32,24},{40,32},{48,40},{56,48},{1,57}... | collective-permute-start | bytes 393224 | tf_op jit(solution)/shard_map/gather_projected/ppermute | solution.py:202
  21.5 6.4 %collective-permute-start.2 = (bf16[16,4096]{1,0:T(8,128)(2,1)S(1)}, bf16[16,4096]{1,0:T(8,128)(2,1)S(1)}, u32[]{:S(2)}, u32[]{:S(2)}) collective-permute-start(bf16[16,4096]{1,0:T(8,128)(2,1)S(1)} %collective-permute-done.refs_2_), channel_id=1, source_target_pairs={{0,8},{8,16},{16,24},{24,32},{32,40},{40,48},{48,56},{56,0},{1,9},... | collective-permute-start | bytes 393224 | tf_op jit(solution)/shard_map/gather_projected/ppermute | solution.py:202
  24.1 4.1 %collective-permute-start.3 = (bf16[16,4096]{1,0:T(8,128)(2,1)S(1)}, bf16[16,4096]{1,0:T(8,128)(2,1)S(1)}, u32[]{:S(2)}, u32[]{:S(2)}) collective-permute-start(bf16[16,4096]{1,0:T(8,128)(2,1)S(1)} %collective-permute-done.1.refs_3_), channel_id=1, source_target_pairs={{0,56},{8,0},{16,8},{24,16},{32,24},{40,32},{48,40},{56,48},{1,57}... | collective-permute-start | bytes 393224 | tf_op jit(solution)/shard_map/gather_projected/ppermute | solution.py:202
  25.4 8.4 %collective-permute-start.10 = (bf16[16,4096]{1,0:T(8,128)(2,1)S(1)}, bf16[16,4096]{1,0:T(8,128)(2,1)S(1)}, u32[]{:S(2)}, u32[]{:S(2)}) collective-permute-start(bf16[16,4096]{1,0:T(8,128)(2,1)S(1)} %collective-permute-done.8.refs_10_), channel_id=1, source_target_pairs={{0,8},{8,16},{16,24},{24,32},{32,40},{40,48},{48,56},{56,0},{1,9},... | collective-permute-start | bytes 393224 | tf_op jit(solution)/shard_map/gather_projected/ppermute | solution.py:202
  27.9 5.9 %collective-permute-start.11 = (bf16[16,4096]{1,0:T(8,128)(2,1)S(1)}, bf16[16,4096]{1,0:T(8,128)(2,1)S(1)}, u32[]{:S(2)}, u32[]{:S(2)}) collective-permute-start(bf16[16,4096]{1,0:T(8,128)(2,1)S(1)} %collective-permute-done.9.refs_11_), channel_id=1, source_target_pairs={{0,56},{8,0},{16,8},{24,16},{32,24},{40,32},{48,40},{56,48},{1,57}... | collective-permute-start | bytes 393224 | tf_op jit(solution)/shard_map/gather_projected/ppermute | solution.py:202
  28.2 15.8 %collective-permute-start.15 = (f32[64,4096]{1,0:T(8,128)}, f32[64,4096]{1,0:T(8,128)S(1)}, u32[]{:S(2)}, u32[]{:S(2)}) collective-permute-start(f32[64,4096]{1,0:T(8,128)} %bitcast.13), channel_id=1, source_target_pairs={{0,1},{1,0},{2,3},{3,2},{4,5},{5,4},{6,7},{7,6},{8,9},{9,8},{10,11... | collective-permute-start | bytes 3145736 | tf_op jit(solution)/shard_map/swap_inverse/ppermute | solution.py:210
  33.8 11.3 %collective-permute-start.17 = (f32[64,4096]{1,0:T(8,128)S(1)}, f32[64,4096]{1,0:T(8,128)S(1)}, u32[]{:S(2)}, u32[]{:S(2)}) collective-permute-start(f32[64,4096]{1,0:T(8,128)S(1)} %collective-permute-done.16.chip_ref), channel_id=1, source_target_pairs={{0,1},{1,0},{2,3},{3,2},{4,5},{5,4},{6,7},{7,6},{8,9},{9,8},{10,11... | collective-permute-start | bytes 3145736 | tf_op jit(solution)/shard_map/swap_inverse/ppermute | solution.py:210
  35.6 6.3 %collective-permute-start.4 = (bf16[16,4096]{1,0:T(8,128)(2,1)S(1)}, bf16[16,4096]{1,0:T(8,128)(2,1)S(1)}, u32[]{:S(2)}, u32[]{:S(2)}) collective-permute-start(bf16[16,4096]{1,0:T(8,128)(2,1)S(1)} %collective-permute-done.2.refs_4_), channel_id=1, source_target_pairs={{0,8},{8,16},{16,24},{24,32},{32,40},{40,48},{48,56},{56,0},{1,9},... | collective-permute-start | bytes 393224 | tf_op jit(solution)/shard_map/gather_projected/ppermute | solution.py:202
  37.3 5.9 %collective-permute-start.13 = (bf16[16,4096]{1,0:T(8,128)(2,1)S(1)}, bf16[16,4096]{1,0:T(8,128)(2,1)S(1)}, u32[]{:S(2)}, u32[]{:S(2)}) collective-permute-start(bf16[16,4096]{1,0:T(8,128)(2,1)S(1)} %collective-permute-done.11.refs_13_), channel_id=1, source_target_pairs={{0,56},{8,0},{16,8},{24,16},{32,24},{40,32},{48,40},{56,48},{1,57}... | collective-permute-start | bytes 393224 | tf_op jit(solution)/shard_map/gather_projected/ppermute | solution.py:202
  41.9 7.2 %collective-permute-start.5 = (bf16[16,4096]{1,0:T(8,128)(2,1)S(1)}, bf16[16,4096]{1,0:T(8,128)(2,1)S(1)}, u32[]{:S(2)}, u32[]{:S(2)}) collective-permute-start(bf16[16,4096]{1,0:T(8,128)(2,1)S(1)} %collective-permute-done.3.refs_5_), channel_id=1, source_target_pairs={{0,56},{8,0},{16,8},{24,16},{32,24},{40,32},{48,40},{56,48},{1,57}... | collective-permute-start | bytes 393224 | tf_op jit(solution)/shard_map/gather_projected/ppermute | solution.py:202
  43.2 5.9 %collective-permute-start.12 = (bf16[16,4096]{1,0:T(8,128)(2,1)S(1)}, bf16[16,4096]{1,0:T(8,128)(2,1)S(1)}, u32[]{:S(2)}, u32[]{:S(2)}) collective-permute-start(bf16[16,4096]{1,0:T(8,128)(2,1)S(1)} %collective-permute-done.10.refs_12_), channel_id=1, source_target_pairs={{0,8},{8,16},{16,24},{24,32},{32,40},{40,48},{48,56},{56,0},{1,9},... | collective-permute-start | bytes 393224 | tf_op jit(solution)/shard_map/gather_projected/ppermute | solution.py:202
  44.0 7.2 %collective-permute-start.6 = (bf16[16,4096]{1,0:T(8,128)(2,1)S(1)}, bf16[16,4096]{1,0:T(8,128)(2,1)S(1)}, u32[]{:S(2)}, u32[]{:S(2)}) collective-permute-start(bf16[16,4096]{1,0:T(8,128)(2,1)S(1)} %collective-permute-done.4.refs_6_), channel_id=1, source_target_pairs={{0,8},{8,16},{16,24},{24,32},{32,40},{40,48},{48,56},{56,0},{1,9},... | collective-permute-start | bytes 393224 | tf_op jit(solution)/shard_map/gather_projected/ppermute | solution.py:202
  45.2 6.0 %collective-permute-start.14 = (bf16[16,4096]{1,0:T(8,128)(2,1)S(1)}, bf16[16,4096]{1,0:T(8,128)(2,1)S(1)}, u32[]{:S(2)}, u32[]{:S(2)}) collective-permute-start(bf16[16,4096]{1,0:T(8,128)(2,1)S(1)} %collective-permute-done.13.refs_15_), channel_id=1, source_target_pairs={{0,56},{8,0},{16,8},{24,16},{32,24},{40,32},{48,40},{56,48},{1,57}... | collective-permute-start | bytes 393224 | tf_op jit(solution)/shard_map/gather_projected/ppermute | solution.py:202
  46.7 1.2 %copy-start.2 = (f32[1,64,4096]{2,1,0:T(8,128)S(1)}, f32[1,64,4096]{2,1,0:T(8,128)}, u32[]{:S(2)}) copy-start(f32[1,64,4096]{2,1,0:T(8,128)} %param.7) | copy-start | bytes 3145732
  53.0 4.2 %collective-permute-start.22 = (bf16[256,256]{1,0:T(8,128)(2,1)S(1)}, bf16[256,256]{1,0:T(8,128)(2,1)S(1)}, u32[]{:S(2)}, u32[]{:S(2)}) collective-permute-start(bf16[256,256]{1,0:T(8,128)(2,1)S(1)} %precondition.1.refs_1_), channel_id=1, source_target_pairs={{0,2},{2,0},{4,6},{6,4},{1,3},{3,1},{5,7},{7,5},{8,10},{10,8},{12,... | collective-permute-start | bytes 393224 | tf_op jit(solution)/shard_map/gather_preconditioned/ppermute | solution.py:245
  53.4 6.5 %collective-permute-start.18 = (bf16[256,256]{1,0:T(8,128)(2,1)S(1)}, bf16[256,256]{1,0:T(8,128)(2,1)S(1)}, u32[]{:S(2)}, u32[]{:S(2)}) collective-permute-start(bf16[256,256]{1,0:T(8,128)(2,1)S(1)} %precondition.1.refs_1_), channel_id=1, source_target_pairs={{0,8},{8,16},{16,24},{24,32},{32,40},{40,48},{48,56},{56,0},{1,9},... | collective-permute-start | bytes 393224 | tf_op jit(solution)/shard_map/gather_preconditioned/ppermute | solution.py:202
  53.7 6.2 %collective-permute-start.32 = (bf16[256,256]{1,0:T(8,128)(2,1)S(1)}, bf16[256,256]{1,0:T(8,128)(2,1)S(1)}, u32[]{:S(2)}, u32[]{:S(2)}) collective-permute-start(bf16[256,256]{1,0:T(8,128)(2,1)S(1)} %precondition.1.refs_1_), channel_id=1, source_target_pairs={{0,56},{8,0},{16,8},{24,16},{32,24},{40,32},{48,40},{56,48},{1,57}... | collective-permute-start | bytes 393224 | tf_op jit(solution)/shard_map/gather_preconditioned/ppermute | solution.py:202
  57.2 5.7 %collective-permute-start.23 = (bf16[256,256]{1,0:T(8,128)(2,1)S(1)}, bf16[256,256]{1,0:T(8,128)(2,1)S(1)}, u32[]{:S(2)}, u32[]{:S(2)}) collective-permute-start(bf16[256,256]{1,0:T(8,128)(2,1)S(1)} %collective-permute-done.22.refs_8_), channel_id=1, source_target_pairs={{0,8},{8,16},{16,24},{24,32},{32,40},{40,48},{48,56},{56,0},{1,9},... | collective-permute-start | bytes 393224 | tf_op jit(solution)/shard_map/gather_preconditioned/ppermute | solution.py:202
  57.2 5.7 %collective-permute-start.26 = (bf16[256,256]{1,0:T(8,128)(2,1)S(1)}, bf16[256,256]{1,0:T(8,128)(2,1)S(1)}, u32[]{:S(2)}, u32[]{:S(2)}) collective-permute-start(bf16[256,256]{1,0:T(8,128)(2,1)S(1)} %collective-permute-done.22.refs_8_), channel_id=1, source_target_pairs={{0,56},{8,0},{16,8},{24,16},{32,24},{40,32},{48,40},{56,48},{1,57}... | collective-permute-start | bytes 393224 | tf_op jit(solution)/shard_map/gather_preconditioned/ppermute | solution.py:202
  59.9 6.2 %collective-permute-start.19 = (bf16[256,256]{1,0:T(8,128)(2,1)S(1)}, bf16[256,256]{1,0:T(8,128)(2,1)S(1)}, u32[]{:S(2)}, u32[]{:S(2)}) collective-permute-start(bf16[256,256]{1,0:T(8,128)(2,1)S(1)} %collective-permute-done.18.refs_2_), channel_id=1, source_target_pairs={{0,8},{8,16},{16,24},{24,32},{32,40},{40,48},{48,56},{56,0},{1,9},... | collective-permute-start | bytes 393224 | tf_op jit(solution)/shard_map/gather_preconditioned/ppermute | solution.py:202
  59.9 6.2 %collective-permute-start.33 = (bf16[256,256]{1,0:T(8,128)(2,1)S(1)}, bf16[256,256]{1,0:T(8,128)(2,1)S(1)}, u32[]{:S(2)}, u32[]{:S(2)}) collective-permute-start(bf16[256,256]{1,0:T(8,128)(2,1)S(1)} %collective-permute-done.32.refs_3_), channel_id=1, source_target_pairs={{0,56},{8,0},{16,8},{24,16},{32,24},{40,32},{48,40},{56,48},{1,57}... | collective-permute-start | bytes 393224 | tf_op jit(solution)/shard_map/gather_preconditioned/ppermute | solution.py:202
  62.9 5.9 %collective-permute-start.24 = (bf16[256,256]{1,0:T(8,128)(2,1)S(1)}, bf16[256,256]{1,0:T(8,128)(2,1)S(1)}, u32[]{:S(2)}, u32[]{:S(2)}) collective-permute-start(bf16[256,256]{1,0:T(8,128)(2,1)S(1)} %collective-permute-done.23.refs_9_), channel_id=1, source_target_pairs={{0,8},{8,16},{16,24},{24,32},{32,40},{40,48},{48,56},{56,0},{1,9},... | collective-permute-start | bytes 393224 | tf_op jit(solution)/shard_map/gather_preconditioned/ppermute | solution.py:202
  62.9 5.9 %collective-permute-start.27 = (bf16[256,256]{1,0:T(8,128)(2,1)S(1)}, bf16[256,256]{1,0:T(8,128)(2,1)S(1)}, u32[]{:S(2)}, u32[]{:S(2)}) collective-permute-start(bf16[256,256]{1,0:T(8,128)(2,1)S(1)} %collective-permute-done.26.refs_10_), channel_id=1, source_target_pairs={{0,56},{8,0},{16,8},{24,16},{32,24},{40,32},{48,40},{56,48},{1,57}... | collective-permute-start | bytes 393224 | tf_op jit(solution)/shard_map/gather_preconditioned/ppermute | solution.py:202
  66.1 10.7 %collective-permute-start.20 = (bf16[256,256]{1,0:T(8,128)(2,1)S(1)}, bf16[256,256]{1,0:T(8,128)(2,1)S(1)}, u32[]{:S(2)}, u32[]{:S(2)}) collective-permute-start(bf16[256,256]{1,0:T(8,128)(2,1)S(1)} %collective-permute-done.19.refs_4_), channel_id=1, source_target_pairs={{0,8},{8,16},{16,24},{24,32},{32,40},{40,48},{48,56},{56,0},{1,9},... | collective-permute-start | bytes 393224 | tf_op jit(solution)/shard_map/gather_preconditioned/ppermute | solution.py:202
  66.1 10.7 %collective-permute-start.34 = (bf16[256,256]{1,0:T(8,128)(2,1)S(1)}, bf16[256,256]{1,0:T(8,128)(2,1)S(1)}, u32[]{:S(2)}, u32[]{:S(2)}) collective-permute-start(bf16[256,256]{1,0:T(8,128)(2,1)S(1)} %collective-permute-done.33.refs_5_), channel_id=1, source_target_pairs={{0,56},{8,0},{16,8},{24,16},{32,24},{40,32},{48,40},{56,48},{1,57}... | collective-permute-start | bytes 393224 | tf_op jit(solution)/shard_map/gather_preconditioned/ppermute | solution.py:202
  68.8 8.0 %collective-permute-start.25 = (bf16[256,256]{1,0:T(8,128)(2,1)S(1)}, bf16[256,256]{1,0:T(8,128)(2,1)S(1)}, u32[]{:S(2)}, u32[]{:S(2)}) collective-permute-start(bf16[256,256]{1,0:T(8,128)(2,1)S(1)} %collective-permute-done.24.refs_11_), channel_id=1, source_target_pairs={{0,8},{8,16},{16,24},{24,32},{32,40},{40,48},{48,56},{56,0},{1,9},... | collective-permute-start | bytes 393224 | tf_op jit(solution)/shard_map/gather_preconditioned/ppermute | solution.py:202
  68.8 8.0 %collective-permute-start.28 = (bf16[256,256]{1,0:T(8,128)(2,1)S(1)}, bf16[256,256]{1,0:T(8,128)(2,1)S(1)}, u32[]{:S(2)}, u32[]{:S(2)}) collective-permute-start(bf16[256,256]{1,0:T(8,128)(2,1)S(1)} %collective-permute-done.27.refs_12_), channel_id=1, source_target_pairs={{0,56},{8,0},{16,8},{24,16},{32,24},{40,32},{48,40},{56,48},{1,57}... | collective-permute-start | bytes 393224 | tf_op jit(solution)/shard_map/gather_preconditioned/ppermute | solution.py:202
  71.7 10.9 %collective-permute-start.30 = (bf16[256,4096]{1,0:T(8,128)(2,1)S(1)}, bf16[256,4096]{1,0:T(8,128)(2,1)S(1)}, u32[]{:S(2)}, u32[]{:S(2)}) collective-permute-start(bf16[256,4096]{1,0:T(8,128)(2,1)S(1)} %bitcast.8), channel_id=1, source_target_pairs={{0,1},{1,0},{2,3},{3,2},{4,5},{5,4},{6,7},{7,6},{8,9},{9,8},{10,11... | collective-permute-start | bytes 6291464 | tf_op jit(solution)/shard_map/swap_stored/ppermute | solution.py:210
  76.8 6.8 %collective-permute-start.35 = (bf16[256,4096]{1,0:T(8,128)(2,1)S(1)}, bf16[256,4096]{1,0:T(8,128)(2,1)S(1)}, u32[]{:S(2)}, u32[]{:S(2)}) collective-permute-start(bf16[256,4096]{1,0:T(8,128)(2,1)S(1)} %collective-permute-done.31.refs_15_.refs_7_), channel_id=1, source_target_pairs={{0,1},{1,0},{2,3},{3,2},{4,5},{5,4},{6,7},{7,6},{8,9},{9,8},{10,11... | collective-permute-start | bytes 6291464 | tf_op jit(solution)/shard_map/swap_stored/ppermute | solution.py:210
  79.7 6.8 %collective-permute-start.21 = (bf16[256,256]{1,0:T(8,128)(2,1)S(1)}, bf16[256,256]{1,0:T(8,128)(2,1)S(1)}, u32[]{:S(2)}, u32[]{:S(2)}) collective-permute-start(bf16[256,256]{1,0:T(8,128)(2,1)S(1)} %collective-permute-done.20.refs_6_), channel_id=1, source_target_pairs={{0,8},{8,16},{16,24},{24,32},{32,40},{40,48},{48,56},{56,0},{1,9},... | collective-permute-start | bytes 393224 | tf_op jit(solution)/shard_map/gather_preconditioned/ppermute | solution.py:202
  79.7 6.8 %collective-permute-start.29 = (bf16[256,256]{1,0:T(8,128)(2,1)S(1)}, bf16[256,256]{1,0:T(8,128)(2,1)S(1)}, u32[]{:S(2)}, u32[]{:S(2)}) collective-permute-start(bf16[256,256]{1,0:T(8,128)(2,1)S(1)} %collective-permute-done.28.refs_3_), channel_id=1, source_target_pairs={{0,56},{8,0},{16,8},{24,16},{32,24},{40,32},{48,40},{56,48},{1,57}... | collective-permute-start | bytes 393224 | tf_op jit(solution)/shard_map/gather_preconditioned/ppermute | solution.py:202
  88.0 5.8 %collective-permute-start.36 = (bf16[64,1024]{1,0:T(8,128)(2,1)S(1)}, bf16[64,1024]{1,0:T(8,128)(2,1)S(1)}, u32[]{:S(2)}, u32[]{:S(2)}) collective-permute-start(bf16[64,1024]{1,0:T(8,128)(2,1)S(1)} %get-tuple-element.28), channel_id=1, source_target_pairs={{0,64},{64,128},{128,192},{192,0},{1,65},{65,129},{129,193},{193,1... | collective-permute-start | bytes 393224 | tf_op jit(solution)/shard_map/sum_layers/ppermute | solution.py:202
  89.3 8.3 %collective-permute-start.37 = (bf16[64,1024]{1,0:T(8,128)(2,1)S(1)}, bf16[64,1024]{1,0:T(8,128)(2,1)S(1)}, u32[]{:S(2)}, u32[]{:S(2)}) collective-permute-start(bf16[64,1024]{1,0:T(8,128)(2,1)S(1)} %get-tuple-element.29), channel_id=1, source_target_pairs={{0,128},{64,192},{128,0},{192,64},{1,129},{65,193},{129,1},{193,65... | collective-permute-start | bytes 393224 | tf_op jit(solution)/shard_map/sum_layers/ppermute | solution.py:202
  91.8 5.8 %collective-permute-start.38 = (bf16[64,1024]{1,0:T(8,128)(2,1)S(1)}, bf16[64,1024]{1,0:T(8,128)(2,1)S(1)}, u32[]{:S(2)}, u32[]{:S(2)}) collective-permute-start(bf16[64,1024]{1,0:T(8,128)(2,1)S(1)} %get-tuple-element.30), channel_id=1, source_target_pairs={{0,192},{64,0},{128,64},{192,128},{1,193},{65,1},{129,65},{193,129... | collective-permute-start | bytes 393224 | tf_op jit(solution)/shard_map/sum_layers/ppermute | solution.py:202
  97.7 4.5 %collective-permute-start.39 = (bf16[64,256]{1,0:T(8,128)(2,1)S(1)}, bf16[64,256]{1,0:T(8,128)(2,1)S(1)}, u32[]{:S(2)}, u32[]{:S(2)}) collective-permute-start(bf16[64,256]{1,0:T(8,128)(2,1)S(1)} %get-tuple-element.32), channel_id=1, source_target_pairs={{0,1},{1,0},{2,3},{3,2},{4,5},{5,4},{6,7},{7,6},{8,9},{9,8},{10,11... | collective-permute-start | bytes 98312 | tf_op jit(solution)/shard_map/exchange_examples/ppermute | solution.py:281
  99.2 4.0 %collective-permute-start.40 = (bf16[64,256]{1,0:T(8,128)(2,1)S(1)}, bf16[64,256]{1,0:T(8,128)(2,1)S(1)}, u32[]{:S(2)}, u32[]{:S(2)}) collective-permute-start(bf16[64,256]{1,0:T(8,128)(2,1)S(1)} %get-tuple-element.33), channel_id=1, source_target_pairs={{0,6},{1,7},{2,4},{3,5},{4,2},{5,3},{6,0},{7,1},{8,14},{9,15},{10,... | collective-permute-start | bytes 98312 | tf_op jit(solution)/shard_map/exchange_examples/ppermute | solution.py:281
  101.4 4.6 %collective-permute-start.41 = (bf16[64,256]{1,0:T(8,128)(2,1)S(1)}, bf16[64,256]{1,0:T(8,128)(2,1)S(1)}, u32[]{:S(2)}, u32[]{:S(2)}) collective-permute-start(bf16[64,256]{1,0:T(8,128)(2,1)S(1)} %get-tuple-element.34), channel_id=1, source_target_pairs={{0,7},{1,6},{2,5},{3,4},{4,3},{5,2},{6,1},{7,0},{8,15},{9,14},{10,... | collective-permute-start | bytes 98312 | tf_op jit(solution)/shard_map/exchange_examples/ppermute | solution.py:281

commit v4 on v3

--- a/solution.py
+++ b/solution.py
@@ -251,7 +251,7 @@
     with jax.named_scope("swap_inverse"):
         core_rows = swap_core(inverse_rows)
         chip_rows = swap_chip(inverse_rows, (0, 3), (1, 2))
-        both_rows = swap_core(after(chip_rows, some(pieces, (2, 0), (-2, 0), (2, 1), (-2, 1))))
+        both_rows = swap_core(after(chip_rows, some(pieces, (3, 0), (-3, 0), (3, 1), (-3, 1))))
     with jax.named_scope("swap_stored"):
         chip_stored = swap_chip(after(stored_rows, some(pieces, (1, 0), (-1, 0), (0, 1))), (0, 3), (1, 2))
     with jax.named_scope("split_inverse"):

time: 107 us -> 106 us (level)
  starting transfers between devices: 67.1 us -> 65.8 us
    ppermute x31, starting transfers between devices: 42.5 us -> 41.3 us  [shift(): lax.ppermute(value, axis, [(i, (i + by) % size) for i in range(size)])]
  transfers between devices with their start and end apart: 42 -> 42, of which waited for: 15 -> 16; matrix products, arithmetic and copies ran while one was open for 1% -> 1% of each run, Pallas kernels for 7% -> 7%
where the time goes in v4:
time: 106 us
  starting transfers between devices  65.8 us (62%)
  waiting for transfers between devices  24.3 us (23%)
  Pallas kernels  10.5 us (10%)
  local copies, waits for them, and re-layouts  4.16 us (4%)
    ppermute x31, starting transfers between devices, shift(): lax.ppermute(value, axis, [(i, (i + by) % size) for i in range(size)])  41.3 us
    ppermute x31, waiting for transfers between devices, shift(): lax.ppermute(value, axis, [(i, (i + by) % size) for i in range(size)])  18.4 us
    ppermute x4, starting transfers between devices, swap_core(): return lax.ppermute(value, 'core', [(0, 1), (1, 0)])  15.4 us
    ppermute x4, starting transfers between devices, swap_chip(): lax.ppermute(value, 'y', [pair for a, b in pairs for pair in ((a, b), (b,...  4.57 us
    ppermute x3, starting transfers between devices, per_device(): lax.ppermute(parts[k], ('y', 'core'), pairs[k - 1])  4.47 us
    pallas_call x2, Pallas kernels, score(): pl.pallas_call(lambda *refs: score_kernel(some, len(stored), before is No...  4.04 us
    unnamed x8, local copies, waits for them, and re-layouts  3.47 us
    ppermute x3, waiting for transfers between devices, per_device(): lax.ppermute(parts[k], ('y', 'core'), pairs[k - 1])  3.44 us
  transfers between devices with their start and end apart: 42, of which 16 were waited for; matrix products, arithmetic and copies ran while one was open for 1% of the time, Pallas kernels for 7%

profile of v4, /device:TPU:1, one launch (start us, length us, event | category | flops | bytes accessed | tf_op | source)
XLA Modules:
  0.0 105.7 jit_solution(17592610102969585525)
XLA Ops:
  0.0 3.6 %collective-permute-start.16 = (f32[64,4096]{1,0:T(8,128)}, f32[64,4096]{1,0:T(8,128)S(1)}, u32[]{:S(2)}, u32[]{:S(2)}) collective-permute-start(f32[64,4096]{1,0:T(8,128)} %bitcast.12), channel_id=1, source_target_pairs={{0,6},{6,0},{2,4},{4,2},{1,7},{7,1},{3,5},{5,3},{8,14},{14,8},{10,... | collective-permute-start | bytes 3145736 | tf_op jit(solution)/shard_map/swap_inverse/ppermute | solution.py:245
  3.7 0.1 xor.12
  3.8 0.7 broadcast_multiply_fusion
  4.8 1.6 %copy-done.1 = bf16[1,16,512,128]{3,2,1,0:T(8,128)(2,1)S(1)} copy-done((bf16[1,16,512,128]{3,2,1,0:T(8,128)(2,1)S(1)}, bf16[1,16,512,128]{3,2,1,0:T(8,128)(2,1)}, u32[]{:S(2)}) %copy-start.1) | copy-done | bytes 2097176
  6.4 0.7 copy-done.3
  7.1 2.1 %form_gradients.1 = bf16[16,64,64]{2,1,0:T(8,128)(2,1)S(1)} custom-call(s32[16]{0:T(128)S(1)} %copy-done.3, bf16[16,512,128]{2,1,0:T(8,128)(2,1)S(1)} %bitcast.11), custom_call_target="tpu_custom_call" | custom-call | flops 268435456 | bytes 2097152 | tf_op jit(solution)/shard_map/gradients/form_gradients/pallas_call | solution.py:41
  9.2 0.3 reshape.12.refs_1_
  9.5 0.1 collective-permute-start.7
  9.6 1.7 %collective-permute-start = (bf16[16,4096]{1,0:T(8,128)(2,1)S(1)}, bf16[16,4096]{1,0:T(8,128)(2,1)S(1)}, u32[]{:S(2)}, u32[]{:S(2)}) collective-permute-start(bf16[16,4096]{1,0:T(8,128)(2,1)S(1)} %reshape.12.refs_1_), channel_id=1, source_target_pairs={{0,8},{8,16},{16,24},{24,32},{32,40},{40,48},{48,56},{56,0},{1,9},... | collective-permute-start | bytes 393224 | tf_op jit(solution)/shard_map/gather_projected/ppermute | solution.py:202
  11.3 4.0 %collective-permute-start.1 = (bf16[16,4096]{1,0:T(8,128)(2,1)S(1)}, bf16[16,4096]{1,0:T(8,128)(2,1)S(1)}, u32[]{:S(2)}, u32[]{:S(2)}) collective-permute-start(bf16[16,4096]{1,0:T(8,128)(2,1)S(1)} %reshape.12.refs_1_), channel_id=1, source_target_pairs={{0,56},{8,0},{16,8},{24,16},{32,24},{40,32},{48,40},{56,48},{1,57}... | collective-permute-start | bytes 393224 | tf_op jit(solution)/shard_map/gather_projected/ppermute | solution.py:202
  15.3 2.8 %collective-permute-done.refs_2_ = bf16[16,4096]{1,0:T(8,128)(2,1)S(1)} collective-permute-done((bf16[16,4096]{1,0:T(8,128)(2,1)S(1)}, bf16[16,4096]{1,0:T(8,128)(2,1)S(1)}, u32[]{:S(2)}, u32[]{:S(2)}) %collective-permute-start) | collective-permute-done | bytes 131104 | tf_op jit(solution)/shard_map/gather_projected/ppermute | solution.py:202
  18.1 0.7 collective-permute-start.31
  18.8 2.5 %collective-permute-start.9 = (bf16[16,4096]{1,0:T(8,128)(2,1)S(1)}, bf16[16,4096]{1,0:T(8,128)(2,1)S(1)}, u32[]{:S(2)}, u32[]{:S(2)}) collective-permute-start(bf16[16,4096]{1,0:T(8,128)(2,1)S(1)} %collective-permute-done.7.refs_9_), channel_id=1, source_target_pairs={{0,56},{8,0},{16,8},{24,16},{32,24},{40,32},{48,40},{56,48},{1,57}... | collective-permute-start | bytes 393224 | tf_op jit(solution)/shard_map/gather_projected/ppermute | solution.py:202
  21.3 0.6 collective-permute-done.8.refs_10_
  21.9 2.1 %collective-permute-start.3 = (bf16[16,4096]{1,0:T(8,128)(2,1)S(1)}, bf16[16,4096]{1,0:T(8,128)(2,1)S(1)}, u32[]{:S(2)}, u32[]{:S(2)}) collective-permute-start(bf16[16,4096]{1,0:T(8,128)(2,1)S(1)} %collective-permute-done.1.refs_3_), channel_id=1, source_target_pairs={{0,56},{8,0},{16,8},{24,16},{32,24},{40,32},{48,40},{56,48},{1,57}... | collective-permute-start | bytes 393224 | tf_op jit(solution)/shard_map/gather_projected/ppermute | solution.py:202
  24.0 2.6 %collective-permute-done.2.refs_4_ = bf16[16,4096]{1,0:T(8,128)(2,1)S(1)} collective-permute-done((bf16[16,4096]{1,0:T(8,128)(2,1)S(1)}, bf16[16,4096]{1,0:T(8,128)(2,1)S(1)}, u32[]{:S(2)}, u32[]{:S(2)}) %collective-permute-start.2) | collective-permute-done | bytes 131104 | tf_op jit(solution)/shard_map/gather_projected/ppermute | solution.py:202
  26.6 0.4 collective-permute-start.11
  27.0 0.3 collective-permute-done.3.refs_5_
  27.3 0.8 collective-permute-start.4
  28.1 2.4 %collective-permute-done.10.refs_12_ = bf16[16,4096]{1,0:T(8,128)(2,1)S(1)} collective-permute-done((bf16[16,4096]{1,0:T(8,128)(2,1)S(1)}, bf16[16,4096]{1,0:T(8,128)(2,1)S(1)}, u32[]{:S(2)}, u32[]{:S(2)}) %collective-permute-start.10) | collective-permute-done | bytes 131104 | tf_op jit(solution)/shard_map/gather_projected/ppermute | solution.py:202
  30.5 0.3 collective-permute-start.5
  30.7 1.2 %collective-permute-start.12 = (bf16[16,4096]{1,0:T(8,128)(2,1)S(1)}, bf16[16,4096]{1,0:T(8,128)(2,1)S(1)}, u32[]{:S(2)}, u32[]{:S(2)}) collective-permute-start(bf16[16,4096]{1,0:T(8,128)(2,1)S(1)} %collective-permute-done.10.refs_12_), channel_id=1, source_target_pairs={{0,8},{8,16},{16,24},{24,32},{32,40},{40,48},{48,56},{56,0},{1,9},... | collective-permute-start | bytes 393224 | tf_op jit(solution)/shard_map/gather_projected/ppermute | solution.py:202
  32.0 2.3 %collective-permute-done.4.refs_6_ = bf16[16,4096]{1,0:T(8,128)(2,1)S(1)} collective-permute-done((bf16[16,4096]{1,0:T(8,128)(2,1)S(1)}, bf16[16,4096]{1,0:T(8,128)(2,1)S(1)}, u32[]{:S(2)}, u32[]{:S(2)}) %collective-permute-start.4) | collective-permute-done | bytes 131104 | tf_op jit(solution)/shard_map/gather_projected/ppermute | solution.py:202
  34.3 1.1 %collective-permute-start.13 = (bf16[16,4096]{1,0:T(8,128)(2,1)S(1)}, bf16[16,4096]{1,0:T(8,128)(2,1)S(1)}, u32[]{:S(2)}, u32[]{:S(2)}) collective-permute-start(bf16[16,4096]{1,0:T(8,128)(2,1)S(1)} %collective-permute-done.11.refs_13_), channel_id=1, source_target_pairs={{0,56},{8,0},{16,8},{24,16},{32,24},{40,32},{48,40},{56,48},{1,57}... | collective-permute-start | bytes 393224 | tf_op jit(solution)/shard_map/gather_projected/ppermute | solution.py:202
  35.4 5.1 %collective-permute-start.15 = (f32[64,4096]{1,0:T(8,128)}, f32[64,4096]{1,0:T(8,128)S(1)}, u32[]{:S(2)}, u32[]{:S(2)}) collective-permute-start(f32[64,4096]{1,0:T(8,128)} %bitcast.13), channel_id=1, source_target_pairs={{0,1},{1,0},{2,3},{3,2},{4,5},{5,4},{6,7},{7,6},{8,9},{9,8},{10,11... | collective-permute-start | bytes 3145736 | tf_op jit(solution)/shard_map/swap_inverse/ppermute | solution.py:210
  40.5 2.9 %collective-permute-start.17 = (f32[64,4096]{1,0:T(8,128)S(1)}, f32[64,4096]{1,0:T(8,128)S(1)}, u32[]{:S(2)}, u32[]{:S(2)}) collective-permute-start(f32[64,4096]{1,0:T(8,128)S(1)} %collective-permute-done.16.chip_ref), channel_id=1, source_target_pairs={{0,1},{1,0},{2,3},{3,2},{4,5},{5,4},{6,7},{7,6},{8,9},{9,8},{10,11... | collective-permute-start | bytes 3145736 | tf_op jit(solution)/shard_map/swap_inverse/ppermute | solution.py:210
  43.5 0.4 collective-permute-start.6
  43.9 2.6 %collective-permute-start.14 = (bf16[16,4096]{1,0:T(8,128)(2,1)S(1)}, bf16[16,4096]{1,0:T(8,128)(2,1)S(1)}, u32[]{:S(2)}, u32[]{:S(2)}) collective-permute-start(bf16[16,4096]{1,0:T(8,128)(2,1)S(1)} %collective-permute-done.13.refs_15_), channel_id=1, source_target_pairs={{0,56},{8,0},{16,8},{24,16},{32,24},{40,32},{48,40},{56,48},{1,57}... | collective-permute-start | bytes 393224 | tf_op jit(solution)/shard_map/gather_projected/ppermute | solution.py:202
  46.5 1.2 %copy-done.2 = f32[1,64,4096]{2,1,0:T(8,128)S(1)} copy-done((f32[1,64,4096]{2,1,0:T(8,128)S(1)}, f32[1,64,4096]{2,1,0:T(8,128)}, u32[]{:S(2)}) %copy-start.2) | copy-done | bytes 1048600
  47.7 1.2 %split_inverse.1 = (bf16[256,4096]{1,0:T(8,128)(2,1)S(1)}, bf16[256,4096]{1,0:T(8,128)(2,1)S(1)}) custom-call(s32[50]{0:T(128)S(1)} %concatenate.3.where_ref.refs_0_, f32[64,4096]{1,0:T(8,128)S(1)} %bitcast.14, f32[64,4096]{1,0:T(8,128)S(1)} %collective-permute-done.15.core_ref, f32[64,4096]{1,0:T(8,128)S(1)} %collective-permute-done.16.chip_ref, ...), custom_call_target="tpu_custom_call" | custom-call | flops 2097152 | bytes 8388608 | tf_op jit(solution)/shard_map/split_inverse/split_inverse/pallas_call | solution.py:71
  48.9 1.3 %collective-permute-done.6.refs_8_ = bf16[16,4096]{1,0:T(8,128)(2,1)S(1)} collective-permute-done((bf16[16,4096]{1,0:T(8,128)(2,1)S(1)}, bf16[16,4096]{1,0:T(8,128)(2,1)S(1)}, u32[]{:S(2)}, u32[]{:S(2)}) %collective-permute-start.6) | collective-permute-done | bytes 131104 | tf_op jit(solution)/shard_map/gather_projected/ppermute | solution.py:202
  50.2 1.8 %precondition.1.refs_1_ = bf16[256,256]{1,0:T(8,128)(2,1)S(1)} custom-call(s32[50]{0:T(128)S(1)} %concatenate.3.where_ref.refs_0_, bf16[16,4096]{1,0:T(8,128)(2,1)S(1)} %reshape.12.refs_1_, bf16[16,4096]{1,0:T(8,128)(2,1)S(1)} %collective-permute-done.refs_2_, bf16[16,4096]{1,0:T(8,128)(2,1)S(1)} %collective-permute-done.1.refs_3_, ...), custom_call_target="tpu_custom_call" | custom-call | flops 1073741824 | bytes 6291456 | tf_op jit(solution)/shard_map/precondition/precondition/pallas_call | solution.py:97
  52.0 0.2 collective-permute-start.22
  52.3 2.0 %collective-permute-start.18 = (bf16[256,256]{1,0:T(8,128)(2,1)S(1)}, bf16[256,256]{1,0:T(8,128)(2,1)S(1)}, u32[]{:S(2)}, u32[]{:S(2)}) collective-permute-start(bf16[256,256]{1,0:T(8,128)(2,1)S(1)} %precondition.1.refs_1_), channel_id=1, source_target_pairs={{0,8},{8,16},{16,24},{24,32},{32,40},{40,48},{48,56},{56,0},{1,9},... | collective-permute-start | bytes 393224 | tf_op jit(solution)/shard_map/gather_preconditioned/ppermute | solution.py:202
  54.3 0.6 collective-permute-start.32
  54.9 1.6 %collective-permute-done.22.refs_8_ = bf16[256,256]{1,0:T(8,128)(2,1)S(1)} collective-permute-done((bf16[256,256]{1,0:T(8,128)(2,1)S(1)}, bf16[256,256]{1,0:T(8,128)(2,1)S(1)}, u32[]{:S(2)}, u32[]{:S(2)}) %collective-permute-start.22) | collective-permute-done | bytes 131104 | tf_op jit(solution)/shard_map/gather_preconditioned/ppermute | solution.py:245
  56.5 1.7 %collective-permute-start.23 = (bf16[256,256]{1,0:T(8,128)(2,1)S(1)}, bf16[256,256]{1,0:T(8,128)(2,1)S(1)}, u32[]{:S(2)}, u32[]{:S(2)}) collective-permute-start(bf16[256,256]{1,0:T(8,128)(2,1)S(1)} %collective-permute-done.22.refs_8_), channel_id=1, source_target_pairs={{0,8},{8,16},{16,24},{24,32},{32,40},{40,48},{48,56},{56,0},{1,9},... | collective-permute-start | bytes 393224 | tf_op jit(solution)/shard_map/gather_preconditioned/ppermute | solution.py:202
  58.2 1.0 collective-permute-start.26
  59.2 0.5 collective-permute-start.19
  59.6 2.2 %collective-permute-start.33 = (bf16[256,256]{1,0:T(8,128)(2,1)S(1)}, bf16[256,256]{1,0:T(8,128)(2,1)S(1)}, u32[]{:S(2)}, u32[]{:S(2)}) collective-permute-start(bf16[256,256]{1,0:T(8,128)(2,1)S(1)} %collective-permute-done.32.refs_3_), channel_id=1, source_target_pairs={{0,56},{8,0},{16,8},{24,16},{32,24},{40,32},{48,40},{56,48},{1,57}... | collective-permute-start | bytes 393224 | tf_op jit(solution)/shard_map/gather_preconditioned/ppermute | solution.py:202
  61.9 0.4 collective-permute-start.24
  62.3 2.3 %collective-permute-start.27 = (bf16[256,256]{1,0:T(8,128)(2,1)S(1)}, bf16[256,256]{1,0:T(8,128)(2,1)S(1)}, u32[]{:S(2)}, u32[]{:S(2)}) collective-permute-start(bf16[256,256]{1,0:T(8,128)(2,1)S(1)} %collective-permute-done.26.refs_10_), channel_id=1, source_target_pairs={{0,56},{8,0},{16,8},{24,16},{32,24},{40,32},{48,40},{56,48},{1,57}... | collective-permute-start | bytes 393224 | tf_op jit(solution)/shard_map/gather_preconditioned/ppermute | solution.py:202
  64.6 0.7 collective-permute-done.19.refs_4_
  65.2 3.0 %collective-permute-start.34 = (bf16[256,256]{1,0:T(8,128)(2,1)S(1)}, bf16[256,256]{1,0:T(8,128)(2,1)S(1)}, u32[]{:S(2)}, u32[]{:S(2)}) collective-permute-start(bf16[256,256]{1,0:T(8,128)(2,1)S(1)} %collective-permute-done.33.refs_5_), channel_id=1, source_target_pairs={{0,56},{8,0},{16,8},{24,16},{32,24},{40,32},{48,40},{56,48},{1,57}... | collective-permute-start | bytes 393224 | tf_op jit(solution)/shard_map/gather_preconditioned/ppermute | solution.py:202
  68.2 0.3 collective-permute-done.24.refs_11_
  68.5 2.7 %collective-permute-start.28 = (bf16[256,256]{1,0:T(8,128)(2,1)S(1)}, bf16[256,256]{1,0:T(8,128)(2,1)S(1)}, u32[]{:S(2)}, u32[]{:S(2)}) collective-permute-start(bf16[256,256]{1,0:T(8,128)(2,1)S(1)} %collective-permute-done.27.refs_12_), channel_id=1, source_target_pairs={{0,56},{8,0},{16,8},{24,16},{32,24},{40,32},{48,40},{56,48},{1,57}... | collective-permute-start | bytes 393224 | tf_op jit(solution)/shard_map/gather_preconditioned/ppermute | solution.py:202
  71.2 4.4 %collective-permute-start.30 = (bf16[256,4096]{1,0:T(8,128)(2,1)S(1)}, bf16[256,4096]{1,0:T(8,128)(2,1)S(1)}, u32[]{:S(2)}, u32[]{:S(2)}) collective-permute-start(bf16[256,4096]{1,0:T(8,128)(2,1)S(1)} %bitcast.8), channel_id=1, source_target_pairs={{0,1},{1,0},{2,3},{3,2},{4,5},{5,4},{6,7},{7,6},{8,9},{9,8},{10,11... | collective-permute-start | bytes 6291464 | tf_op jit(solution)/shard_map/swap_stored/ppermute | solution.py:210
  75.6 2.9 %collective-permute-start.35 = (bf16[256,4096]{1,0:T(8,128)(2,1)S(1)}, bf16[256,4096]{1,0:T(8,128)(2,1)S(1)}, u32[]{:S(2)}, u32[]{:S(2)}) collective-permute-start(bf16[256,4096]{1,0:T(8,128)(2,1)S(1)} %collective-permute-done.31.refs_15_.refs_7_), channel_id=1, source_target_pairs={{0,1},{1,0},{2,3},{3,2},{4,5},{5,4},{6,7},{7,6},{8,9},{9,8},{10,11... | collective-permute-start | bytes 6291464 | tf_op jit(solution)/shard_map/swap_stored/ppermute | solution.py:210
  78.5 3.0 %collective-permute-start.29 = (bf16[256,256]{1,0:T(8,128)(2,1)S(1)}, bf16[256,256]{1,0:T(8,128)(2,1)S(1)}, u32[]{:S(2)}, u32[]{:S(2)}) collective-permute-start(bf16[256,256]{1,0:T(8,128)(2,1)S(1)} %collective-permute-done.28.refs_3_), channel_id=1, source_target_pairs={{0,56},{8,0},{16,8},{24,16},{32,24},{40,32},{48,40},{56,48},{1,57}... | collective-permute-start | bytes 393224 | tf_op jit(solution)/shard_map/gather_preconditioned/ppermute | solution.py:202
  81.5 0.9 collective-permute-done.35.refs_16_.refs_8_
  82.4 2.5 %score.2.refs_9_ = f32[256,1024]{1,0:T(8,128)S(1)} custom-call(s32[50]{0:T(128)S(1)} %concatenate.3.where_ref.refs_0_, bf16[256,256]{1,0:T(8,128)(2,1)S(1)} %precondition.1.refs_1_, bf16[256,256]{1,0:T(8,128)(2,1)S(1)} %collective-permute-done.18.refs_2_, bf16[256,256]{1,0:T(8,128)(2,1)S(1)} %collective-permute-done.32.refs_3_, ...), custom_call_target="tpu_custom_call" | custom-call | flops 1610612736 | bytes 7864320 | tf_op jit(solution)/shard_map/score/score/pallas_call | solution.py:144
  84.9 0.4 collective-permute-done.21.refs_1_
  85.4 1.5 %score.3 = (f32[64,1024]{1,0:T(8,128)S(1)}, bf16[64,1024]{1,0:T(8,128)(2,1)S(1)}, bf16[64,1024]{1,0:T(8,128)(2,1)S(1)}, bf16[64,1024]{1,0:T(8,128)(2,1)S(1)}) custom-call(s32[50]{0:T(128)S(1)} %concatenate.3.where_ref.refs_0_, bf16[256,256]{1,0:T(8,128)(2,1)S(1)} %collective-permute-done.21.refs_1_, bf16[256,256]{1,0:T(8,128)(2,1)S(1)} %collective-permute-done.25.refs_2_, ...), custom_call_target="tpu_custom_call" | custom-call | flops 536870912 | bytes 2621440 | tf_op jit(solution)/shard_map/score/score/pallas_call | solution.py:144
  86.9 1.3 %collective-permute-start.36 = (bf16[64,1024]{1,0:T(8,128)(2,1)S(1)}, bf16[64,1024]{1,0:T(8,128)(2,1)S(1)}, u32[]{:S(2)}, u32[]{:S(2)}) collective-permute-start(bf16[64,1024]{1,0:T(8,128)(2,1)S(1)} %get-tuple-element.28), channel_id=1, source_target_pairs={{0,64},{64,128},{128,192},{192,0},{1,65},{65,129},{129,193},{193,1... | collective-permute-start | bytes 393224 | tf_op jit(solution)/shard_map/sum_layers/ppermute | solution.py:202
  88.2 2.5 %collective-permute-start.37 = (bf16[64,1024]{1,0:T(8,128)(2,1)S(1)}, bf16[64,1024]{1,0:T(8,128)(2,1)S(1)}, u32[]{:S(2)}, u32[]{:S(2)}) collective-permute-start(bf16[64,1024]{1,0:T(8,128)(2,1)S(1)} %get-tuple-element.29), channel_id=1, source_target_pairs={{0,128},{64,192},{128,0},{192,64},{1,129},{65,193},{129,1},{193,65... | collective-permute-start | bytes 393224 | tf_op jit(solution)/shard_map/sum_layers/ppermute | solution.py:202
  90.6 1.2 %collective-permute-start.38 = (bf16[64,1024]{1,0:T(8,128)(2,1)S(1)}, bf16[64,1024]{1,0:T(8,128)(2,1)S(1)}, u32[]{:S(2)}, u32[]{:S(2)}) collective-permute-start(bf16[64,1024]{1,0:T(8,128)(2,1)S(1)} %get-tuple-element.30), channel_id=1, source_target_pairs={{0,192},{64,0},{128,64},{192,128},{1,193},{65,1},{129,65},{193,129... | collective-permute-start | bytes 393224 | tf_op jit(solution)/shard_map/sum_layers/ppermute | solution.py:202
  91.8 0.9 collective-permute-done.36.a_ref
  92.6 3.8 %collective-permute-done.37.b_ref = bf16[64,1024]{1,0:T(8,128)(2,1)S(1)} collective-permute-done((bf16[64,1024]{1,0:T(8,128)(2,1)S(1)}, bf16[64,1024]{1,0:T(8,128)(2,1)S(1)}, u32[]{:S(2)}, u32[]{:S(2)}) %collective-permute-start.37) | collective-permute-done | bytes 131104 | tf_op jit(solution)/shard_map/sum_layers/ppermute | solution.py:202
  96.5 1.5 %collective-permute-start.39 = (bf16[64,256]{1,0:T(8,128)(2,1)S(1)}, bf16[64,256]{1,0:T(8,128)(2,1)S(1)}, u32[]{:S(2)}, u32[]{:S(2)}) collective-permute-start(bf16[64,256]{1,0:T(8,128)(2,1)S(1)} %get-tuple-element.32), channel_id=1, source_target_pairs={{0,1},{1,0},{2,3},{3,2},{4,5},{5,4},{6,7},{7,6},{8,9},{9,8},{10,11... | collective-permute-start | bytes 98312 | tf_op jit(solution)/shard_map/exchange_examples/ppermute | solution.py:281
  98.0 1.8 %collective-permute-start.40 = (bf16[64,256]{1,0:T(8,128)(2,1)S(1)}, bf16[64,256]{1,0:T(8,128)(2,1)S(1)}, u32[]{:S(2)}, u32[]{:S(2)}) collective-permute-start(bf16[64,256]{1,0:T(8,128)(2,1)S(1)} %get-tuple-element.33), channel_id=1, source_target_pairs={{0,6},{1,7},{2,4},{3,5},{4,2},{5,3},{6,0},{7,1},{8,14},{9,15},{10,... | collective-permute-start | bytes 98312 | tf_op jit(solution)/shard_map/exchange_examples/ppermute | solution.py:281
  99.8 1.1 %collective-permute-start.41 = (bf16[64,256]{1,0:T(8,128)(2,1)S(1)}, bf16[64,256]{1,0:T(8,128)(2,1)S(1)}, u32[]{:S(2)}, u32[]{:S(2)}) collective-permute-start(bf16[64,256]{1,0:T(8,128)(2,1)S(1)} %get-tuple-element.34), channel_id=1, source_target_pairs={{0,7},{1,6},{2,5},{3,4},{4,3},{5,2},{6,1},{7,0},{8,15},{9,14},{10,... | collective-permute-start | bytes 98312 | tf_op jit(solution)/shard_map/exchange_examples/ppermute | solution.py:281
  101.0 1.0 collective-permute-done.40.refs_2_
  102.0 2.4 %collective-permute-done.41.refs_3_ = bf16[64,256]{1,0:T(8,128)(2,1)S(1)} collective-permute-done((bf16[64,256]{1,0:T(8,128)(2,1)S(1)}, bf16[64,256]{1,0:T(8,128)(2,1)S(1)}, u32[]{:S(2)}, u32[]{:S(2)}) %collective-permute-start.41) | collective-permute-done | bytes 32800 | tf_op jit(solution)/shard_map/exchange_examples/ppermute | solution.py:281
  104.4 1.3 %place_parts.1 = f32[256,256]{1,0:T(8,128)} custom-call(s32[50]{0:T(128)S(1)} %concatenate.3.where_ref.refs_0_, f32[64,256]{1,0:T(8,128)S(1)} %get-tuple-element.31.refs_0_, bf16[64,256]{1,0:T(8,128)(2,1)S(1)} %collective-permute-done.39.refs_1_, bf16[64,256]{1,0:T(8,128)(2,1)S(1)} %collective-permute-done.40.refs_2_, ...), custom_call_target="tpu_custom_call" | custom-call | flops 65536 | bytes 524288 | tf_op jit(solution)/shard_map/exchange_examples/place_parts/pallas_call | solution.py:190
  (47 shorter events, 0.7 us)
Async XLA Ops:
  0.0 18.1 %copy-start = (bf16[1,256,4096]{2,1,0:T(8,128)(2,1)S(1)}, bf16[1,256,4096]{2,1,0:T(8,128)(2,1)}, u32[]{:S(2)}) copy-start(bf16[1,256,4096]{2,1,0:T(8,128)(2,1)} %param.8) | copy-start | bytes 6291460
  0.0 40.5 %collective-permute-start.16 = (f32[64,4096]{1,0:T(8,128)}, f32[64,4096]{1,0:T(8,128)S(1)}, u32[]{:S(2)}, u32[]{:S(2)}) collective-permute-start(f32[64,4096]{1,0:T(8,128)} %bitcast.12), channel_id=1, source_target_pairs={{0,6},{6,0},{2,4},{4,2},{1,7},{7,1},{3,5},{5,3},{8,14},{14,8},{10,... | collective-permute-start | bytes 3145736 | tf_op jit(solution)/shard_map/swap_inverse/ppermute | solution.py:245
  4.8 1.6 %copy-start.1 = (bf16[1,16,512,128]{3,2,1,0:T(8,128)(2,1)S(1)}, bf16[1,16,512,128]{3,2,1,0:T(8,128)(2,1)}, u32[]{:S(2)}) copy-start(bf16[1,16,512,128]{3,2,1,0:T(8,128)(2,1)} %param.5) | copy-start | bytes 6291460
  6.4 0.7 copy-start.3
  9.5 5.8 %collective-permute-start.7 = (bf16[16,4096]{1,0:T(8,128)(2,1)S(1)}, bf16[16,4096]{1,0:T(8,128)(2,1)S(1)}, u32[]{:S(2)}, u32[]{:S(2)}) collective-permute-start(bf16[16,4096]{1,0:T(8,128)(2,1)S(1)} %reshape.12.refs_1_), channel_id=1, source_target_pairs={{0,2},{2,0},{4,6},{6,4},{1,3},{3,1},{5,7},{7,5},{8,10},{10,8},{12,... | collective-permute-start | bytes 393224 | tf_op jit(solution)/shard_map/gather_projected/ppermute | solution.py:245
  9.6 8.5 %collective-permute-start = (bf16[16,4096]{1,0:T(8,128)(2,1)S(1)}, bf16[16,4096]{1,0:T(8,128)(2,1)S(1)}, u32[]{:S(2)}, u32[]{:S(2)}) collective-permute-start(bf16[16,4096]{1,0:T(8,128)(2,1)S(1)} %reshape.12.refs_1_), channel_id=1, source_target_pairs={{0,8},{8,16},{16,24},{24,32},{32,40},{40,48},{48,56},{56,0},{1,9},... | collective-permute-start | bytes 393224 | tf_op jit(solution)/shard_map/gather_projected/ppermute | solution.py:202
  11.3 6.8 %collective-permute-start.1 = (bf16[16,4096]{1,0:T(8,128)(2,1)S(1)}, bf16[16,4096]{1,0:T(8,128)(2,1)S(1)}, u32[]{:S(2)}, u32[]{:S(2)}) collective-permute-start(bf16[16,4096]{1,0:T(8,128)(2,1)S(1)} %reshape.12.refs_1_), channel_id=1, source_target_pairs={{0,56},{8,0},{16,8},{24,16},{32,24},{40,32},{48,40},{56,48},{1,57}... | collective-permute-start | bytes 393224 | tf_op jit(solution)/shard_map/gather_projected/ppermute | solution.py:202
  15.3 6.6 %collective-permute-start.8 = (bf16[16,4096]{1,0:T(8,128)(2,1)S(1)}, bf16[16,4096]{1,0:T(8,128)(2,1)S(1)}, u32[]{:S(2)}, u32[]{:S(2)}) collective-permute-start(bf16[16,4096]{1,0:T(8,128)(2,1)S(1)} %collective-permute-done.7.refs_9_), channel_id=1, source_target_pairs={{0,8},{8,16},{16,24},{24,32},{32,40},{40,48},{48,56},{56,0},{1,9},... | collective-permute-start | bytes 393224 | tf_op jit(solution)/shard_map/gather_projected/ppermute | solution.py:202
  18.1 53.1 %collective-permute-start.31 = (bf16[256,4096]{1,0:T(8,128)(2,1)S(1)}, bf16[256,4096]{1,0:T(8,128)(2,1)S(1)}, u32[]{:S(2)}, u32[]{:S(2)}) collective-permute-start(bf16[256,4096]{1,0:T(8,128)(2,1)S(1)} %bitcast.7), channel_id=1, source_target_pairs={{0,6},{6,0},{2,4},{4,2},{1,7},{7,1},{3,5},{5,3},{8,14},{14,8},{10,... | collective-permute-start | bytes 6291464 | tf_op jit(solution)/shard_map/swap_stored/ppermute | solution.py:245
  18.8 5.2 %collective-permute-start.9 = (bf16[16,4096]{1,0:T(8,128)(2,1)S(1)}, bf16[16,4096]{1,0:T(8,128)(2,1)S(1)}, u32[]{:S(2)}, u32[]{:S(2)}) collective-permute-start(bf16[16,4096]{1,0:T(8,128)(2,1)S(1)} %collective-permute-done.7.refs_9_), channel_id=1, source_target_pairs={{0,56},{8,0},{16,8},{24,16},{32,24},{40,32},{48,40},{56,48},{1,57}... | collective-permute-start | bytes 393224 | tf_op jit(solution)/shard_map/gather_projected/ppermute | solution.py:202
  21.3 5.3 %collective-permute-start.2 = (bf16[16,4096]{1,0:T(8,128)(2,1)S(1)}, bf16[16,4096]{1,0:T(8,128)(2,1)S(1)}, u32[]{:S(2)}, u32[]{:S(2)}) collective-permute-start(bf16[16,4096]{1,0:T(8,128)(2,1)S(1)} %collective-permute-done.refs_2_), channel_id=1, source_target_pairs={{0,8},{8,16},{16,24},{24,32},{32,40},{40,48},{48,56},{56,0},{1,9},... | collective-permute-start | bytes 393224 | tf_op jit(solution)/shard_map/gather_projected/ppermute | solution.py:202
  21.9 5.4 %collective-permute-start.3 = (bf16[16,4096]{1,0:T(8,128)(2,1)S(1)}, bf16[16,4096]{1,0:T(8,128)(2,1)S(1)}, u32[]{:S(2)}, u32[]{:S(2)}) collective-permute-start(bf16[16,4096]{1,0:T(8,128)(2,1)S(1)} %collective-permute-done.1.refs_3_), channel_id=1, source_target_pairs={{0,56},{8,0},{16,8},{24,16},{32,24},{40,32},{48,40},{56,48},{1,57}... | collective-permute-start | bytes 393224 | tf_op jit(solution)/shard_map/gather_projected/ppermute | solution.py:202
  24.0 6.5 %collective-permute-start.10 = (bf16[16,4096]{1,0:T(8,128)(2,1)S(1)}, bf16[16,4096]{1,0:T(8,128)(2,1)S(1)}, u32[]{:S(2)}, u32[]{:S(2)}) collective-permute-start(bf16[16,4096]{1,0:T(8,128)(2,1)S(1)} %collective-permute-done.8.refs_10_), channel_id=1, source_target_pairs={{0,8},{8,16},{16,24},{24,32},{32,40},{40,48},{48,56},{56,0},{1,9},... | collective-permute-start | bytes 393224 | tf_op jit(solution)/shard_map/gather_projected/ppermute | solution.py:202
  26.6 4.1 %collective-permute-start.11 = (bf16[16,4096]{1,0:T(8,128)(2,1)S(1)}, bf16[16,4096]{1,0:T(8,128)(2,1)S(1)}, u32[]{:S(2)}, u32[]{:S(2)}) collective-permute-start(bf16[16,4096]{1,0:T(8,128)(2,1)S(1)} %collective-permute-done.9.refs_11_), channel_id=1, source_target_pairs={{0,56},{8,0},{16,8},{24,16},{32,24},{40,32},{48,40},{56,48},{1,57}... | collective-permute-start | bytes 393224 | tf_op jit(solution)/shard_map/gather_projected/ppermute | solution.py:202
  27.3 7.0 %collective-permute-start.4 = (bf16[16,4096]{1,0:T(8,128)(2,1)S(1)}, bf16[16,4096]{1,0:T(8,128)(2,1)S(1)}, u32[]{:S(2)}, u32[]{:S(2)}) collective-permute-start(bf16[16,4096]{1,0:T(8,128)(2,1)S(1)} %collective-permute-done.2.refs_4_), channel_id=1, source_target_pairs={{0,8},{8,16},{16,24},{24,32},{32,40},{40,48},{48,56},{56,0},{1,9},... | collective-permute-start | bytes 393224 | tf_op jit(solution)/shard_map/gather_projected/ppermute | solution.py:202
  30.5 4.9 %collective-permute-start.5 = (bf16[16,4096]{1,0:T(8,128)(2,1)S(1)}, bf16[16,4096]{1,0:T(8,128)(2,1)S(1)}, u32[]{:S(2)}, u32[]{:S(2)}) collective-permute-start(bf16[16,4096]{1,0:T(8,128)(2,1)S(1)} %collective-permute-done.3.refs_5_), channel_id=1, source_target_pairs={{0,56},{8,0},{16,8},{24,16},{32,24},{40,32},{48,40},{56,48},{1,57}... | collective-permute-start | bytes 393224 | tf_op jit(solution)/shard_map/gather_projected/ppermute | solution.py:202
  30.7 9.8 %collective-permute-start.12 = (bf16[16,4096]{1,0:T(8,128)(2,1)S(1)}, bf16[16,4096]{1,0:T(8,128)(2,1)S(1)}, u32[]{:S(2)}, u32[]{:S(2)}) collective-permute-start(bf16[16,4096]{1,0:T(8,128)(2,1)S(1)} %collective-permute-done.10.refs_12_), channel_id=1, source_target_pairs={{0,8},{8,16},{16,24},{24,32},{32,40},{40,48},{48,56},{56,0},{1,9},... | collective-permute-start | bytes 393224 | tf_op jit(solution)/shard_map/gather_projected/ppermute | solution.py:202
  34.3 6.3 %collective-permute-start.13 = (bf16[16,4096]{1,0:T(8,128)(2,1)S(1)}, bf16[16,4096]{1,0:T(8,128)(2,1)S(1)}, u32[]{:S(2)}, u32[]{:S(2)}) collective-permute-start(bf16[16,4096]{1,0:T(8,128)(2,1)S(1)} %collective-permute-done.11.refs_13_), channel_id=1, source_target_pairs={{0,56},{8,0},{16,8},{24,16},{32,24},{40,32},{48,40},{56,48},{1,57}... | collective-permute-start | bytes 393224 | tf_op jit(solution)/shard_map/gather_projected/ppermute | solution.py:202
  35.4 11.0 %collective-permute-start.15 = (f32[64,4096]{1,0:T(8,128)}, f32[64,4096]{1,0:T(8,128)S(1)}, u32[]{:S(2)}, u32[]{:S(2)}) collective-permute-start(f32[64,4096]{1,0:T(8,128)} %bitcast.13), channel_id=1, source_target_pairs={{0,1},{1,0},{2,3},{3,2},{4,5},{5,4},{6,7},{7,6},{8,9},{9,8},{10,11... | collective-permute-start | bytes 3145736 | tf_op jit(solution)/shard_map/swap_inverse/ppermute | solution.py:210
  40.5 5.9 %collective-permute-start.17 = (f32[64,4096]{1,0:T(8,128)S(1)}, f32[64,4096]{1,0:T(8,128)S(1)}, u32[]{:S(2)}, u32[]{:S(2)}) collective-permute-start(f32[64,4096]{1,0:T(8,128)S(1)} %collective-permute-done.16.chip_ref), channel_id=1, source_target_pairs={{0,1},{1,0},{2,3},{3,2},{4,5},{5,4},{6,7},{7,6},{8,9},{9,8},{10,11... | collective-permute-start | bytes 3145736 | tf_op jit(solution)/shard_map/swap_inverse/ppermute | solution.py:210
  43.5 6.7 %collective-permute-start.6 = (bf16[16,4096]{1,0:T(8,128)(2,1)S(1)}, bf16[16,4096]{1,0:T(8,128)(2,1)S(1)}, u32[]{:S(2)}, u32[]{:S(2)}) collective-permute-start(bf16[16,4096]{1,0:T(8,128)(2,1)S(1)} %collective-permute-done.4.refs_6_), channel_id=1, source_target_pairs={{0,8},{8,16},{16,24},{24,32},{32,40},{40,48},{48,56},{56,0},{1,9},... | collective-permute-start | bytes 393224 | tf_op jit(solution)/shard_map/gather_projected/ppermute | solution.py:202
  43.9 6.4 %collective-permute-start.14 = (bf16[16,4096]{1,0:T(8,128)(2,1)S(1)}, bf16[16,4096]{1,0:T(8,128)(2,1)S(1)}, u32[]{:S(2)}, u32[]{:S(2)}) collective-permute-start(bf16[16,4096]{1,0:T(8,128)(2,1)S(1)} %collective-permute-done.13.refs_15_), channel_id=1, source_target_pairs={{0,56},{8,0},{16,8},{24,16},{32,24},{40,32},{48,40},{56,48},{1,57}... | collective-permute-start | bytes 393224 | tf_op jit(solution)/shard_map/gather_projected/ppermute | solution.py:202
  46.5 1.2 %copy-start.2 = (f32[1,64,4096]{2,1,0:T(8,128)S(1)}, f32[1,64,4096]{2,1,0:T(8,128)}, u32[]{:S(2)}) copy-start(f32[1,64,4096]{2,1,0:T(8,128)} %param.7) | copy-start | bytes 3145732
  52.0 4.5 %collective-permute-start.22 = (bf16[256,256]{1,0:T(8,128)(2,1)S(1)}, bf16[256,256]{1,0:T(8,128)(2,1)S(1)}, u32[]{:S(2)}, u32[]{:S(2)}) collective-permute-start(bf16[256,256]{1,0:T(8,128)(2,1)S(1)} %precondition.1.refs_1_), channel_id=1, source_target_pairs={{0,2},{2,0},{4,6},{6,4},{1,3},{3,1},{5,7},{7,5},{8,10},{10,8},{12,... | collective-permute-start | bytes 393224 | tf_op jit(solution)/shard_map/gather_preconditioned/ppermute | solution.py:245
  52.3 6.9 %collective-permute-start.18 = (bf16[256,256]{1,0:T(8,128)(2,1)S(1)}, bf16[256,256]{1,0:T(8,128)(2,1)S(1)}, u32[]{:S(2)}, u32[]{:S(2)}) collective-permute-start(bf16[256,256]{1,0:T(8,128)(2,1)S(1)} %precondition.1.refs_1_), channel_id=1, source_target_pairs={{0,8},{8,16},{16,24},{24,32},{32,40},{40,48},{48,56},{56,0},{1,9},... | collective-permute-start | bytes 393224 | tf_op jit(solution)/shard_map/gather_preconditioned/ppermute | solution.py:202
  54.3 5.3 %collective-permute-start.32 = (bf16[256,256]{1,0:T(8,128)(2,1)S(1)}, bf16[256,256]{1,0:T(8,128)(2,1)S(1)}, u32[]{:S(2)}, u32[]{:S(2)}) collective-permute-start(bf16[256,256]{1,0:T(8,128)(2,1)S(1)} %precondition.1.refs_1_), channel_id=1, source_target_pairs={{0,56},{8,0},{16,8},{24,16},{32,24},{40,32},{48,40},{56,48},{1,57}... | collective-permute-start | bytes 393224 | tf_op jit(solution)/shard_map/gather_preconditioned/ppermute | solution.py:202
  56.5 5.4 %collective-permute-start.23 = (bf16[256,256]{1,0:T(8,128)(2,1)S(1)}, bf16[256,256]{1,0:T(8,128)(2,1)S(1)}, u32[]{:S(2)}, u32[]{:S(2)}) collective-permute-start(bf16[256,256]{1,0:T(8,128)(2,1)S(1)} %collective-permute-done.22.refs_8_), channel_id=1, source_target_pairs={{0,8},{8,16},{16,24},{24,32},{32,40},{40,48},{48,56},{56,0},{1,9},... | collective-permute-start | bytes 393224 | tf_op jit(solution)/shard_map/gather_preconditioned/ppermute | solution.py:202
  58.2 4.1 %collective-permute-start.26 = (bf16[256,256]{1,0:T(8,128)(2,1)S(1)}, bf16[256,256]{1,0:T(8,128)(2,1)S(1)}, u32[]{:S(2)}, u32[]{:S(2)}) collective-permute-start(bf16[256,256]{1,0:T(8,128)(2,1)S(1)} %collective-permute-done.22.refs_8_), channel_id=1, source_target_pairs={{0,56},{8,0},{16,8},{24,16},{32,24},{40,32},{48,40},{56,48},{1,57}... | collective-permute-start | bytes 393224 | tf_op jit(solution)/shard_map/gather_preconditioned/ppermute | solution.py:202
  59.2 6.0 %collective-permute-start.19 = (bf16[256,256]{1,0:T(8,128)(2,1)S(1)}, bf16[256,256]{1,0:T(8,128)(2,1)S(1)}, u32[]{:S(2)}, u32[]{:S(2)}) collective-permute-start(bf16[256,256]{1,0:T(8,128)(2,1)S(1)} %collective-permute-done.18.refs_2_), channel_id=1, source_target_pairs={{0,8},{8,16},{16,24},{24,32},{32,40},{40,48},{48,56},{56,0},{1,9},... | collective-permute-start | bytes 393224 | tf_op jit(solution)/shard_map/gather_preconditioned/ppermute | solution.py:202
  59.6 5.6 %collective-permute-start.33 = (bf16[256,256]{1,0:T(8,128)(2,1)S(1)}, bf16[256,256]{1,0:T(8,128)(2,1)S(1)}, u32[]{:S(2)}, u32[]{:S(2)}) collective-permute-start(bf16[256,256]{1,0:T(8,128)(2,1)S(1)} %collective-permute-done.32.refs_3_), channel_id=1, source_target_pairs={{0,56},{8,0},{16,8},{24,16},{32,24},{40,32},{48,40},{56,48},{1,57}... | collective-permute-start | bytes 393224 | tf_op jit(solution)/shard_map/gather_preconditioned/ppermute | solution.py:202
  61.9 6.6 %collective-permute-start.24 = (bf16[256,256]{1,0:T(8,128)(2,1)S(1)}, bf16[256,256]{1,0:T(8,128)(2,1)S(1)}, u32[]{:S(2)}, u32[]{:S(2)}) collective-permute-start(bf16[256,256]{1,0:T(8,128)(2,1)S(1)} %collective-permute-done.23.refs_9_), channel_id=1, source_target_pairs={{0,8},{8,16},{16,24},{24,32},{32,40},{40,48},{48,56},{56,0},{1,9},... | collective-permute-start | bytes 393224 | tf_op jit(solution)/shard_map/gather_preconditioned/ppermute | solution.py:202
  62.3 6.2 %collective-permute-start.27 = (bf16[256,256]{1,0:T(8,128)(2,1)S(1)}, bf16[256,256]{1,0:T(8,128)(2,1)S(1)}, u32[]{:S(2)}, u32[]{:S(2)}) collective-permute-start(bf16[256,256]{1,0:T(8,128)(2,1)S(1)} %collective-permute-done.26.refs_10_), channel_id=1, source_target_pairs={{0,56},{8,0},{16,8},{24,16},{32,24},{40,32},{48,40},{56,48},{1,57}... | collective-permute-start | bytes 393224 | tf_op jit(solution)/shard_map/gather_preconditioned/ppermute | solution.py:202
  65.2 10.4 %collective-permute-start.20 = (bf16[256,256]{1,0:T(8,128)(2,1)S(1)}, bf16[256,256]{1,0:T(8,128)(2,1)S(1)}, u32[]{:S(2)}, u32[]{:S(2)}) collective-permute-start(bf16[256,256]{1,0:T(8,128)(2,1)S(1)} %collective-permute-done.19.refs_4_), channel_id=1, source_target_pairs={{0,8},{8,16},{16,24},{24,32},{32,40},{40,48},{48,56},{56,0},{1,9},... | collective-permute-start | bytes 393224 | tf_op jit(solution)/shard_map/gather_preconditioned/ppermute | solution.py:202
  65.2 10.4 %collective-permute-start.34 = (bf16[256,256]{1,0:T(8,128)(2,1)S(1)}, bf16[256,256]{1,0:T(8,128)(2,1)S(1)}, u32[]{:S(2)}, u32[]{:S(2)}) collective-permute-start(bf16[256,256]{1,0:T(8,128)(2,1)S(1)} %collective-permute-done.33.refs_5_), channel_id=1, source_target_pairs={{0,56},{8,0},{16,8},{24,16},{32,24},{40,32},{48,40},{56,48},{1,57}... | collective-permute-start | bytes 393224 | tf_op jit(solution)/shard_map/gather_preconditioned/ppermute | solution.py:202
  68.5 7.1 %collective-permute-start.25 = (bf16[256,256]{1,0:T(8,128)(2,1)S(1)}, bf16[256,256]{1,0:T(8,128)(2,1)S(1)}, u32[]{:S(2)}, u32[]{:S(2)}) collective-permute-start(bf16[256,256]{1,0:T(8,128)(2,1)S(1)} %collective-permute-done.24.refs_11_), channel_id=1, source_target_pairs={{0,8},{8,16},{16,24},{24,32},{32,40},{40,48},{48,56},{56,0},{1,9},... | collective-permute-start | bytes 393224 | tf_op jit(solution)/shard_map/gather_preconditioned/ppermute | solution.py:202
  68.5 7.1 %collective-permute-start.28 = (bf16[256,256]{1,0:T(8,128)(2,1)S(1)}, bf16[256,256]{1,0:T(8,128)(2,1)S(1)}, u32[]{:S(2)}, u32[]{:S(2)}) collective-permute-start(bf16[256,256]{1,0:T(8,128)(2,1)S(1)} %collective-permute-done.27.refs_12_), channel_id=1, source_target_pairs={{0,56},{8,0},{16,8},{24,16},{32,24},{40,32},{48,40},{56,48},{1,57}... | collective-permute-start | bytes 393224 | tf_op jit(solution)/shard_map/gather_preconditioned/ppermute | solution.py:202
  71.2 10.3 %collective-permute-start.30 = (bf16[256,4096]{1,0:T(8,128)(2,1)S(1)}, bf16[256,4096]{1,0:T(8,128)(2,1)S(1)}, u32[]{:S(2)}, u32[]{:S(2)}) collective-permute-start(bf16[256,4096]{1,0:T(8,128)(2,1)S(1)} %bitcast.8), channel_id=1, source_target_pairs={{0,1},{1,0},{2,3},{3,2},{4,5},{5,4},{6,7},{7,6},{8,9},{9,8},{10,11... | collective-permute-start | bytes 6291464 | tf_op jit(solution)/shard_map/swap_stored/ppermute | solution.py:210
  75.6 6.8 %collective-permute-start.35 = (bf16[256,4096]{1,0:T(8,128)(2,1)S(1)}, bf16[256,4096]{1,0:T(8,128)(2,1)S(1)}, u32[]{:S(2)}, u32[]{:S(2)}) collective-permute-start(bf16[256,4096]{1,0:T(8,128)(2,1)S(1)} %collective-permute-done.31.refs_15_.refs_7_), channel_id=1, source_target_pairs={{0,1},{1,0},{2,3},{3,2},{4,5},{5,4},{6,7},{7,6},{8,9},{9,8},{10,11... | collective-permute-start | bytes 6291464 | tf_op jit(solution)/shard_map/swap_stored/ppermute | solution.py:210
  78.5 6.8 %collective-permute-start.21 = (bf16[256,256]{1,0:T(8,128)(2,1)S(1)}, bf16[256,256]{1,0:T(8,128)(2,1)S(1)}, u32[]{:S(2)}, u32[]{:S(2)}) collective-permute-start(bf16[256,256]{1,0:T(8,128)(2,1)S(1)} %collective-permute-done.20.refs_6_), channel_id=1, source_target_pairs={{0,8},{8,16},{16,24},{24,32},{32,40},{40,48},{48,56},{56,0},{1,9},... | collective-permute-start | bytes 393224 | tf_op jit(solution)/shard_map/gather_preconditioned/ppermute | solution.py:202
  78.5 6.8 %collective-permute-start.29 = (bf16[256,256]{1,0:T(8,128)(2,1)S(1)}, bf16[256,256]{1,0:T(8,128)(2,1)S(1)}, u32[]{:S(2)}, u32[]{:S(2)}) collective-permute-start(bf16[256,256]{1,0:T(8,128)(2,1)S(1)} %collective-permute-done.28.refs_3_), channel_id=1, source_target_pairs={{0,56},{8,0},{16,8},{24,16},{32,24},{40,32},{48,40},{56,48},{1,57}... | collective-permute-start | bytes 393224 | tf_op jit(solution)/shard_map/gather_preconditioned/ppermute | solution.py:202
  86.9 5.8 %collective-permute-start.36 = (bf16[64,1024]{1,0:T(8,128)(2,1)S(1)}, bf16[64,1024]{1,0:T(8,128)(2,1)S(1)}, u32[]{:S(2)}, u32[]{:S(2)}) collective-permute-start(bf16[64,1024]{1,0:T(8,128)(2,1)S(1)} %get-tuple-element.28), channel_id=1, source_target_pairs={{0,64},{64,128},{128,192},{192,0},{1,65},{65,129},{129,193},{193,1... | collective-permute-start | bytes 393224 | tf_op jit(solution)/shard_map/sum_layers/ppermute | solution.py:202
  88.2 8.3 %collective-permute-start.37 = (bf16[64,1024]{1,0:T(8,128)(2,1)S(1)}, bf16[64,1024]{1,0:T(8,128)(2,1)S(1)}, u32[]{:S(2)}, u32[]{:S(2)}) collective-permute-start(bf16[64,1024]{1,0:T(8,128)(2,1)S(1)} %get-tuple-element.29), channel_id=1, source_target_pairs={{0,128},{64,192},{128,0},{192,64},{1,129},{65,193},{129,1},{193,65... | collective-permute-start | bytes 393224 | tf_op jit(solution)/shard_map/sum_layers/ppermute | solution.py:202
  90.6 5.8 %collective-permute-start.38 = (bf16[64,1024]{1,0:T(8,128)(2,1)S(1)}, bf16[64,1024]{1,0:T(8,128)(2,1)S(1)}, u32[]{:S(2)}, u32[]{:S(2)}) collective-permute-start(bf16[64,1024]{1,0:T(8,128)(2,1)S(1)} %get-tuple-element.30), channel_id=1, source_target_pairs={{0,192},{64,0},{128,64},{192,128},{1,193},{65,1},{129,65},{193,129... | collective-permute-start | bytes 393224 | tf_op jit(solution)/shard_map/sum_layers/ppermute | solution.py:202
  96.5 4.5 %collective-permute-start.39 = (bf16[64,256]{1,0:T(8,128)(2,1)S(1)}, bf16[64,256]{1,0:T(8,128)(2,1)S(1)}, u32[]{:S(2)}, u32[]{:S(2)}) collective-permute-start(bf16[64,256]{1,0:T(8,128)(2,1)S(1)} %get-tuple-element.32), channel_id=1, source_target_pairs={{0,1},{1,0},{2,3},{3,2},{4,5},{5,4},{6,7},{7,6},{8,9},{9,8},{10,11... | collective-permute-start | bytes 98312 | tf_op jit(solution)/shard_map/exchange_examples/ppermute | solution.py:281
  98.0 4.0 %collective-permute-start.40 = (bf16[64,256]{1,0:T(8,128)(2,1)S(1)}, bf16[64,256]{1,0:T(8,128)(2,1)S(1)}, u32[]{:S(2)}, u32[]{:S(2)}) collective-permute-start(bf16[64,256]{1,0:T(8,128)(2,1)S(1)} %get-tuple-element.33), channel_id=1, source_target_pairs={{0,6},{1,7},{2,4},{3,5},{4,2},{5,3},{6,0},{7,1},{8,14},{9,15},{10,... | collective-permute-start | bytes 98312 | tf_op jit(solution)/shard_map/exchange_examples/ppermute | solution.py:281
  99.8 4.6 %collective-permute-start.41 = (bf16[64,256]{1,0:T(8,128)(2,1)S(1)}, bf16[64,256]{1,0:T(8,128)(2,1)S(1)}, u32[]{:S(2)}, u32[]{:S(2)}) collective-permute-start(bf16[64,256]{1,0:T(8,128)(2,1)S(1)} %get-tuple-element.34), channel_id=1, source_target_pairs={{0,7},{1,6},{2,5},{3,4},{4,3},{5,2},{6,1},{7,0},{8,15},{9,14},{10,... | collective-permute-start | bytes 98312 | tf_op jit(solution)/shard_map/exchange_examples/ppermute | solution.py:281

commit v5 on v4

--- a/solution.py
+++ b/solution.py
@@ -272,7 +272,7 @@
             total = score(where, part, [pieces[k][2] for k in part], stored_parts, total, part is late)
         kept, *sent = total
     with jax.named_scope("sum_layers"):
-        others = [shift(value, "layer", LAYER, k + 1) for k, value in enumerate(sent)]
+        others = [shift(sent[k], "layer", LAYER, k + 1) for k in (1, 0, 2)]
         parts = add_layers(kept, others)
     with jax.named_scope("exchange_examples"):
         pairs = []

time: 106 us -> 106 us (level)
  no operation moved by 1% of the time
where the time goes in v5:
time: 106 us; the launch traced here: 105 us
  starting transfers between devices  66.1 us (62%)
  waiting for transfers between devices  23.7 us (22%)
  Pallas kernels  10.5 us (10%)
  local copies, waits for them, and re-layouts  4.16 us (4%)
    ppermute x31, starting transfers between devices, shift(): lax.ppermute(value, axis, [(i, (i + by) % size) for i in range(size)])  41.9 us
    ppermute x31, waiting for transfers between devices, shift(): lax.ppermute(value, axis, [(i, (i + by) % size) for i in range(size)])  17.8 us
    ppermute x4, starting transfers between devices, swap_core(): return lax.ppermute(value, 'core', [(0, 1), (1, 0)])  15.4 us
    ppermute x4, starting transfers between devices, swap_chip(): lax.ppermute(value, 'y', [pair for a, b in pairs for pair in ((a, b), (b,...  4.57 us
    ppermute x3, starting transfers between devices, per_device(): lax.ppermute(parts[k], ('y', 'core'), pairs[k - 1])  4.13 us
    pallas_call x2, Pallas kernels, score(): pl.pallas_call(lambda *refs: score_kernel(some, len(stored), before is No...  4.04 us
    unnamed x8, local copies, waits for them, and re-layouts  3.47 us
    ppermute x3, waiting for transfers between devices, per_device(): lax.ppermute(parts[k], ('y', 'core'), pairs[k - 1])  3.45 us
  transfers between devices with their start and end apart: 42, of which 16 were waited for; matrix products, arithmetic and copies ran while one was open for 1% of the time, Pallas kernels for 7%

profile of v5, /device:TPU:1, one launch (start us, length us, event | category | flops | bytes accessed | tf_op | source)
XLA Modules:
  0.0 105.4 jit_solution(15454128687100130548)
XLA Ops:
  0.0 3.6 %collective-permute-start.16 = (f32[64,4096]{1,0:T(8,128)}, f32[64,4096]{1,0:T(8,128)S(1)}, u32[]{:S(2)}, u32[]{:S(2)}) collective-permute-start(f32[64,4096]{1,0:T(8,128)} %bitcast.12), channel_id=1, source_target_pairs={{0,6},{6,0},{2,4},{4,2},{1,7},{7,1},{3,5},{5,3},{8,14},{14,8},{10,... | collective-permute-start | bytes 3145736 | tf_op jit(solution)/shard_map/swap_inverse/ppermute | solution.py:245
  3.7 0.1 xor.12
  3.8 0.7 broadcast_multiply_fusion
  4.8 1.6 %copy-done.1 = bf16[1,16,512,128]{3,2,1,0:T(8,128)(2,1)S(1)} copy-done((bf16[1,16,512,128]{3,2,1,0:T(8,128)(2,1)S(1)}, bf16[1,16,512,128]{3,2,1,0:T(8,128)(2,1)}, u32[]{:S(2)}) %copy-start.1) | copy-done | bytes 2097176
  6.4 0.7 copy-done.3
  7.1 2.1 %form_gradients.1 = bf16[16,64,64]{2,1,0:T(8,128)(2,1)S(1)} custom-call(s32[16]{0:T(128)S(1)} %copy-done.3, bf16[16,512,128]{2,1,0:T(8,128)(2,1)S(1)} %bitcast.11), custom_call_target="tpu_custom_call" | custom-call | flops 268435456 | bytes 2097152 | tf_op jit(solution)/shard_map/gradients/form_gradients/pallas_call | solution.py:41
  9.2 0.3 reshape.12.refs_1_
  9.5 0.1 collective-permute-start.7
  9.6 1.7 %collective-permute-start = (bf16[16,4096]{1,0:T(8,128)(2,1)S(1)}, bf16[16,4096]{1,0:T(8,128)(2,1)S(1)}, u32[]{:S(2)}, u32[]{:S(2)}) collective-permute-start(bf16[16,4096]{1,0:T(8,128)(2,1)S(1)} %reshape.12.refs_1_), channel_id=1, source_target_pairs={{0,8},{8,16},{16,24},{24,32},{32,40},{40,48},{48,56},{56,0},{1,9},... | collective-permute-start | bytes 393224 | tf_op jit(solution)/shard_map/gather_projected/ppermute | solution.py:202
  11.3 4.0 %collective-permute-start.1 = (bf16[16,4096]{1,0:T(8,128)(2,1)S(1)}, bf16[16,4096]{1,0:T(8,128)(2,1)S(1)}, u32[]{:S(2)}, u32[]{:S(2)}) collective-permute-start(bf16[16,4096]{1,0:T(8,128)(2,1)S(1)} %reshape.12.refs_1_), channel_id=1, source_target_pairs={{0,56},{8,0},{16,8},{24,16},{32,24},{40,32},{48,40},{56,48},{1,57}... | collective-permute-start | bytes 393224 | tf_op jit(solution)/shard_map/gather_projected/ppermute | solution.py:202
  15.3 2.8 %collective-permute-done.refs_2_ = bf16[16,4096]{1,0:T(8,128)(2,1)S(1)} collective-permute-done((bf16[16,4096]{1,0:T(8,128)(2,1)S(1)}, bf16[16,4096]{1,0:T(8,128)(2,1)S(1)}, u32[]{:S(2)}, u32[]{:S(2)}) %collective-permute-start) | collective-permute-done | bytes 131104 | tf_op jit(solution)/shard_map/gather_projected/ppermute | solution.py:202
  18.1 0.7 collective-permute-start.31
  18.8 2.5 %collective-permute-start.9 = (bf16[16,4096]{1,0:T(8,128)(2,1)S(1)}, bf16[16,4096]{1,0:T(8,128)(2,1)S(1)}, u32[]{:S(2)}, u32[]{:S(2)}) collective-permute-start(bf16[16,4096]{1,0:T(8,128)(2,1)S(1)} %collective-permute-done.7.refs_9_), channel_id=1, source_target_pairs={{0,56},{8,0},{16,8},{24,16},{32,24},{40,32},{48,40},{56,48},{1,57}... | collective-permute-start | bytes 393224 | tf_op jit(solution)/shard_map/gather_projected/ppermute | solution.py:202
  21.3 0.6 collective-permute-done.8.refs_10_
  21.9 2.1 %collective-permute-start.3 = (bf16[16,4096]{1,0:T(8,128)(2,1)S(1)}, bf16[16,4096]{1,0:T(8,128)(2,1)S(1)}, u32[]{:S(2)}, u32[]{:S(2)}) collective-permute-start(bf16[16,4096]{1,0:T(8,128)(2,1)S(1)} %collective-permute-done.1.refs_3_), channel_id=1, source_target_pairs={{0,56},{8,0},{16,8},{24,16},{32,24},{40,32},{48,40},{56,48},{1,57}... | collective-permute-start | bytes 393224 | tf_op jit(solution)/shard_map/gather_projected/ppermute | solution.py:202
  24.0 2.6 %collective-permute-done.2.refs_4_ = bf16[16,4096]{1,0:T(8,128)(2,1)S(1)} collective-permute-done((bf16[16,4096]{1,0:T(8,128)(2,1)S(1)}, bf16[16,4096]{1,0:T(8,128)(2,1)S(1)}, u32[]{:S(2)}, u32[]{:S(2)}) %collective-permute-start.2) | collective-permute-done | bytes 131104 | tf_op jit(solution)/shard_map/gather_projected/ppermute | solution.py:202
  26.6 0.4 collective-permute-start.11
  27.0 0.3 collective-permute-done.3.refs_5_
  27.3 0.8 collective-permute-start.4
  28.1 2.4 %collective-permute-done.10.refs_12_ = bf16[16,4096]{1,0:T(8,128)(2,1)S(1)} collective-permute-done((bf16[16,4096]{1,0:T(8,128)(2,1)S(1)}, bf16[16,4096]{1,0:T(8,128)(2,1)S(1)}, u32[]{:S(2)}, u32[]{:S(2)}) %collective-permute-start.10) | collective-permute-done | bytes 131104 | tf_op jit(solution)/shard_map/gather_projected/ppermute | solution.py:202
  30.5 0.3 collective-permute-start.5
  30.7 1.2 %collective-permute-start.12 = (bf16[16,4096]{1,0:T(8,128)(2,1)S(1)}, bf16[16,4096]{1,0:T(8,128)(2,1)S(1)}, u32[]{:S(2)}, u32[]{:S(2)}) collective-permute-start(bf16[16,4096]{1,0:T(8,128)(2,1)S(1)} %collective-permute-done.10.refs_12_), channel_id=1, source_target_pairs={{0,8},{8,16},{16,24},{24,32},{32,40},{40,48},{48,56},{56,0},{1,9},... | collective-permute-start | bytes 393224 | tf_op jit(solution)/shard_map/gather_projected/ppermute | solution.py:202
  32.0 2.3 %collective-permute-done.4.refs_6_ = bf16[16,4096]{1,0:T(8,128)(2,1)S(1)} collective-permute-done((bf16[16,4096]{1,0:T(8,128)(2,1)S(1)}, bf16[16,4096]{1,0:T(8,128)(2,1)S(1)}, u32[]{:S(2)}, u32[]{:S(2)}) %collective-permute-start.4) | collective-permute-done | bytes 131104 | tf_op jit(solution)/shard_map/gather_projected/ppermute | solution.py:202
  34.3 1.1 %collective-permute-start.13 = (bf16[16,4096]{1,0:T(8,128)(2,1)S(1)}, bf16[16,4096]{1,0:T(8,128)(2,1)S(1)}, u32[]{:S(2)}, u32[]{:S(2)}) collective-permute-start(bf16[16,4096]{1,0:T(8,128)(2,1)S(1)} %collective-permute-done.11.refs_13_), channel_id=1, source_target_pairs={{0,56},{8,0},{16,8},{24,16},{32,24},{40,32},{48,40},{56,48},{1,57}... | collective-permute-start | bytes 393224 | tf_op jit(solution)/shard_map/gather_projected/ppermute | solution.py:202
  35.4 5.1 %collective-permute-start.15 = (f32[64,4096]{1,0:T(8,128)}, f32[64,4096]{1,0:T(8,128)S(1)}, u32[]{:S(2)}, u32[]{:S(2)}) collective-permute-start(f32[64,4096]{1,0:T(8,128)} %bitcast.13), channel_id=1, source_target_pairs={{0,1},{1,0},{2,3},{3,2},{4,5},{5,4},{6,7},{7,6},{8,9},{9,8},{10,11... | collective-permute-start | bytes 3145736 | tf_op jit(solution)/shard_map/swap_inverse/ppermute | solution.py:210
  40.5 2.9 %collective-permute-start.17 = (f32[64,4096]{1,0:T(8,128)S(1)}, f32[64,4096]{1,0:T(8,128)S(1)}, u32[]{:S(2)}, u32[]{:S(2)}) collective-permute-start(f32[64,4096]{1,0:T(8,128)S(1)} %collective-permute-done.16.chip_ref), channel_id=1, source_target_pairs={{0,1},{1,0},{2,3},{3,2},{4,5},{5,4},{6,7},{7,6},{8,9},{9,8},{10,11... | collective-permute-start | bytes 3145736 | tf_op jit(solution)/shard_map/swap_inverse/ppermute | solution.py:210
  43.5 0.4 collective-permute-start.6
  43.9 2.6 %collective-permute-start.14 = (bf16[16,4096]{1,0:T(8,128)(2,1)S(1)}, bf16[16,4096]{1,0:T(8,128)(2,1)S(1)}, u32[]{:S(2)}, u32[]{:S(2)}) collective-permute-start(bf16[16,4096]{1,0:T(8,128)(2,1)S(1)} %collective-permute-done.13.refs_15_), channel_id=1, source_target_pairs={{0,56},{8,0},{16,8},{24,16},{32,24},{40,32},{48,40},{56,48},{1,57}... | collective-permute-start | bytes 393224 | tf_op jit(solution)/shard_map/gather_projected/ppermute | solution.py:202
  46.5 1.2 %copy-done.2 = f32[1,64,4096]{2,1,0:T(8,128)S(1)} copy-done((f32[1,64,4096]{2,1,0:T(8,128)S(1)}, f32[1,64,4096]{2,1,0:T(8,128)}, u32[]{:S(2)}) %copy-start.2) | copy-done | bytes 1048600
  47.7 1.2 %split_inverse.1 = (bf16[256,4096]{1,0:T(8,128)(2,1)S(1)}, bf16[256,4096]{1,0:T(8,128)(2,1)S(1)}) custom-call(s32[50]{0:T(128)S(1)} %concatenate.3.where_ref.refs_0_, f32[64,4096]{1,0:T(8,128)S(1)} %bitcast.14, f32[64,4096]{1,0:T(8,128)S(1)} %collective-permute-done.15.core_ref, f32[64,4096]{1,0:T(8,128)S(1)} %collective-permute-done.16.chip_ref, ...), custom_call_target="tpu_custom_call" | custom-call | flops 2097152 | bytes 8388608 | tf_op jit(solution)/shard_map/split_inverse/split_inverse/pallas_call | solution.py:71
  48.9 1.3 %collective-permute-done.6.refs_8_ = bf16[16,4096]{1,0:T(8,128)(2,1)S(1)} collective-permute-done((bf16[16,4096]{1,0:T(8,128)(2,1)S(1)}, bf16[16,4096]{1,0:T(8,128)(2,1)S(1)}, u32[]{:S(2)}, u32[]{:S(2)}) %collective-permute-start.6) | collective-permute-done | bytes 131104 | tf_op jit(solution)/shard_map/gather_projected/ppermute | solution.py:202
  50.2 1.8 %precondition.1.refs_1_ = bf16[256,256]{1,0:T(8,128)(2,1)S(1)} custom-call(s32[50]{0:T(128)S(1)} %concatenate.3.where_ref.refs_0_, bf16[16,4096]{1,0:T(8,128)(2,1)S(1)} %reshape.12.refs_1_, bf16[16,4096]{1,0:T(8,128)(2,1)S(1)} %collective-permute-done.refs_2_, bf16[16,4096]{1,0:T(8,128)(2,1)S(1)} %collective-permute-done.1.refs_3_, ...), custom_call_target="tpu_custom_call" | custom-call | flops 1073741824 | bytes 6291456 | tf_op jit(solution)/shard_map/precondition/precondition/pallas_call | solution.py:97
  52.0 0.2 collective-permute-start.22
  52.3 2.0 %collective-permute-start.18 = (bf16[256,256]{1,0:T(8,128)(2,1)S(1)}, bf16[256,256]{1,0:T(8,128)(2,1)S(1)}, u32[]{:S(2)}, u32[]{:S(2)}) collective-permute-start(bf16[256,256]{1,0:T(8,128)(2,1)S(1)} %precondition.1.refs_1_), channel_id=1, source_target_pairs={{0,8},{8,16},{16,24},{24,32},{32,40},{40,48},{48,56},{56,0},{1,9},... | collective-permute-start | bytes 393224 | tf_op jit(solution)/shard_map/gather_preconditioned/ppermute | solution.py:202
  54.3 0.6 collective-permute-start.32
  54.9 1.6 %collective-permute-done.22.refs_8_ = bf16[256,256]{1,0:T(8,128)(2,1)S(1)} collective-permute-done((bf16[256,256]{1,0:T(8,128)(2,1)S(1)}, bf16[256,256]{1,0:T(8,128)(2,1)S(1)}, u32[]{:S(2)}, u32[]{:S(2)}) %collective-permute-start.22) | collective-permute-done | bytes 131104 | tf_op jit(solution)/shard_map/gather_preconditioned/ppermute | solution.py:245
  56.5 1.7 %collective-permute-start.23 = (bf16[256,256]{1,0:T(8,128)(2,1)S(1)}, bf16[256,256]{1,0:T(8,128)(2,1)S(1)}, u32[]{:S(2)}, u32[]{:S(2)}) collective-permute-start(bf16[256,256]{1,0:T(8,128)(2,1)S(1)} %collective-permute-done.22.refs_8_), channel_id=1, source_target_pairs={{0,8},{8,16},{16,24},{24,32},{32,40},{40,48},{48,56},{56,0},{1,9},... | collective-permute-start | bytes 393224 | tf_op jit(solution)/shard_map/gather_preconditioned/ppermute | solution.py:202
  58.2 1.0 collective-permute-start.26
  59.2 0.5 collective-permute-start.19
  59.6 2.2 %collective-permute-start.33 = (bf16[256,256]{1,0:T(8,128)(2,1)S(1)}, bf16[256,256]{1,0:T(8,128)(2,1)S(1)}, u32[]{:S(2)}, u32[]{:S(2)}) collective-permute-start(bf16[256,256]{1,0:T(8,128)(2,1)S(1)} %collective-permute-done.32.refs_3_), channel_id=1, source_target_pairs={{0,56},{8,0},{16,8},{24,16},{32,24},{40,32},{48,40},{56,48},{1,57}... | collective-permute-start | bytes 393224 | tf_op jit(solution)/shard_map/gather_preconditioned/ppermute | solution.py:202
  61.9 0.4 collective-permute-start.24
  62.3 2.3 %collective-permute-start.27 = (bf16[256,256]{1,0:T(8,128)(2,1)S(1)}, bf16[256,256]{1,0:T(8,128)(2,1)S(1)}, u32[]{:S(2)}, u32[]{:S(2)}) collective-permute-start(bf16[256,256]{1,0:T(8,128)(2,1)S(1)} %collective-permute-done.26.refs_10_), channel_id=1, source_target_pairs={{0,56},{8,0},{16,8},{24,16},{32,24},{40,32},{48,40},{56,48},{1,57}... | collective-permute-start | bytes 393224 | tf_op jit(solution)/shard_map/gather_preconditioned/ppermute | solution.py:202
  64.6 0.7 collective-permute-done.19.refs_4_
  65.2 3.0 %collective-permute-start.34 = (bf16[256,256]{1,0:T(8,128)(2,1)S(1)}, bf16[256,256]{1,0:T(8,128)(2,1)S(1)}, u32[]{:S(2)}, u32[]{:S(2)}) collective-permute-start(bf16[256,256]{1,0:T(8,128)(2,1)S(1)} %collective-permute-done.33.refs_5_), channel_id=1, source_target_pairs={{0,56},{8,0},{16,8},{24,16},{32,24},{40,32},{48,40},{56,48},{1,57}... | collective-permute-start | bytes 393224 | tf_op jit(solution)/shard_map/gather_preconditioned/ppermute | solution.py:202
  68.2 0.3 collective-permute-done.24.refs_11_
  68.5 2.7 %collective-permute-start.28 = (bf16[256,256]{1,0:T(8,128)(2,1)S(1)}, bf16[256,256]{1,0:T(8,128)(2,1)S(1)}, u32[]{:S(2)}, u32[]{:S(2)}) collective-permute-start(bf16[256,256]{1,0:T(8,128)(2,1)S(1)} %collective-permute-done.27.refs_12_), channel_id=1, source_target_pairs={{0,56},{8,0},{16,8},{24,16},{32,24},{40,32},{48,40},{56,48},{1,57}... | collective-permute-start | bytes 393224 | tf_op jit(solution)/shard_map/gather_preconditioned/ppermute | solution.py:202
  71.2 4.4 %collective-permute-start.30 = (bf16[256,4096]{1,0:T(8,128)(2,1)S(1)}, bf16[256,4096]{1,0:T(8,128)(2,1)S(1)}, u32[]{:S(2)}, u32[]{:S(2)}) collective-permute-start(bf16[256,4096]{1,0:T(8,128)(2,1)S(1)} %bitcast.8), channel_id=1, source_target_pairs={{0,1},{1,0},{2,3},{3,2},{4,5},{5,4},{6,7},{7,6},{8,9},{9,8},{10,11... | collective-permute-start | bytes 6291464 | tf_op jit(solution)/shard_map/swap_stored/ppermute | solution.py:210
  75.6 2.9 %collective-permute-start.35 = (bf16[256,4096]{1,0:T(8,128)(2,1)S(1)}, bf16[256,4096]{1,0:T(8,128)(2,1)S(1)}, u32[]{:S(2)}, u32[]{:S(2)}) collective-permute-start(bf16[256,4096]{1,0:T(8,128)(2,1)S(1)} %collective-permute-done.31.refs_15_.refs_7_), channel_id=1, source_target_pairs={{0,1},{1,0},{2,3},{3,2},{4,5},{5,4},{6,7},{7,6},{8,9},{9,8},{10,11... | collective-permute-start | bytes 6291464 | tf_op jit(solution)/shard_map/swap_stored/ppermute | solution.py:210
  78.5 3.0 %collective-permute-start.29 = (bf16[256,256]{1,0:T(8,128)(2,1)S(1)}, bf16[256,256]{1,0:T(8,128)(2,1)S(1)}, u32[]{:S(2)}, u32[]{:S(2)}) collective-permute-start(bf16[256,256]{1,0:T(8,128)(2,1)S(1)} %collective-permute-done.28.refs_3_), channel_id=1, source_target_pairs={{0,56},{8,0},{16,8},{24,16},{32,24},{40,32},{48,40},{56,48},{1,57}... | collective-permute-start | bytes 393224 | tf_op jit(solution)/shard_map/gather_preconditioned/ppermute | solution.py:202
  81.5 0.9 collective-permute-done.35.refs_16_.refs_8_
  82.4 2.5 %score.2.refs_9_ = f32[256,1024]{1,0:T(8,128)S(1)} custom-call(s32[50]{0:T(128)S(1)} %concatenate.3.where_ref.refs_0_, bf16[256,256]{1,0:T(8,128)(2,1)S(1)} %precondition.1.refs_1_, bf16[256,256]{1,0:T(8,128)(2,1)S(1)} %collective-permute-done.18.refs_2_, bf16[256,256]{1,0:T(8,128)(2,1)S(1)} %collective-permute-done.32.refs_3_, ...), custom_call_target="tpu_custom_call" | custom-call | flops 1610612736 | bytes 7864320 | tf_op jit(solution)/shard_map/score/score/pallas_call | solution.py:144
  84.9 0.4 collective-permute-done.21.refs_1_
  85.4 1.5 %score.3 = (f32[64,1024]{1,0:T(8,128)S(1)}, bf16[64,1024]{1,0:T(8,128)(2,1)S(1)}, bf16[64,1024]{1,0:T(8,128)(2,1)S(1)}, bf16[64,1024]{1,0:T(8,128)(2,1)S(1)}) custom-call(s32[50]{0:T(128)S(1)} %concatenate.3.where_ref.refs_0_, bf16[256,256]{1,0:T(8,128)(2,1)S(1)} %collective-permute-done.21.refs_1_, bf16[256,256]{1,0:T(8,128)(2,1)S(1)} %collective-permute-done.25.refs_2_, ...), custom_call_target="tpu_custom_call" | custom-call | flops 536870912 | bytes 2621440 | tf_op jit(solution)/shard_map/score/score/pallas_call | solution.py:144
  86.9 2.8 %collective-permute-start.36 = (bf16[64,1024]{1,0:T(8,128)(2,1)S(1)}, bf16[64,1024]{1,0:T(8,128)(2,1)S(1)}, u32[]{:S(2)}, u32[]{:S(2)}) collective-permute-start(bf16[64,1024]{1,0:T(8,128)(2,1)S(1)} %get-tuple-element.28), channel_id=1, source_target_pairs={{0,128},{64,192},{128,0},{192,64},{1,129},{65,193},{129,1},{193,65... | collective-permute-start | bytes 393224 | tf_op jit(solution)/shard_map/sum_layers/ppermute | solution.py:202
  89.7 0.3 collective-permute-start.37
  90.0 2.4 %collective-permute-start.38 = (bf16[64,1024]{1,0:T(8,128)(2,1)S(1)}, bf16[64,1024]{1,0:T(8,128)(2,1)S(1)}, u32[]{:S(2)}, u32[]{:S(2)}) collective-permute-start(bf16[64,1024]{1,0:T(8,128)(2,1)S(1)} %get-tuple-element.30), channel_id=1, source_target_pairs={{0,192},{64,0},{128,64},{192,128},{1,193},{65,1},{129,65},{193,129... | collective-permute-start | bytes 393224 | tf_op jit(solution)/shard_map/sum_layers/ppermute | solution.py:202
  92.4 0.5 collective-permute-done.36.a_ref
  92.9 3.5 %collective-permute-done.37.b_ref = bf16[64,1024]{1,0:T(8,128)(2,1)S(1)} collective-permute-done((bf16[64,1024]{1,0:T(8,128)(2,1)S(1)}, bf16[64,1024]{1,0:T(8,128)(2,1)S(1)}, u32[]{:S(2)}, u32[]{:S(2)}) %collective-permute-start.37) | collective-permute-done | bytes 131104 | tf_op jit(solution)/shard_map/sum_layers/ppermute | solution.py:202
  96.5 1.2 %collective-permute-start.39 = (bf16[64,256]{1,0:T(8,128)(2,1)S(1)}, bf16[64,256]{1,0:T(8,128)(2,1)S(1)}, u32[]{:S(2)}, u32[]{:S(2)}) collective-permute-start(bf16[64,256]{1,0:T(8,128)(2,1)S(1)} %get-tuple-element.32), channel_id=1, source_target_pairs={{0,1},{1,0},{2,3},{3,2},{4,5},{5,4},{6,7},{7,6},{8,9},{9,8},{10,11... | collective-permute-start | bytes 98312 | tf_op jit(solution)/shard_map/exchange_examples/ppermute | solution.py:281
  97.7 1.8 %collective-permute-start.40 = (bf16[64,256]{1,0:T(8,128)(2,1)S(1)}, bf16[64,256]{1,0:T(8,128)(2,1)S(1)}, u32[]{:S(2)}, u32[]{:S(2)}) collective-permute-start(bf16[64,256]{1,0:T(8,128)(2,1)S(1)} %get-tuple-element.33), channel_id=1, source_target_pairs={{0,6},{1,7},{2,4},{3,5},{4,2},{5,3},{6,0},{7,1},{8,14},{9,15},{10,... | collective-permute-start | bytes 98312 | tf_op jit(solution)/shard_map/exchange_examples/ppermute | solution.py:281
  99.5 1.1 %collective-permute-start.41 = (bf16[64,256]{1,0:T(8,128)(2,1)S(1)}, bf16[64,256]{1,0:T(8,128)(2,1)S(1)}, u32[]{:S(2)}, u32[]{:S(2)}) collective-permute-start(bf16[64,256]{1,0:T(8,128)(2,1)S(1)} %get-tuple-element.34), channel_id=1, source_target_pairs={{0,7},{1,6},{2,5},{3,4},{4,3},{5,2},{6,1},{7,0},{8,15},{9,14},{10,... | collective-permute-start | bytes 98312 | tf_op jit(solution)/shard_map/exchange_examples/ppermute | solution.py:281
  100.6 1.0 collective-permute-done.40.refs_2_
  101.7 2.4 %collective-permute-done.41.refs_3_ = bf16[64,256]{1,0:T(8,128)(2,1)S(1)} collective-permute-done((bf16[64,256]{1,0:T(8,128)(2,1)S(1)}, bf16[64,256]{1,0:T(8,128)(2,1)S(1)}, u32[]{:S(2)}, u32[]{:S(2)}) %collective-permute-start.41) | collective-permute-done | bytes 32800 | tf_op jit(solution)/shard_map/exchange_examples/ppermute | solution.py:281
  104.1 1.3 %place_parts.1 = f32[256,256]{1,0:T(8,128)} custom-call(s32[50]{0:T(128)S(1)} %concatenate.3.where_ref.refs_0_, f32[64,256]{1,0:T(8,128)S(1)} %get-tuple-element.31.refs_0_, bf16[64,256]{1,0:T(8,128)(2,1)S(1)} %collective-permute-done.39.refs_1_, bf16[64,256]{1,0:T(8,128)(2,1)S(1)} %collective-permute-done.40.refs_2_, ...), custom_call_target="tpu_custom_call" | custom-call | flops 65536 | bytes 524288 | tf_op jit(solution)/shard_map/exchange_examples/place_parts/pallas_call | solution.py:190
  (47 shorter events, 0.7 us)
Async XLA Ops:
  0.0 18.1 %copy-start = (bf16[1,256,4096]{2,1,0:T(8,128)(2,1)S(1)}, bf16[1,256,4096]{2,1,0:T(8,128)(2,1)}, u32[]{:S(2)}) copy-start(bf16[1,256,4096]{2,1,0:T(8,128)(2,1)} %param.8) | copy-start | bytes 6291460
  0.0 40.5 %collective-permute-start.16 = (f32[64,4096]{1,0:T(8,128)}, f32[64,4096]{1,0:T(8,128)S(1)}, u32[]{:S(2)}, u32[]{:S(2)}) collective-permute-start(f32[64,4096]{1,0:T(8,128)} %bitcast.12), channel_id=1, source_target_pairs={{0,6},{6,0},{2,4},{4,2},{1,7},{7,1},{3,5},{5,3},{8,14},{14,8},{10,... | collective-permute-start | bytes 3145736 | tf_op jit(solution)/shard_map/swap_inverse/ppermute | solution.py:245
  4.8 1.6 %copy-start.1 = (bf16[1,16,512,128]{3,2,1,0:T(8,128)(2,1)S(1)}, bf16[1,16,512,128]{3,2,1,0:T(8,128)(2,1)}, u32[]{:S(2)}) copy-start(bf16[1,16,512,128]{3,2,1,0:T(8,128)(2,1)} %param.5) | copy-start | bytes 6291460
  6.4 0.7 copy-start.3
  9.5 5.8 %collective-permute-start.7 = (bf16[16,4096]{1,0:T(8,128)(2,1)S(1)}, bf16[16,4096]{1,0:T(8,128)(2,1)S(1)}, u32[]{:S(2)}, u32[]{:S(2)}) collective-permute-start(bf16[16,4096]{1,0:T(8,128)(2,1)S(1)} %reshape.12.refs_1_), channel_id=1, source_target_pairs={{0,2},{2,0},{4,6},{6,4},{1,3},{3,1},{5,7},{7,5},{8,10},{10,8},{12,... | collective-permute-start | bytes 393224 | tf_op jit(solution)/shard_map/gather_projected/ppermute | solution.py:245
  9.6 8.5 %collective-permute-start = (bf16[16,4096]{1,0:T(8,128)(2,1)S(1)}, bf16[16,4096]{1,0:T(8,128)(2,1)S(1)}, u32[]{:S(2)}, u32[]{:S(2)}) collective-permute-start(bf16[16,4096]{1,0:T(8,128)(2,1)S(1)} %reshape.12.refs_1_), channel_id=1, source_target_pairs={{0,8},{8,16},{16,24},{24,32},{32,40},{40,48},{48,56},{56,0},{1,9},... | collective-permute-start | bytes 393224 | tf_op jit(solution)/shard_map/gather_projected/ppermute | solution.py:202
  11.3 6.8 %collective-permute-start.1 = (bf16[16,4096]{1,0:T(8,128)(2,1)S(1)}, bf16[16,4096]{1,0:T(8,128)(2,1)S(1)}, u32[]{:S(2)}, u32[]{:S(2)}) collective-permute-start(bf16[16,4096]{1,0:T(8,128)(2,1)S(1)} %reshape.12.refs_1_), channel_id=1, source_target_pairs={{0,56},{8,0},{16,8},{24,16},{32,24},{40,32},{48,40},{56,48},{1,57}... | collective-permute-start | bytes 393224 | tf_op jit(solution)/shard_map/gather_projected/ppermute | solution.py:202
  15.3 6.6 %collective-permute-start.8 = (bf16[16,4096]{1,0:T(8,128)(2,1)S(1)}, bf16[16,4096]{1,0:T(8,128)(2,1)S(1)}, u32[]{:S(2)}, u32[]{:S(2)}) collective-permute-start(bf16[16,4096]{1,0:T(8,128)(2,1)S(1)} %collective-permute-done.7.refs_9_), channel_id=1, source_target_pairs={{0,8},{8,16},{16,24},{24,32},{32,40},{40,48},{48,56},{56,0},{1,9},... | collective-permute-start | bytes 393224 | tf_op jit(solution)/shard_map/gather_projected/ppermute | solution.py:202
  18.1 53.1 %collective-permute-start.31 = (bf16[256,4096]{1,0:T(8,128)(2,1)S(1)}, bf16[256,4096]{1,0:T(8,128)(2,1)S(1)}, u32[]{:S(2)}, u32[]{:S(2)}) collective-permute-start(bf16[256,4096]{1,0:T(8,128)(2,1)S(1)} %bitcast.7), channel_id=1, source_target_pairs={{0,6},{6,0},{2,4},{4,2},{1,7},{7,1},{3,5},{5,3},{8,14},{14,8},{10,... | collective-permute-start | bytes 6291464 | tf_op jit(solution)/shard_map/swap_stored/ppermute | solution.py:245
  18.8 5.2 %collective-permute-start.9 = (bf16[16,4096]{1,0:T(8,128)(2,1)S(1)}, bf16[16,4096]{1,0:T(8,128)(2,1)S(1)}, u32[]{:S(2)}, u32[]{:S(2)}) collective-permute-start(bf16[16,4096]{1,0:T(8,128)(2,1)S(1)} %collective-permute-done.7.refs_9_), channel_id=1, source_target_pairs={{0,56},{8,0},{16,8},{24,16},{32,24},{40,32},{48,40},{56,48},{1,57}... | collective-permute-start | bytes 393224 | tf_op jit(solution)/shard_map/gather_projected/ppermute | solution.py:202
  21.3 5.3 %collective-permute-start.2 = (bf16[16,4096]{1,0:T(8,128)(2,1)S(1)}, bf16[16,4096]{1,0:T(8,128)(2,1)S(1)}, u32[]{:S(2)}, u32[]{:S(2)}) collective-permute-start(bf16[16,4096]{1,0:T(8,128)(2,1)S(1)} %collective-permute-done.refs_2_), channel_id=1, source_target_pairs={{0,8},{8,16},{16,24},{24,32},{32,40},{40,48},{48,56},{56,0},{1,9},... | collective-permute-start | bytes 393224 | tf_op jit(solution)/shard_map/gather_projected/ppermute | solution.py:202
  21.9 5.4 %collective-permute-start.3 = (bf16[16,4096]{1,0:T(8,128)(2,1)S(1)}, bf16[16,4096]{1,0:T(8,128)(2,1)S(1)}, u32[]{:S(2)}, u32[]{:S(2)}) collective-permute-start(bf16[16,4096]{1,0:T(8,128)(2,1)S(1)} %collective-permute-done.1.refs_3_), channel_id=1, source_target_pairs={{0,56},{8,0},{16,8},{24,16},{32,24},{40,32},{48,40},{56,48},{1,57}... | collective-permute-start | bytes 393224 | tf_op jit(solution)/shard_map/gather_projected/ppermute | solution.py:202
  24.0 6.5 %collective-permute-start.10 = (bf16[16,4096]{1,0:T(8,128)(2,1)S(1)}, bf16[16,4096]{1,0:T(8,128)(2,1)S(1)}, u32[]{:S(2)}, u32[]{:S(2)}) collective-permute-start(bf16[16,4096]{1,0:T(8,128)(2,1)S(1)} %collective-permute-done.8.refs_10_), channel_id=1, source_target_pairs={{0,8},{8,16},{16,24},{24,32},{32,40},{40,48},{48,56},{56,0},{1,9},... | collective-permute-start | bytes 393224 | tf_op jit(solution)/shard_map/gather_projected/ppermute | solution.py:202
  26.6 4.1 %collective-permute-start.11 = (bf16[16,4096]{1,0:T(8,128)(2,1)S(1)}, bf16[16,4096]{1,0:T(8,128)(2,1)S(1)}, u32[]{:S(2)}, u32[]{:S(2)}) collective-permute-start(bf16[16,4096]{1,0:T(8,128)(2,1)S(1)} %collective-permute-done.9.refs_11_), channel_id=1, source_target_pairs={{0,56},{8,0},{16,8},{24,16},{32,24},{40,32},{48,40},{56,48},{1,57}... | collective-permute-start | bytes 393224 | tf_op jit(solution)/shard_map/gather_projected/ppermute | solution.py:202
  27.3 7.0 %collective-permute-start.4 = (bf16[16,4096]{1,0:T(8,128)(2,1)S(1)}, bf16[16,4096]{1,0:T(8,128)(2,1)S(1)}, u32[]{:S(2)}, u32[]{:S(2)}) collective-permute-start(bf16[16,4096]{1,0:T(8,128)(2,1)S(1)} %collective-permute-done.2.refs_4_), channel_id=1, source_target_pairs={{0,8},{8,16},{16,24},{24,32},{32,40},{40,48},{48,56},{56,0},{1,9},... | collective-permute-start | bytes 393224 | tf_op jit(solution)/shard_map/gather_projected/ppermute | solution.py:202
  30.5 4.9 %collective-permute-start.5 = (bf16[16,4096]{1,0:T(8,128)(2,1)S(1)}, bf16[16,4096]{1,0:T(8,128)(2,1)S(1)}, u32[]{:S(2)}, u32[]{:S(2)}) collective-permute-start(bf16[16,4096]{1,0:T(8,128)(2,1)S(1)} %collective-permute-done.3.refs_5_), channel_id=1, source_target_pairs={{0,56},{8,0},{16,8},{24,16},{32,24},{40,32},{48,40},{56,48},{1,57}... | collective-permute-start | bytes 393224 | tf_op jit(solution)/shard_map/gather_projected/ppermute | solution.py:202
  30.7 9.8 %collective-permute-start.12 = (bf16[16,4096]{1,0:T(8,128)(2,1)S(1)}, bf16[16,4096]{1,0:T(8,128)(2,1)S(1)}, u32[]{:S(2)}, u32[]{:S(2)}) collective-permute-start(bf16[16,4096]{1,0:T(8,128)(2,1)S(1)} %collective-permute-done.10.refs_12_), channel_id=1, source_target_pairs={{0,8},{8,16},{16,24},{24,32},{32,40},{40,48},{48,56},{56,0},{1,9},... | collective-permute-start | bytes 393224 | tf_op jit(solution)/shard_map/gather_projected/ppermute | solution.py:202
  34.3 6.3 %collective-permute-start.13 = (bf16[16,4096]{1,0:T(8,128)(2,1)S(1)}, bf16[16,4096]{1,0:T(8,128)(2,1)S(1)}, u32[]{:S(2)}, u32[]{:S(2)}) collective-permute-start(bf16[16,4096]{1,0:T(8,128)(2,1)S(1)} %collective-permute-done.11.refs_13_), channel_id=1, source_target_pairs={{0,56},{8,0},{16,8},{24,16},{32,24},{40,32},{48,40},{56,48},{1,57}... | collective-permute-start | bytes 393224 | tf_op jit(solution)/shard_map/gather_projected/ppermute | solution.py:202
  35.4 11.0 %collective-permute-start.15 = (f32[64,4096]{1,0:T(8,128)}, f32[64,4096]{1,0:T(8,128)S(1)}, u32[]{:S(2)}, u32[]{:S(2)}) collective-permute-start(f32[64,4096]{1,0:T(8,128)} %bitcast.13), channel_id=1, source_target_pairs={{0,1},{1,0},{2,3},{3,2},{4,5},{5,4},{6,7},{7,6},{8,9},{9,8},{10,11... | collective-permute-start | bytes 3145736 | tf_op jit(solution)/shard_map/swap_inverse/ppermute | solution.py:210
  40.5 5.9 %collective-permute-start.17 = (f32[64,4096]{1,0:T(8,128)S(1)}, f32[64,4096]{1,0:T(8,128)S(1)}, u32[]{:S(2)}, u32[]{:S(2)}) collective-permute-start(f32[64,4096]{1,0:T(8,128)S(1)} %collective-permute-done.16.chip_ref), channel_id=1, source_target_pairs={{0,1},{1,0},{2,3},{3,2},{4,5},{5,4},{6,7},{7,6},{8,9},{9,8},{10,11... | collective-permute-start | bytes 3145736 | tf_op jit(solution)/shard_map/swap_inverse/ppermute | solution.py:210
  43.5 6.7 %collective-permute-start.6 = (bf16[16,4096]{1,0:T(8,128)(2,1)S(1)}, bf16[16,4096]{1,0:T(8,128)(2,1)S(1)}, u32[]{:S(2)}, u32[]{:S(2)}) collective-permute-start(bf16[16,4096]{1,0:T(8,128)(2,1)S(1)} %collective-permute-done.4.refs_6_), channel_id=1, source_target_pairs={{0,8},{8,16},{16,24},{24,32},{32,40},{40,48},{48,56},{56,0},{1,9},... | collective-permute-start | bytes 393224 | tf_op jit(solution)/shard_map/gather_projected/ppermute | solution.py:202
  43.9 6.4 %collective-permute-start.14 = (bf16[16,4096]{1,0:T(8,128)(2,1)S(1)}, bf16[16,4096]{1,0:T(8,128)(2,1)S(1)}, u32[]{:S(2)}, u32[]{:S(2)}) collective-permute-start(bf16[16,4096]{1,0:T(8,128)(2,1)S(1)} %collective-permute-done.13.refs_15_), channel_id=1, source_target_pairs={{0,56},{8,0},{16,8},{24,16},{32,24},{40,32},{48,40},{56,48},{1,57}... | collective-permute-start | bytes 393224 | tf_op jit(solution)/shard_map/gather_projected/ppermute | solution.py:202
  46.5 1.2 %copy-start.2 = (f32[1,64,4096]{2,1,0:T(8,128)S(1)}, f32[1,64,4096]{2,1,0:T(8,128)}, u32[]{:S(2)}) copy-start(f32[1,64,4096]{2,1,0:T(8,128)} %param.7) | copy-start | bytes 3145732
  52.0 4.5 %collective-permute-start.22 = (bf16[256,256]{1,0:T(8,128)(2,1)S(1)}, bf16[256,256]{1,0:T(8,128)(2,1)S(1)}, u32[]{:S(2)}, u32[]{:S(2)}) collective-permute-start(bf16[256,256]{1,0:T(8,128)(2,1)S(1)} %precondition.1.refs_1_), channel_id=1, source_target_pairs={{0,2},{2,0},{4,6},{6,4},{1,3},{3,1},{5,7},{7,5},{8,10},{10,8},{12,... | collective-permute-start | bytes 393224 | tf_op jit(solution)/shard_map/gather_preconditioned/ppermute | solution.py:245
  52.3 6.9 %collective-permute-start.18 = (bf16[256,256]{1,0:T(8,128)(2,1)S(1)}, bf16[256,256]{1,0:T(8,128)(2,1)S(1)}, u32[]{:S(2)}, u32[]{:S(2)}) collective-permute-start(bf16[256,256]{1,0:T(8,128)(2,1)S(1)} %precondition.1.refs_1_), channel_id=1, source_target_pairs={{0,8},{8,16},{16,24},{24,32},{32,40},{40,48},{48,56},{56,0},{1,9},... | collective-permute-start | bytes 393224 | tf_op jit(solution)/shard_map/gather_preconditioned/ppermute | solution.py:202
  54.3 5.3 %collective-permute-start.32 = (bf16[256,256]{1,0:T(8,128)(2,1)S(1)}, bf16[256,256]{1,0:T(8,128)(2,1)S(1)}, u32[]{:S(2)}, u32[]{:S(2)}) collective-permute-start(bf16[256,256]{1,0:T(8,128)(2,1)S(1)} %precondition.1.refs_1_), channel_id=1, source_target_pairs={{0,56},{8,0},{16,8},{24,16},{32,24},{40,32},{48,40},{56,48},{1,57}... | collective-permute-start | bytes 393224 | tf_op jit(solution)/shard_map/gather_preconditioned/ppermute | solution.py:202
  56.5 5.4 %collective-permute-start.23 = (bf16[256,256]{1,0:T(8,128)(2,1)S(1)}, bf16[256,256]{1,0:T(8,128)(2,1)S(1)}, u32[]{:S(2)}, u32[]{:S(2)}) collective-permute-start(bf16[256,256]{1,0:T(8,128)(2,1)S(1)} %collective-permute-done.22.refs_8_), channel_id=1, source_target_pairs={{0,8},{8,16},{16,24},{24,32},{32,40},{40,48},{48,56},{56,0},{1,9},... | collective-permute-start | bytes 393224 | tf_op jit(solution)/shard_map/gather_preconditioned/ppermute | solution.py:202
  58.2 4.1 %collective-permute-start.26 = (bf16[256,256]{1,0:T(8,128)(2,1)S(1)}, bf16[256,256]{1,0:T(8,128)(2,1)S(1)}, u32[]{:S(2)}, u32[]{:S(2)}) collective-permute-start(bf16[256,256]{1,0:T(8,128)(2,1)S(1)} %collective-permute-done.22.refs_8_), channel_id=1, source_target_pairs={{0,56},{8,0},{16,8},{24,16},{32,24},{40,32},{48,40},{56,48},{1,57}... | collective-permute-start | bytes 393224 | tf_op jit(solution)/shard_map/gather_preconditioned/ppermute | solution.py:202
  59.2 6.0 %collective-permute-start.19 = (bf16[256,256]{1,0:T(8,128)(2,1)S(1)}, bf16[256,256]{1,0:T(8,128)(2,1)S(1)}, u32[]{:S(2)}, u32[]{:S(2)}) collective-permute-start(bf16[256,256]{1,0:T(8,128)(2,1)S(1)} %collective-permute-done.18.refs_2_), channel_id=1, source_target_pairs={{0,8},{8,16},{16,24},{24,32},{32,40},{40,48},{48,56},{56,0},{1,9},... | collective-permute-start | bytes 393224 | tf_op jit(solution)/shard_map/gather_preconditioned/ppermute | solution.py:202
  59.6 5.6 %collective-permute-start.33 = (bf16[256,256]{1,0:T(8,128)(2,1)S(1)}, bf16[256,256]{1,0:T(8,128)(2,1)S(1)}, u32[]{:S(2)}, u32[]{:S(2)}) collective-permute-start(bf16[256,256]{1,0:T(8,128)(2,1)S(1)} %collective-permute-done.32.refs_3_), channel_id=1, source_target_pairs={{0,56},{8,0},{16,8},{24,16},{32,24},{40,32},{48,40},{56,48},{1,57}... | collective-permute-start | bytes 393224 | tf_op jit(solution)/shard_map/gather_preconditioned/ppermute | solution.py:202
  61.9 6.6 %collective-permute-start.24 = (bf16[256,256]{1,0:T(8,128)(2,1)S(1)}, bf16[256,256]{1,0:T(8,128)(2,1)S(1)}, u32[]{:S(2)}, u32[]{:S(2)}) collective-permute-start(bf16[256,256]{1,0:T(8,128)(2,1)S(1)} %collective-permute-done.23.refs_9_), channel_id=1, source_target_pairs={{0,8},{8,16},{16,24},{24,32},{32,40},{40,48},{48,56},{56,0},{1,9},... | collective-permute-start | bytes 393224 | tf_op jit(solution)/shard_map/gather_preconditioned/ppermute | solution.py:202
  62.3 6.2 %collective-permute-start.27 = (bf16[256,256]{1,0:T(8,128)(2,1)S(1)}, bf16[256,256]{1,0:T(8,128)(2,1)S(1)}, u32[]{:S(2)}, u32[]{:S(2)}) collective-permute-start(bf16[256,256]{1,0:T(8,128)(2,1)S(1)} %collective-permute-done.26.refs_10_), channel_id=1, source_target_pairs={{0,56},{8,0},{16,8},{24,16},{32,24},{40,32},{48,40},{56,48},{1,57}... | collective-permute-start | bytes 393224 | tf_op jit(solution)/shard_map/gather_preconditioned/ppermute | solution.py:202
  65.2 10.4 %collective-permute-start.20 = (bf16[256,256]{1,0:T(8,128)(2,1)S(1)}, bf16[256,256]{1,0:T(8,128)(2,1)S(1)}, u32[]{:S(2)}, u32[]{:S(2)}) collective-permute-start(bf16[256,256]{1,0:T(8,128)(2,1)S(1)} %collective-permute-done.19.refs_4_), channel_id=1, source_target_pairs={{0,8},{8,16},{16,24},{24,32},{32,40},{40,48},{48,56},{56,0},{1,9},... | collective-permute-start | bytes 393224 | tf_op jit(solution)/shard_map/gather_preconditioned/ppermute | solution.py:202
  65.2 10.4 %collective-permute-start.34 = (bf16[256,256]{1,0:T(8,128)(2,1)S(1)}, bf16[256,256]{1,0:T(8,128)(2,1)S(1)}, u32[]{:S(2)}, u32[]{:S(2)}) collective-permute-start(bf16[256,256]{1,0:T(8,128)(2,1)S(1)} %collective-permute-done.33.refs_5_), channel_id=1, source_target_pairs={{0,56},{8,0},{16,8},{24,16},{32,24},{40,32},{48,40},{56,48},{1,57}... | collective-permute-start | bytes 393224 | tf_op jit(solution)/shard_map/gather_preconditioned/ppermute | solution.py:202
  68.5 7.1 %collective-permute-start.25 = (bf16[256,256]{1,0:T(8,128)(2,1)S(1)}, bf16[256,256]{1,0:T(8,128)(2,1)S(1)}, u32[]{:S(2)}, u32[]{:S(2)}) collective-permute-start(bf16[256,256]{1,0:T(8,128)(2,1)S(1)} %collective-permute-done.24.refs_11_), channel_id=1, source_target_pairs={{0,8},{8,16},{16,24},{24,32},{32,40},{40,48},{48,56},{56,0},{1,9},... | collective-permute-start | bytes 393224 | tf_op jit(solution)/shard_map/gather_preconditioned/ppermute | solution.py:202
  68.5 7.1 %collective-permute-start.28 = (bf16[256,256]{1,0:T(8,128)(2,1)S(1)}, bf16[256,256]{1,0:T(8,128)(2,1)S(1)}, u32[]{:S(2)}, u32[]{:S(2)}) collective-permute-start(bf16[256,256]{1,0:T(8,128)(2,1)S(1)} %collective-permute-done.27.refs_12_), channel_id=1, source_target_pairs={{0,56},{8,0},{16,8},{24,16},{32,24},{40,32},{48,40},{56,48},{1,57}... | collective-permute-start | bytes 393224 | tf_op jit(solution)/shard_map/gather_preconditioned/ppermute | solution.py:202
  71.2 10.3 %collective-permute-start.30 = (bf16[256,4096]{1,0:T(8,128)(2,1)S(1)}, bf16[256,4096]{1,0:T(8,128)(2,1)S(1)}, u32[]{:S(2)}, u32[]{:S(2)}) collective-permute-start(bf16[256,4096]{1,0:T(8,128)(2,1)S(1)} %bitcast.8), channel_id=1, source_target_pairs={{0,1},{1,0},{2,3},{3,2},{4,5},{5,4},{6,7},{7,6},{8,9},{9,8},{10,11... | collective-permute-start | bytes 6291464 | tf_op jit(solution)/shard_map/swap_stored/ppermute | solution.py:210
  75.6 6.8 %collective-permute-start.35 = (bf16[256,4096]{1,0:T(8,128)(2,1)S(1)}, bf16[256,4096]{1,0:T(8,128)(2,1)S(1)}, u32[]{:S(2)}, u32[]{:S(2)}) collective-permute-start(bf16[256,4096]{1,0:T(8,128)(2,1)S(1)} %collective-permute-done.31.refs_15_.refs_7_), channel_id=1, source_target_pairs={{0,1},{1,0},{2,3},{3,2},{4,5},{5,4},{6,7},{7,6},{8,9},{9,8},{10,11... | collective-permute-start | bytes 6291464 | tf_op jit(solution)/shard_map/swap_stored/ppermute | solution.py:210
  78.5 6.8 %collective-permute-start.21 = (bf16[256,256]{1,0:T(8,128)(2,1)S(1)}, bf16[256,256]{1,0:T(8,128)(2,1)S(1)}, u32[]{:S(2)}, u32[]{:S(2)}) collective-permute-start(bf16[256,256]{1,0:T(8,128)(2,1)S(1)} %collective-permute-done.20.refs_6_), channel_id=1, source_target_pairs={{0,8},{8,16},{16,24},{24,32},{32,40},{40,48},{48,56},{56,0},{1,9},... | collective-permute-start | bytes 393224 | tf_op jit(solution)/shard_map/gather_preconditioned/ppermute | solution.py:202
  78.5 6.8 %collective-permute-start.29 = (bf16[256,256]{1,0:T(8,128)(2,1)S(1)}, bf16[256,256]{1,0:T(8,128)(2,1)S(1)}, u32[]{:S(2)}, u32[]{:S(2)}) collective-permute-start(bf16[256,256]{1,0:T(8,128)(2,1)S(1)} %collective-permute-done.28.refs_3_), channel_id=1, source_target_pairs={{0,56},{8,0},{16,8},{24,16},{32,24},{40,32},{48,40},{56,48},{1,57}... | collective-permute-start | bytes 393224 | tf_op jit(solution)/shard_map/gather_preconditioned/ppermute | solution.py:202
  86.9 6.1 %collective-permute-start.36 = (bf16[64,1024]{1,0:T(8,128)(2,1)S(1)}, bf16[64,1024]{1,0:T(8,128)(2,1)S(1)}, u32[]{:S(2)}, u32[]{:S(2)}) collective-permute-start(bf16[64,1024]{1,0:T(8,128)(2,1)S(1)} %get-tuple-element.28), channel_id=1, source_target_pairs={{0,128},{64,192},{128,0},{192,64},{1,129},{65,193},{129,1},{193,65... | collective-permute-start | bytes 393224 | tf_op jit(solution)/shard_map/sum_layers/ppermute | solution.py:202
  89.7 6.7 %collective-permute-start.37 = (bf16[64,1024]{1,0:T(8,128)(2,1)S(1)}, bf16[64,1024]{1,0:T(8,128)(2,1)S(1)}, u32[]{:S(2)}, u32[]{:S(2)}) collective-permute-start(bf16[64,1024]{1,0:T(8,128)(2,1)S(1)} %get-tuple-element.29), channel_id=1, source_target_pairs={{0,64},{64,128},{128,192},{192,0},{1,65},{65,129},{129,193},{193,1... | collective-permute-start | bytes 393224 | tf_op jit(solution)/shard_map/sum_layers/ppermute | solution.py:202
  90.0 6.4 %collective-permute-start.38 = (bf16[64,1024]{1,0:T(8,128)(2,1)S(1)}, bf16[64,1024]{1,0:T(8,128)(2,1)S(1)}, u32[]{:S(2)}, u32[]{:S(2)}) collective-permute-start(bf16[64,1024]{1,0:T(8,128)(2,1)S(1)} %get-tuple-element.30), channel_id=1, source_target_pairs={{0,192},{64,0},{128,64},{192,128},{1,193},{65,1},{129,65},{193,129... | collective-permute-start | bytes 393224 | tf_op jit(solution)/shard_map/sum_layers/ppermute | solution.py:202
  96.5 4.1 %collective-permute-start.39 = (bf16[64,256]{1,0:T(8,128)(2,1)S(1)}, bf16[64,256]{1,0:T(8,128)(2,1)S(1)}, u32[]{:S(2)}, u32[]{:S(2)}) collective-permute-start(bf16[64,256]{1,0:T(8,128)(2,1)S(1)} %get-tuple-element.32), channel_id=1, source_target_pairs={{0,1},{1,0},{2,3},{3,2},{4,5},{5,4},{6,7},{7,6},{8,9},{9,8},{10,11... | collective-permute-start | bytes 98312 | tf_op jit(solution)/shard_map/exchange_examples/ppermute | solution.py:281
  97.7 4.0 %collective-permute-start.40 = (bf16[64,256]{1,0:T(8,128)(2,1)S(1)}, bf16[64,256]{1,0:T(8,128)(2,1)S(1)}, u32[]{:S(2)}, u32[]{:S(2)}) collective-permute-start(bf16[64,256]{1,0:T(8,128)(2,1)S(1)} %get-tuple-element.33), channel_id=1, source_target_pairs={{0,6},{1,7},{2,4},{3,5},{4,2},{5,3},{6,0},{7,1},{8,14},{9,15},{10,... | collective-permute-start | bytes 98312 | tf_op jit(solution)/shard_map/exchange_examples/ppermute | solution.py:281
  99.5 4.6 %collective-permute-start.41 = (bf16[64,256]{1,0:T(8,128)(2,1)S(1)}, bf16[64,256]{1,0:T(8,128)(2,1)S(1)}, u32[]{:S(2)}, u32[]{:S(2)}) collective-permute-start(bf16[64,256]{1,0:T(8,128)(2,1)S(1)} %get-tuple-element.34), channel_id=1, source_target_pairs={{0,7},{1,6},{2,5},{3,4},{4,3},{5,2},{6,1},{7,0},{8,15},{9,14},{10,... | collective-permute-start | bytes 98312 | tf_op jit(solution)/shard_map/exchange_examples/ppermute | solution.py:281
